TPU v7x, 256 devices: a whole 4x4x8 slice. The times are simulated.
256 devices in a mesh: grp: 8 (over y, core), dev: 32 (over z, x).
Axes of the slice: x: 4, y: 4, z: 8, core: 2. Of those that a mesh axis runs over, the one named last changes fastest.
Arguments:
- right_side: float32 [1024, 32, 256], P(('grp', 'dev')), may hold values from -6 to 6
- cotangent: float32 [1024, 32, 256], P(('grp', 'dev')), may hold values from -6 to 6
- texture: float32 [1024, 32, 256], P(('grp', 'dev')), may hold values from 0.5 to 2
- labels: int32 [1024, 32, 2], P(('grp', 'dev')), may hold values from 0 to 63
- coef_table: float32 [8, 64], P('grp', 'dev'), may hold values from 0.1 to 0.4
Outputs:
- source_grad: float32 [1024, 32, 256], P(('grp', 'dev'))
- table_grad: float32 [8, 64], P('grp', 'dev')
All inputs are finite; a program needn't handle non-finite values.
Results may differ from a plain program's by a relative error of at most 0.000041.
Values sent between devices are 32-bit elements; how exact they have to be, the bound alone decides.
No kernel may reach another device: no remote copies, remote signals or barrier semaphores. Data moves between devices by JAX's collectives and lax.ppermute only.
A program may use at most 64 MiB of HBM per device.

v0:
```python
import jax
import jax.numpy as jnp
from jax import lax
from jax.sharding import PartitionSpec as P

SWEEPS = 4


RELAX = 0.2
REACTION = 0.1
INNER = (slice(1, -1), slice(1, -1), slice(1, -1))
NEIGHBOURS = (
    (slice(0, -2), slice(1, -1), slice(1, -1)),
    (slice(2, None), slice(1, -1), slice(1, -1)),
    (slice(1, -1), slice(0, -2), slice(1, -1)),
    (slice(1, -1), slice(2, None), slice(1, -1)),
    (slice(1, -1), slice(1, -1), slice(0, -2)),
    (slice(1, -1), slice(1, -1), slice(2, None)),
)


def extended(cells, sides, width):
    for axis, dim in sides:
        count = lax.axis_size(axis)
        ends = count - 1
        head = lax.slice_in_dim(cells, 0, width, axis=dim)
        tail = lax.slice_in_dim(cells, cells.shape[dim] - width, cells.shape[dim], axis=dim)
        cells = jnp.concatenate(
            [
                lax.ppermute(tail, axis, [(i, (i + 1) % count) for i in range(ends)]),
                cells,
                lax.ppermute(head, axis, [((i + 1) % count, i) for i in range(ends)]),
            ],
            axis=dim,
        )
    return cells


def shifted(block, axis, distance):
    devices = range(lax.axis_size(axis))
    route = [(i - distance, i) for i in devices if i - distance in devices]
    return lax.ppermute(block, axis, route)


def swapped(value, axis, distance):
    mask = 2**distance
    pairs = [(source, source ^ mask) for source in range(lax.axis_size(axis))]
    return lax.ppermute(value, axis, pairs)


def stencil(field_pad, kappa_pad):
    centre = field_pad[INNER]
    kappa_centre = kappa_pad[INNER]
    result = REACTION * centre
    for offset_slice in NEIGHBOURS:
        result = result + 0.5 * (kappa_centre + kappa_pad[offset_slice]) * (
            centre - field_pad[offset_slice]
        )
    return result


def face_grad(adjoint_pad, field_pad):
    adjoint_centre = adjoint_pad[INNER]
    field_centre = field_pad[INNER]
    total = jnp.zeros_like(field_centre)
    for offset_slice in NEIGHBOURS:
        total = total + (adjoint_centre - adjoint_pad[offset_slice]) * (
            field_centre - field_pad[offset_slice]
        )
    return 0.5 * total


def pad_plane(block):
    return jnp.pad(block, ((0, 0), (1, 1), (1, 1)))


def pair_sum(block):
    shaped = block.reshape(block.shape[0] // 2, 2, block.shape[1], block.shape[2])
    return shaped[:, 0] + shaped[:, 1]


def neighbours(stacked, reach_kind, stride):
    if reach_kind == "near":
        return extended(stacked, ((("grp", "dev"), 1),), 1)
    below = shifted(stacked, ("grp", "dev"), stride)
    above = shifted(stacked, ("grp", "dev"), -stride)
    return jnp.concatenate([below, stacked, above], axis=1)


def on_device(right_side, cotangent, texture, labels, coef_table):
    coef_row = lax.all_gather(coef_table, "dev", axis=1, tiled=True)
    label_count = coef_row.shape[1]
    onehot = (labels[..., None] == jnp.arange(label_count, dtype=jnp.int32)).astype(jnp.float32)
    tile_coef = jnp.sum(onehot * coef_row[0], axis=-1)
    tile_width = right_side.shape[2] // labels.shape[2]
    kappa_zero = jnp.repeat(tile_coef, tile_width, axis=2) * texture
    layouts = []
    cell_count = right_side.shape[0]
    while cell_count > 1:
        layouts.append(("near", 1, "halve", 0))
        cell_count = cell_count // 2
    merge_bits = lax.axis_size("dev").bit_length() - 1
    for merge_bit in range(merge_bits):
        layouts.append(("near" if merge_bit == 0 else "far", 2**merge_bit, "merge", merge_bit))
    coarse_kpad_apart = None
    saved = []
    level_source = right_side
    kappa_level = kappa_zero
    for level, layout in enumerate(layouts):
        reach_kind, stride, how_coarse, merge_bit = layout
        smoothed = RELAX * level_source
        operand = jnp.stack([smoothed, kappa_level])
        widened = neighbours(operand, reach_kind, stride)
        smooth_pad = pad_plane(widened[0])
        kappa_pad = pad_plane(widened[1])
        residual = level_source - stencil(smooth_pad, kappa_pad)
        saved.append((level_source, smooth_pad, kappa_pad))
        if how_coarse == "halve":
            next_source = pair_sum(residual) * 0.5
            next_kappa = pair_sum(kappa_level) * 0.5
        else:
            operand = jnp.stack([residual, kappa_level])
            partner = swapped(operand, "dev", merge_bit)
            next_source = (residual + partner[0]) * 0.5
            next_kappa = (kappa_level + partner[1]) * 0.5
        level_source = next_source
        kappa_level = next_kappa
    coarse_source = level_source
    states = []
    coarse_kpad = coarse_kpad_apart
    iterate = RELAX * coarse_source
    for sweep_index in range(SWEEPS - 1):
        ride_along = sweep_index == 0
        operand = jnp.stack([iterate, kappa_level]) if ride_along else iterate[None]
        widened = extended(operand, (("grp", 1),), 1)
        iterate_pad = pad_plane(widened[0])
        if ride_along:
            coarse_kpad = pad_plane(widened[1])
        states.append(iterate_pad)
        iterate = iterate + RELAX * (coarse_source - stencil(iterate_pad, coarse_kpad))

    def coarse_adjoint(adjoint):
        source_adj = jnp.zeros_like(adjoint)
        kappa_adj = jnp.zeros_like(adjoint)
        for sweep_index in reversed(range(SWEEPS - 1)):
            source_adj = source_adj + RELAX * adjoint
            adjoint_pad = pad_plane(extended(adjoint[None], (("grp", 1),), 1)[0])
            kappa_adj = kappa_adj - RELAX * face_grad(adjoint_pad, states[sweep_index])
            adjoint = adjoint - RELAX * stencil(adjoint_pad, coarse_kpad)
        source_adj = source_adj + RELAX * adjoint
        return (source_adj, kappa_adj)

    corrected_pads = [None] * len(layouts)
    correction = iterate
    for level in reversed(range(len(layouts))):
        reach_kind, stride, how_coarse, merge_bit = layouts[level]
        level_source, smooth_pad, kappa_pad = saved[level]
        fine_correction = jnp.repeat(correction, 2, axis=0) if how_coarse == "halve" else correction
        corrected = smooth_pad[INNER] + fine_correction
        corrected_pad = pad_plane(neighbours(corrected[None], reach_kind, stride)[0])
        corrected_pads[level] = corrected_pad
        if level > 0:
            correction = corrected + RELAX * (level_source - stencil(corrected_pad, kappa_pad))
    adjoint = cotangent
    partial_terms = []
    for level, layout in enumerate(layouts):
        reach_kind, stride, how_coarse, merge_bit = layout
        level_source, smooth_pad, kappa_pad = saved[level]
        source_part = RELAX * adjoint
        adjoint_pad = pad_plane(neighbours(adjoint[None], reach_kind, stride)[0])
        kappa_part = -(RELAX * face_grad(adjoint_pad, corrected_pads[level]))
        corrected_adj = adjoint - RELAX * stencil(adjoint_pad, kappa_pad)
        partial_terms.append((source_part, corrected_adj, kappa_part))
        if how_coarse == "halve":
            adjoint = pair_sum(corrected_adj)
        else:
            adjoint = corrected_adj + swapped(corrected_adj, "dev", merge_bit)
    source_adj, kappa_adj = coarse_adjoint(adjoint)
    for level in reversed(range(len(layouts))):
        reach_kind, stride, how_coarse, merge_bit = layouts[level]
        level_source, smooth_pad, kappa_pad = saved[level]
        source_part, smooth_adj, kappa_part = partial_terms[level]
        if how_coarse == "halve":
            residual_adj = jnp.repeat(source_adj, 2, axis=0) * 0.5
            kappa_from = jnp.repeat(kappa_adj, 2, axis=0) * 0.5
        else:
            residual_adj = source_adj * 0.5
            kappa_from = kappa_adj * 0.5
        residual_pad = pad_plane(neighbours(residual_adj[None], reach_kind, stride)[0])
        smooth_adj = smooth_adj - stencil(residual_pad, kappa_pad)
        kappa_adj = kappa_part - face_grad(residual_pad, smooth_pad) + kappa_from
        source_adj = source_part + residual_adj + RELAX * smooth_adj
    weighted = kappa_adj * texture
    tile_sums = jnp.sum(
        weighted.reshape(weighted.shape[0], weighted.shape[1], labels.shape[2], tile_width), axis=-1
    )
    label_sums = jnp.sum(onehot * tile_sums[..., None], axis=(0, 1, 2))
    table_grad = lax.psum_scatter(label_sums[None], "dev", scatter_dimension=1, tiled=True)
    return (source_adj, table_grad)


def solution(mesh):
    in_specs = (
        P(("grp", "dev"), None, None),
        P(("grp", "dev"), None, None),
        P(("grp", "dev"), None, None),
        P(("grp", "dev"), None, None),
        P("grp", "dev"),
    )
    out_specs = (P(("grp", "dev"), None, None), P("grp", "dev"))
    return jax.shard_map(
        on_device, mesh=mesh, in_specs=in_specs, out_specs=out_specs, check_vma=False
    )
```

profile of v0, /device:TPU:1, one launch (start us, length us, event | category | flops | bytes accessed | tf_op | source)
XLA Modules:
  0.0 593.1 jit_solution(12291878168189582265)
XLA Ops:
  2.7 64.3 %all-reduce.42 = f32[64]{0:T(128)S(1)} all-reduce(f32[64]{0:T(128)S(1)} %bitcast_dynamic-update-slice_fusion), channel_id=1, replica_groups=mesh['grp'=8,'dev'=32] {'dev'}, use_global_device_ids=true, to_apply=%add.42 | all-reduce | flops 64 | bytes 512
  71.3 16.1 %collective-permute-start.2 = (f32[2,1,32,256]{3,2,1,0:T(8,128)S(1)}, f32[2,1,32,256]{3,2,1,0:T(8,128)S(1)}, u32[]{:S(2)}, u32[]{:S(2)}) collective-permute-start(f32[2,1,32,256]{3,2,1,0:T(8,128)S(1)} %get-tuple-element.89), channel_id=1, source_target_pairs={{1,0},{2,1},{3,2},{4,3},{5,4},{6,5},{7,6},{8,7},{9,8},{10,9},{11,1... | collective-permute-start | bytes 196616 | tf_op jit(solution)/shard_map/ppermute | solution.py:32
  91.6 7.6 %collective-permute-start.6 = (f32[2,1,32,256]{3,2,1,0:T(8,128)S(1)}, f32[2,1,32,256]{3,2,1,0:T(8,128)S(1)}, u32[]{:S(2)}, u32[]{:S(2)}) collective-permute-start(f32[2,1,32,256]{3,2,1,0:T(8,128)S(1)} %get-tuple-element.107), channel_id=1, source_target_pairs={{1,0},{2,1},{3,2},{4,3},{5,4},{6,5},{7,6},{8,7},{9,8},{10,9},{11,1... | collective-permute-start | bytes 196616 | tf_op jit(solution)/shard_map/ppermute | solution.py:32
  101.4 7.6 %collective-permute-start.10 = (f32[2,1,32,256]{3,2,1,0:T(8,128)S(1)}, f32[2,1,32,256]{3,2,1,0:T(8,128)S(1)}, u32[]{:S(2)}, u32[]{:S(2)}) collective-permute-start(f32[2,1,32,256]{3,2,1,0:T(8,128)S(1)} %pad_maximum_fusion.19), channel_id=1, source_target_pairs={{1,0},{2,1},{3,2},{4,3},{5,4},{6,5},{7,6},{8,7},{9,8},{10,9},{11,1... | collective-permute-start | bytes 196616 | tf_op jit(solution)/shard_map/ppermute | solution.py:32
  110.9 7.0 %collective-permute-done.8 = f32[2,1,32,256]{3,2,1,0:T(8,128)S(1)} collective-permute-done((f32[2,1,32,256]{3,2,1,0:T(8,128)S(1)}, f32[2,1,32,256]{3,2,1,0:T(8,128)S(1)}, u32[]{:S(2)}, u32[]{:S(2)}) %collective-permute-start.8) | collective-permute-done | bytes 65568 | tf_op jit(solution)/shard_map/ppermute | solution.py:30
  152.5 12.6 %collective-permute-start.28 = (f32[2,1,32,256]{3,2,1,0:T(8,128)S(1)}, f32[2,1,32,256]{3,2,1,0:T(8,128)S(1)}, u32[]{:S(2)}, u32[]{:S(2)}) collective-permute-start(f32[2,1,32,256]{3,2,1,0:T(8,128)S(1)} %pad_maximum_fusion.25), channel_id=1, source_target_pairs={{8,0},{9,1},{10,2},{11,3},{12,4},{13,5},{14,6},{15,7},{16,8},{17,9... | collective-permute-start | bytes 196616 | tf_op jit(solution)/shard_map/ppermute | solution.py:42
  167.1 6.1 %collective-permute-done.26 = f32[2,1,32,256]{3,2,1,0:T(8,128)S(1)} collective-permute-done((f32[2,1,32,256]{3,2,1,0:T(8,128)S(1)}, f32[2,1,32,256]{3,2,1,0:T(8,128)S(1)}, u32[]{:S(2)}, u32[]{:S(2)}) %collective-permute-start.26) | collective-permute-done | bytes 65568 | tf_op jit(solution)/shard_map/ppermute | solution.py:42
  178.0 7.2 %collective-permute-start.34 = (f32[2,1,32,256]{3,2,1,0:T(8,128)S(1)}, f32[2,1,32,256]{3,2,1,0:T(8,128)S(1)}, u32[]{:S(2)}, u32[]{:S(2)}) collective-permute-start(f32[2,1,32,256]{3,2,1,0:T(8,128)S(1)} %pad_maximum_fusion.27), channel_id=1, source_target_pairs={{16,0},{17,1},{18,2},{19,3},{20,4},{21,5},{22,6},{23,7},{24,8},{25... | collective-permute-start | bytes 196616 | tf_op jit(solution)/shard_map/ppermute | solution.py:42
  187.7 7.1 %collective-permute-done.32 = f32[2,1,32,256]{3,2,1,0:T(8,128)S(1)} collective-permute-done((f32[2,1,32,256]{3,2,1,0:T(8,128)S(1)}, f32[2,1,32,256]{3,2,1,0:T(8,128)S(1)}, u32[]{:S(2)}, u32[]{:S(2)}) %collective-permute-start.32) | collective-permute-done | bytes 65568 | tf_op jit(solution)/shard_map/ppermute | solution.py:42
  196.0 6.6 %collective-permute-done.37 = f32[2,1,32,256]{3,2,1,0:T(8,128)S(1)} collective-permute-done((f32[2,1,32,256]{3,2,1,0:T(8,128)S(1)}, f32[2,1,32,256]{3,2,1,0:T(8,128)S(1)}, u32[]{:S(2)}, u32[]{:S(2)}) %collective-permute-start.37) | collective-permute-done | bytes 65568 | tf_op jit(solution)/shard_map/ppermute | solution.py:48
  204.6 6.2 %collective-permute-start.38 = (f32[2,1,32,256]{3,2,1,0:T(8,128)S(1)}, f32[2,1,32,256]{3,2,1,0:T(8,128)S(1)}, u32[]{:S(2)}, u32[]{:S(2)}) collective-permute-start(f32[2,1,32,256]{3,2,1,0:T(8,128)S(1)} %pad_maximum_fusion.41), channel_id=1, source_target_pairs={{0,32},{32,64},{64,96},{96,128},{128,160},{160,192},{192,224},{1,3... | collective-permute-start | bytes 196616 | tf_op jit(solution)/shard_map/ppermute | solution.py:30
  241.6 5.7 collective-permute-start.3
  254.8 5.3 collective-permute-done.66
  290.0 6.5 %collective-permute-start.7 = (f32[1,1,32,256]{3,2,1,0:T(8,128)S(1)}, f32[1,1,32,256]{3,2,1,0:T(8,128)S(1)}, u32[]{:S(2)}, u32[]{:S(2)}) collective-permute-start(f32[1,1,32,256]{3,2,1,0:T(8,128)S(1)} %get-tuple-element.113), channel_id=1, source_target_pairs={{1,0},{2,1},{3,2},{4,3},{5,4},{6,5},{7,6},{8,7},{9,8},{10,9},{11,1... | collective-permute-start | bytes 98312 | tf_op jit(solution)/shard_map/ppermute | solution.py:32
  299.2 7.0 %collective-permute-start.75 = (f32[1,1,32,256]{3,2,1,0:T(8,128)S(1)}, f32[1,1,32,256]{3,2,1,0:T(8,128)S(1)}, u32[]{:S(2)}, u32[]{:S(2)}) collective-permute-start(f32[1,1,32,256]{3,2,1,0:T(8,128)S(1)} %get-tuple-element.111), channel_id=1, source_target_pairs={{1,0},{2,1},{3,2},{4,3},{5,4},{6,5},{7,6},{8,7},{9,8},{10,9},{11,1... | collective-permute-start | bytes 98312 | tf_op jit(solution)/shard_map/ppermute | solution.py:32
  308.6 7.5 %collective-permute-start.11 = (f32[1,1,32,256]{3,2,1,0:T(8,128)S(1)}, f32[1,1,32,256]{3,2,1,0:T(8,128)S(1)}, u32[]{:S(2)}, u32[]{:S(2)}) collective-permute-start(f32[1,1,32,256]{3,2,1,0:T(8,128)S(1)} %slice_add_fusion.8), channel_id=1, source_target_pairs={{1,0},{2,1},{3,2},{4,3},{5,4},{6,5},{7,6},{8,7},{9,8},{10,9},{11,1... | collective-permute-start | bytes 98312 | tf_op jit(solution)/shard_map/ppermute | solution.py:32
  318.1 6.6 %collective-permute-done.9 = f32[1,1,32,256]{3,2,1,0:T(8,128)S(1)} collective-permute-done((f32[1,1,32,256]{3,2,1,0:T(8,128)S(1)}, f32[1,1,32,256]{3,2,1,0:T(8,128)S(1)}, u32[]{:S(2)}, u32[]{:S(2)}) %collective-permute-start.9) | collective-permute-done | bytes 32800 | tf_op jit(solution)/shard_map/ppermute | solution.py:30
  358.0 9.8 %collective-permute-start.29 = (f32[1,1,32,256]{3,2,1,0:T(8,128)S(1)}, f32[1,1,32,256]{3,2,1,0:T(8,128)S(1)}, u32[]{:S(2)}, u32[]{:S(2)}) collective-permute-start(f32[1,1,32,256]{3,2,1,0:T(8,128)S(1)} %bitcast.1383), channel_id=1, source_target_pairs={{8,0},{9,1},{10,2},{11,3},{12,4},{13,5},{14,6},{15,7},{16,8},{17,9... | collective-permute-start | bytes 98312 | tf_op jit(solution)/shard_map/ppermute | solution.py:42
  369.8 5.4 collective-permute-done.27
  380.1 5.8 collective-permute-start.35
  404.9 10.0 %collective-permute-start.39 = (f32[1,1,32,256]{3,2,1,0:T(8,128)S(1)}, f32[1,1,32,256]{3,2,1,0:T(8,128)S(1)}, u32[]{:S(2)}, u32[]{:S(2)}) collective-permute-start(f32[1,1,32,256]{3,2,1,0:T(8,128)S(1)} %bitcast.1390), channel_id=1, source_target_pairs={{0,32},{32,64},{64,96},{96,128},{128,160},{160,192},{192,224},{1,3... | collective-permute-start | bytes 98312 | tf_op jit(solution)/shard_map/ppermute | solution.py:30
  478.7 7.1 %collective-permute-start.77 = (f32[1,1,32,256]{3,2,1,0:T(8,128)S(1)}, f32[1,1,32,256]{3,2,1,0:T(8,128)S(1)}, u32[]{:S(2)}, u32[]{:S(2)}) collective-permute-start(f32[1,1,32,256]{3,2,1,0:T(8,128)S(1)} %get-tuple-element.103), channel_id=1, source_target_pairs={{1,0},{2,1},{3,2},{4,3},{5,4},{6,5},{7,6},{8,7},{9,8},{10,9},{11,1... | collective-permute-start | bytes 98312 | tf_op jit(solution)/shard_map/ppermute | solution.py:32
  511.7 7.0 %collective-permute-start.59 = (f32[1,1,32,256]{3,2,1,0:T(8,128)S(1)}, f32[1,1,32,256]{3,2,1,0:T(8,128)S(1)}, u32[]{:S(2)}, u32[]{:S(2)}) collective-permute-start(f32[1,1,32,256]{3,2,1,0:T(8,128)S(1)} %get-tuple-element.105), channel_id=1, source_target_pairs={{1,0},{2,1},{3,2},{4,3},{5,4},{6,5},{7,6},{8,7},{9,8},{10,9},{11,1... | collective-permute-start | bytes 98312 | tf_op jit(solution)/shard_map/ppermute | solution.py:32
  521.0 70.7 %all-reduce.43 = f32[1,64]{1,0:T(1,128)S(1)} all-reduce(f32[1,64]{1,0:T(1,128)S(1)} %bitcast.1425), channel_id=2, replica_groups=mesh['grp'=8,'dev'=32] {'dev'}, use_global_device_ids=true, to_apply=%region_3.4.clone | all-reduce | flops 64 | bytes 512
  (636 shorter events, 284.8 us)
Async XLA Ops:
  69.4 18.1 %collective-permute-start = (f32[2,1,32,256]{3,2,1,0:T(8,128)S(1)}, f32[2,1,32,256]{3,2,1,0:T(8,128)S(1)}, u32[]{:S(2)}, u32[]{:S(2)}) collective-permute-start(f32[2,1,32,256]{3,2,1,0:T(8,128)S(1)} %get-tuple-element.88), channel_id=1, source_target_pairs={{0,1},{1,2},{2,3},{3,4},{4,5},{5,6},{6,7},{7,8},{8,9},{9,10},{10,1... | collective-permute-start | bytes 196616 | tf_op jit(solution)/shard_map/ppermute | solution.py:30
  71.3 17.4 %collective-permute-start.2 = (f32[2,1,32,256]{3,2,1,0:T(8,128)S(1)}, f32[2,1,32,256]{3,2,1,0:T(8,128)S(1)}, u32[]{:S(2)}, u32[]{:S(2)}) collective-permute-start(f32[2,1,32,256]{3,2,1,0:T(8,128)S(1)} %get-tuple-element.89), channel_id=1, source_target_pairs={{1,0},{2,1},{3,2},{4,3},{5,4},{6,5},{7,6},{8,7},{9,8},{10,9},{11,1... | collective-permute-start | bytes 196616 | tf_op jit(solution)/shard_map/ppermute | solution.py:32
  89.6 9.5 %collective-permute-start.4 = (f32[2,1,32,256]{3,2,1,0:T(8,128)S(1)}, f32[2,1,32,256]{3,2,1,0:T(8,128)S(1)}, u32[]{:S(2)}, u32[]{:S(2)}) collective-permute-start(f32[2,1,32,256]{3,2,1,0:T(8,128)S(1)} %get-tuple-element.106), channel_id=1, source_target_pairs={{0,1},{1,2},{2,3},{3,4},{4,5},{5,6},{6,7},{7,8},{8,9},{9,10},{10,1... | collective-permute-start | bytes 196616 | tf_op jit(solution)/shard_map/ppermute | solution.py:30
  101.4 9.5 %collective-permute-start.10 = (f32[2,1,32,256]{3,2,1,0:T(8,128)S(1)}, f32[2,1,32,256]{3,2,1,0:T(8,128)S(1)}, u32[]{:S(2)}, u32[]{:S(2)}) collective-permute-start(f32[2,1,32,256]{3,2,1,0:T(8,128)S(1)} %pad_maximum_fusion.19), channel_id=1, source_target_pairs={{1,0},{2,1},{3,2},{4,3},{5,4},{6,5},{7,6},{8,7},{9,8},{10,9},{11,1... | collective-permute-start | bytes 196616 | tf_op jit(solution)/shard_map/ppermute | solution.py:32
  152.5 14.5 %collective-permute-start.28 = (f32[2,1,32,256]{3,2,1,0:T(8,128)S(1)}, f32[2,1,32,256]{3,2,1,0:T(8,128)S(1)}, u32[]{:S(2)}, u32[]{:S(2)}) collective-permute-start(f32[2,1,32,256]{3,2,1,0:T(8,128)S(1)} %pad_maximum_fusion.25), channel_id=1, source_target_pairs={{8,0},{9,1},{10,2},{11,3},{12,4},{13,5},{14,6},{15,7},{16,8},{17,9... | collective-permute-start | bytes 196616 | tf_op jit(solution)/shard_map/ppermute | solution.py:42
  178.0 9.7 %collective-permute-start.34 = (f32[2,1,32,256]{3,2,1,0:T(8,128)S(1)}, f32[2,1,32,256]{3,2,1,0:T(8,128)S(1)}, u32[]{:S(2)}, u32[]{:S(2)}) collective-permute-start(f32[2,1,32,256]{3,2,1,0:T(8,128)S(1)} %pad_maximum_fusion.27), channel_id=1, source_target_pairs={{16,0},{17,1},{18,2},{19,3},{20,4},{21,5},{22,6},{23,7},{24,8},{25... | collective-permute-start | bytes 196616 | tf_op jit(solution)/shard_map/ppermute | solution.py:42
  185.2 9.5 %collective-permute-start.32 = (f32[2,1,32,256]{3,2,1,0:T(8,128)S(1)}, f32[2,1,32,256]{3,2,1,0:T(8,128)S(1)}, u32[]{:S(2)}, u32[]{:S(2)}) collective-permute-start(f32[2,1,32,256]{3,2,1,0:T(8,128)S(1)} %pad_maximum_fusion.27), channel_id=1, source_target_pairs={{0,16},{1,17},{2,18},{3,19},{4,20},{5,21},{6,22},{7,23},{8,24},{9,... | collective-permute-start | bytes 196616 | tf_op jit(solution)/shard_map/ppermute | solution.py:42
  229.3 18.1 %collective-permute-start.65 = (f32[1,1,32,256]{3,2,1,0:T(8,128)S(1)}, f32[1,1,32,256]{3,2,1,0:T(8,128)S(1)}, u32[]{:S(2)}, u32[]{:S(2)}) collective-permute-start(f32[1,1,32,256]{3,2,1,0:T(8,128)S(1)} %bitcast.1407), channel_id=1, source_target_pairs={{16,0},{17,1},{18,2},{19,3},{20,4},{21,5},{22,6},{23,7},{24,8},{25... | collective-permute-start | bytes 98312 | tf_op jit(solution)/shard_map/ppermute | solution.py:42
  234.2 13.2 %collective-permute-start.64 = (f32[1,1,32,256]{3,2,1,0:T(8,128)S(1)}, f32[1,1,32,256]{3,2,1,0:T(8,128)S(1)}, u32[]{:S(2)}, u32[]{:S(2)}) collective-permute-start(f32[1,1,32,256]{3,2,1,0:T(8,128)S(1)} %bitcast.1408), channel_id=1, source_target_pairs={{0,16},{1,17},{2,18},{3,19},{4,20},{5,21},{6,22},{7,23},{8,24},{9,... | collective-permute-start | bytes 98312 | tf_op jit(solution)/shard_map/ppermute | solution.py:42
  238.5 16.3 %collective-permute-start.1 = (f32[1,1,32,256]{3,2,1,0:T(8,128)S(1)}, f32[1,1,32,256]{3,2,1,0:T(8,128)S(1)}, u32[]{:S(2)}, u32[]{:S(2)}) collective-permute-start(f32[1,1,32,256]{3,2,1,0:T(8,128)S(1)} %get-tuple-element.108), channel_id=1, source_target_pairs={{0,1},{1,2},{2,3},{3,4},{4,5},{5,6},{6,7},{7,8},{8,9},{9,10},{10,1... | collective-permute-start | bytes 98312 | tf_op jit(solution)/shard_map/ppermute | solution.py:30
  241.6 13.1 %collective-permute-start.3 = (f32[1,1,32,256]{3,2,1,0:T(8,128)S(1)}, f32[1,1,32,256]{3,2,1,0:T(8,128)S(1)}, u32[]{:S(2)}, u32[]{:S(2)}) collective-permute-start(f32[1,1,32,256]{3,2,1,0:T(8,128)S(1)} %get-tuple-element.109), channel_id=1, source_target_pairs={{1,0},{2,1},{3,2},{4,3},{5,4},{6,5},{7,6},{8,7},{9,8},{10,9},{11,1... | collective-permute-start | bytes 98312 | tf_op jit(solution)/shard_map/ppermute | solution.py:32
  282.3 14.2 %collective-permute-start.73 = (f32[1,1,32,256]{3,2,1,0:T(8,128)S(1)}, f32[1,1,32,256]{3,2,1,0:T(8,128)S(1)}, u32[]{:S(2)}, u32[]{:S(2)}) collective-permute-start(f32[1,1,32,256]{3,2,1,0:T(8,128)S(1)} %bitcast.1401), channel_id=1, source_target_pairs={{1,0},{2,1},{3,2},{4,3},{5,4},{6,5},{7,6},{8,7},{9,8},{10,9},{11,1... | collective-permute-start | bytes 98312 | tf_op jit(solution)/shard_map/ppermute | solution.py:32
  284.2 12.3 %collective-permute-start.72 = (f32[1,1,32,256]{3,2,1,0:T(8,128)S(1)}, f32[1,1,32,256]{3,2,1,0:T(8,128)S(1)}, u32[]{:S(2)}, u32[]{:S(2)}) collective-permute-start(f32[1,1,32,256]{3,2,1,0:T(8,128)S(1)} %bitcast.1402), channel_id=1, source_target_pairs={{0,1},{1,2},{2,3},{3,4},{4,5},{5,6},{6,7},{7,8},{8,9},{9,10},{10,1... | collective-permute-start | bytes 98312 | tf_op jit(solution)/shard_map/ppermute | solution.py:30
  287.6 18.6 %collective-permute-start.5 = (f32[1,1,32,256]{3,2,1,0:T(8,128)S(1)}, f32[1,1,32,256]{3,2,1,0:T(8,128)S(1)}, u32[]{:S(2)}, u32[]{:S(2)}) collective-permute-start(f32[1,1,32,256]{3,2,1,0:T(8,128)S(1)} %get-tuple-element.112), channel_id=1, source_target_pairs={{0,1},{1,2},{2,3},{3,4},{4,5},{5,6},{6,7},{7,8},{8,9},{9,10},{10,1... | collective-permute-start | bytes 98312 | tf_op jit(solution)/shard_map/ppermute | solution.py:30
  290.0 16.2 %collective-permute-start.7 = (f32[1,1,32,256]{3,2,1,0:T(8,128)S(1)}, f32[1,1,32,256]{3,2,1,0:T(8,128)S(1)}, u32[]{:S(2)}, u32[]{:S(2)}) collective-permute-start(f32[1,1,32,256]{3,2,1,0:T(8,128)S(1)} %get-tuple-element.113), channel_id=1, source_target_pairs={{1,0},{2,1},{3,2},{4,3},{5,4},{6,5},{7,6},{8,7},{9,8},{10,9},{11,1... | collective-permute-start | bytes 98312 | tf_op jit(solution)/shard_map/ppermute | solution.py:32
  308.6 9.5 %collective-permute-start.11 = (f32[1,1,32,256]{3,2,1,0:T(8,128)S(1)}, f32[1,1,32,256]{3,2,1,0:T(8,128)S(1)}, u32[]{:S(2)}, u32[]{:S(2)}) collective-permute-start(f32[1,1,32,256]{3,2,1,0:T(8,128)S(1)} %slice_add_fusion.8), channel_id=1, source_target_pairs={{1,0},{2,1},{3,2},{4,3},{5,4},{6,5},{7,6},{8,7},{9,8},{10,9},{11,1... | collective-permute-start | bytes 98312 | tf_op jit(solution)/shard_map/ppermute | solution.py:32
  358.0 11.8 %collective-permute-start.29 = (f32[1,1,32,256]{3,2,1,0:T(8,128)S(1)}, f32[1,1,32,256]{3,2,1,0:T(8,128)S(1)}, u32[]{:S(2)}, u32[]{:S(2)}) collective-permute-start(f32[1,1,32,256]{3,2,1,0:T(8,128)S(1)} %bitcast.1383), channel_id=1, source_target_pairs={{8,0},{9,1},{10,2},{11,3},{12,4},{13,5},{14,6},{15,7},{16,8},{17,9... | collective-permute-start | bytes 98312 | tf_op jit(solution)/shard_map/ppermute | solution.py:42
  380.1 10.3 %collective-permute-start.35 = (f32[1,1,32,256]{3,2,1,0:T(8,128)S(1)}, f32[1,1,32,256]{3,2,1,0:T(8,128)S(1)}, u32[]{:S(2)}, u32[]{:S(2)}) collective-permute-start(f32[1,1,32,256]{3,2,1,0:T(8,128)S(1)} %bitcast.1386), channel_id=1, source_target_pairs={{16,0},{17,1},{18,2},{19,3},{20,4},{21,5},{22,6},{23,7},{24,8},{25... | collective-permute-start | bytes 98312 | tf_op jit(solution)/shard_map/ppermute | solution.py:42
  403.0 12.0 %collective-permute-start.41 = (f32[1,1,32,256]{3,2,1,0:T(8,128)S(1)}, f32[1,1,32,256]{3,2,1,0:T(8,128)S(1)}, u32[]{:S(2)}, u32[]{:S(2)}) collective-permute-start(f32[1,1,32,256]{3,2,1,0:T(8,128)S(1)} %bitcast.1389), channel_id=1, source_target_pairs={{32,0},{64,32},{96,64},{128,96},{160,128},{192,160},{224,192},{33,... | collective-permute-start | bytes 98312 | tf_op jit(solution)/shard_map/ppermute | solution.py:32
  404.9 11.0 %collective-permute-start.39 = (f32[1,1,32,256]{3,2,1,0:T(8,128)S(1)}, f32[1,1,32,256]{3,2,1,0:T(8,128)S(1)}, u32[]{:S(2)}, u32[]{:S(2)}) collective-permute-start(f32[1,1,32,256]{3,2,1,0:T(8,128)S(1)} %bitcast.1390), channel_id=1, source_target_pairs={{0,32},{32,64},{64,96},{96,128},{128,160},{160,192},{192,224},{1,3... | collective-permute-start | bytes 98312 | tf_op jit(solution)/shard_map/ppermute | solution.py:30
  469.9 15.9 %collective-permute-start.53 = (f32[1,1,32,256]{3,2,1,0:T(8,128)S(1)}, f32[1,1,32,256]{3,2,1,0:T(8,128)S(1)}, u32[]{:S(2)}, u32[]{:S(2)}) collective-permute-start(f32[1,1,32,256]{3,2,1,0:T(8,128)S(1)} %get-tuple-element.15), channel_id=1, source_target_pairs={{2,0},{3,1},{4,2},{5,3},{6,4},{7,5},{8,6},{9,7},{10,8},{11,9},{12,... | collective-permute-start | bytes 98312 | tf_op jit(solution)/shard_map/ppermute | solution.py:42
  472.9 13.0 %collective-permute-start.52 = (f32[1,1,32,256]{3,2,1,0:T(8,128)S(1)}, f32[1,1,32,256]{3,2,1,0:T(8,128)S(1)}, u32[]{:S(2)}, u32[]{:S(2)}) collective-permute-start(f32[1,1,32,256]{3,2,1,0:T(8,128)S(1)} %get-tuple-element.15), channel_id=1, source_target_pairs={{0,2},{1,3},{2,4},{3,5},{4,6},{5,7},{6,8},{7,9},{8,10},{9,11},{10,... | collective-permute-start | bytes 98312 | tf_op jit(solution)/shard_map/ppermute | solution.py:42
  476.8 14.8 %collective-permute-start.76 = (f32[1,1,32,256]{3,2,1,0:T(8,128)S(1)}, f32[1,1,32,256]{3,2,1,0:T(8,128)S(1)}, u32[]{:S(2)}, u32[]{:S(2)}) collective-permute-start(f32[1,1,32,256]{3,2,1,0:T(8,128)S(1)} %get-tuple-element.102), channel_id=1, source_target_pairs={{0,1},{1,2},{2,3},{3,4},{4,5},{5,6},{6,7},{7,8},{8,9},{9,10},{10,1... | collective-permute-start | bytes 98312 | tf_op jit(solution)/shard_map/ppermute | solution.py:30
  478.7 12.8 %collective-permute-start.77 = (f32[1,1,32,256]{3,2,1,0:T(8,128)S(1)}, f32[1,1,32,256]{3,2,1,0:T(8,128)S(1)}, u32[]{:S(2)}, u32[]{:S(2)}) collective-permute-start(f32[1,1,32,256]{3,2,1,0:T(8,128)S(1)} %get-tuple-element.103), channel_id=1, source_target_pairs={{1,0},{2,1},{3,2},{4,3},{5,4},{6,5},{7,6},{8,7},{9,8},{10,9},{11,1... | collective-permute-start | bytes 98312 | tf_op jit(solution)/shard_map/ppermute | solution.py:32
  (237 other events, 5930.2 us)
where the time goes:
time: 605 us; the launch traced here: 593 us
  starting transfers between devices  283 us (47%)
  blocking collectives  135 us (22%)
  waiting for transfers between devices  131 us (22%)
  local copies, waits for them, and re-layouts  24.1 us (4%)
  other arithmetic  14.6 us (2%)
    unnamed x2, blocking collectives  135 us
    ppermute x32, starting transfers between devices, shifted(): return lax.ppermute(block, axis, route)  125 us
    ppermute x18, starting transfers between devices, extended(): lax.ppermute(head, axis, [((i + 1) % count, i) for i in range(ends)])  89.5 us
    ppermute x18, starting transfers between devices, extended(): lax.ppermute(tail, axis, [(i, (i + 1) % count) for i in range(ends)])  62.4 us
    ppermute x32, waiting for transfers between devices, shifted(): return lax.ppermute(block, axis, route)  62.4 us
    ppermute x10, waiting for transfers between devices, swapped(): return lax.ppermute(value, axis, pairs)  36.7 us
    ppermute x18, waiting for transfers between devices, extended(): lax.ppermute(tail, axis, [(i, (i + 1) % count) for i in range(ends)])  27.4 us
    unnamed x370, local copies, waits for them, and re-layouts  23.3 us
  transfers between devices with their start and end apart: 78, of which 39 were waited for; matrix products, arithmetic and copies ran while one was open for 1% of the time, Pallas kernels for 0%

commit v1 on v0

v1 whole, which is shorter than its diff:
```python
import jax
import jax.numpy as jnp
from jax import lax
from jax.experimental import pallas as pl
from jax.experimental.pallas import tpu as pltpu
from jax.sharding import PartitionSpec as P


GD = ("grp", "dev")
F32 = jnp.float32
NY = 32
NZ = 256
TILE = 128
PLANE = (NY, NZ)
TRIPLE = (3,) + PLANE


def at_next(value, axis):
    return pltpu.roll(value, value.shape[axis] - 1, axis)


def at_prev(value, axis):
    return pltpu.roll(value, 1, axis)


class Grid:
    def __init__(self):
        row = lax.broadcasted_iota(jnp.int32, PLANE, 0)
        col = lax.broadcasted_iota(jnp.int32, PLANE, 1)
        one = lambda cond: jnp.where(cond, 1.0, 0.0).astype(F32)
        self.has_y = one(row < NY - 1)
        self.has_z = one(col < NZ - 1)
        self.ends = one(row == 0) + one(row == NY - 1) + one(col == 0) + one(col == NZ - 1)


def smooth_planes(grid, k_prev, k_here, k_next, fields):
    w_prev = 0.1 * (k_prev + k_here)
    w_next = 0.1 * (k_here + k_next)
    w_y = 0.1 * (k_here + at_next(k_here, 0)) * grid.has_y
    w_z = 0.1 * (k_here + at_next(k_here, 1)) * grid.has_z
    diag = 0.98 - 0.1 * k_here * grid.ends
    out = []
    for s_prev, s_here, s_next in fields:
        flux_y = w_y * (at_next(s_here, 0) - s_here)
        flux_z = w_z * (at_next(s_here, 1) - s_here)
        total = diag * s_here + w_next * (s_next - s_here) - w_prev * (s_here - s_prev)
        total = total + (flux_y - at_prev(flux_y, 0)) + (flux_z - at_prev(flux_z, 1))
        out.append(total)
    return out


def face_products(grid, a, b):
    a_prev, a_here, a_next = a
    b_prev, b_here, b_next = b
    prod_y = (at_next(a_here, 0) - a_here) * (at_next(b_here, 0) - b_here) * grid.has_y
    prod_z = (at_next(a_here, 1) - a_here) * (at_next(b_here, 1) - b_here) * grid.has_z
    total = a_here * b_here * grid.ends
    total = total + (a_next - a_here) * (b_next - b_here) + (a_here - a_prev) * (b_here - b_prev)
    return total + (prod_y + at_prev(prod_y, 0)) + (prod_z + at_prev(prod_z, 1))


def flag(cond):
    return jnp.where(cond, 1.0, 0.0).astype(F32)


def halve(grid, get, low):
    planes = [get(low + i) for i in (-1, 0, 1, 2)]
    rests = []
    for i in (1, 2):
        before, here, after = planes[i - 1], planes[i], planes[i + 1]
        rests.append(
            smooth_planes(
                grid,
                before[2],
                here[2],
                after[2],
                [(before[f], here[f], after[f]) for f in (0, 1)],
            )
        )
    coarse = [0.5 * (rests[0][f] + rests[1][f]) for f in (0, 1)]
    return coarse + [0.5 * (planes[1][2] + planes[2][2])]


def two_levels(grid, get, lo_ok, hi_ok, mid_ref, out_ref):
    scale = [lo_ok, None, None, hi_ok]
    for q in range(4):
        triple = halve(grid, get, 1 + 2 * q)
        if scale[q] is not None:
            triple = [triple[0] * scale[q], triple[1] * scale[q], triple[2]]
        for f in range(3):
            mid_ref[q, f] = triple[f]

    def mid(p):
        return [mid_ref[p, f] for f in range(3)]

    triple = halve(grid, mid, 1)
    for f in range(3):
        out_ref[f] = triple[f]


def place():
    g = lax.axis_index("grp")
    d = lax.axis_index("dev")
    return g, d // 4, d % 4


def shift(block, axes, distance):
    count = lax.axis_size(axes)
    route = [(i, i + distance) for i in range(count) if 0 <= i + distance < count]
    return lax.ppermute(block, axes, route)


def swap(block, axis, mask):
    return lax.ppermute(block, axis, [(i, i ^ mask) for i in range(lax.axis_size(axis))])


def call(kernel, outs, scratch, *args):
    vmem = pl.BlockSpec(memory_space=pltpu.VMEM)
    return pl.pallas_call(
        kernel,
        out_shape=[jax.ShapeDtypeStruct(shape, F32) for shape in outs],
        in_specs=[vmem] * len(args),
        out_specs=[vmem] * len(outs),
        scratch_shapes=[pltpu.VMEM(shape, F32) for shape in scratch],
    )(*args)


def pack_kernel(s_ref, c_ref, tex_ref, lab_ref, up_ref, down_ref):
    lane = lax.broadcasted_iota(jnp.int32, PLANE, 1)
    for out_ref, first in ((up_ref, 1), (down_ref, 0)):
        marks = jnp.zeros(PLANE, F32)
        for p in range(3):
            out_ref[p] = s_ref[first + p]
            out_ref[3 + p] = c_ref[first + p]
            out_ref[6 + p] = tex_ref[first + p]
            for t in range(2):
                column = lab_ref[first + p, :, t : t + 1].astype(F32)
                marks = jnp.where(lane == 2 * p + t, column, marks)
        out_ref[9] = marks


def fine_kernel(
    s_ref, c_ref, tex_ref, lab_ref, lo_ref, hi_ref, coef_ref,
    kappa_ref, one_ref, two_ref, edge0_ref, edge1_ref, k_ref,
):
    g, z, x = place()
    grid = Grid()
    first = (z == 0) & (x == 0)
    last = (z == 7) & (x == 3)
    row_here = coef_ref[1:2, :]
    row_lo = jnp.where(first, coef_ref[0:1, :], row_here)
    row_hi = jnp.where(last, coef_ref[2:3, :], row_here)
    lane = lax.broadcasted_iota(jnp.int32, (NY, TILE), 1)
    lane_f = lane.astype(F32)

    def looked_up(column, row):
        hit = lane_f == column
        return jnp.sum(jnp.where(hit, row, 0.0), axis=1, keepdims=True)

    for p in range(10):
        for t in range(2):
            if p < 3:
                column, row, tex = lo_ref[9, :, 2 * p + t : 2 * p + t + 1], row_lo, lo_ref[6 + p]
            elif p < 7:
                column, row = lab_ref[p - 3, :, t : t + 1].astype(F32), row_here
                tex = tex_ref[p - 3]
            else:
                q = p - 7
                column, row, tex = hi_ref[9, :, 2 * q + t : 2 * q + t + 1], row_hi, hi_ref[6 + q]
            cut = slice(t * TILE, (t + 1) * TILE)
            k_ref[p, :, cut] = looked_up(column, row) * tex[:, cut]
    for p in range(6):
        kappa_ref[p] = k_ref[2 + p]

    def get(p):
        if p < 3:
            return [lo_ref[p], lo_ref[3 + p], k_ref[p]]
        if p < 7:
            return [s_ref[p - 3], c_ref[p - 3], k_ref[p]]
        return [hi_ref[p - 7], hi_ref[p - 4], k_ref[p]]

    lo_ok = flag(jnp.logical_not(first & (g == 0)))
    hi_ok = flag(jnp.logical_not(last & (g == 7)))
    two_levels(grid, get, lo_ok, hi_ok, one_ref, two_ref)
    for f in range(3):
        edge0_ref[f] = one_ref[1, f]
        edge1_ref[f] = one_ref[2, f]


def order4_kernel(a0_ref, a1_ref, a2_ref, a3_ref, mid_ref, up_ref, down_ref, all_ref):
    g, z, x = place()
    for e, ref in enumerate((a0_ref, a1_ref, a2_ref, a3_ref)):
        all_ref[e] = ref[...]
    for p in range(4):
        triple = all_ref[x ^ p]
        mid_ref[p] = triple
        if p > 0:
            up_ref[p - 1] = triple
        if p < 3:
            down_ref[p] = triple


def block_kernel(
    mid_ref, lo_ref, hi_ref, own_ref, three_ref, four_ref, edge0_ref, edge1_ref, all_ref
):
    g, z, x = place()
    grid = Grid()
    for p in range(3):
        all_ref[p] = lo_ref[p]
        all_ref[7 + p] = hi_ref[p]
    for p in range(4):
        all_ref[3 + p] = mid_ref[p]
    for d in range(5):
        own_ref[d] = all_ref[x + 1 + d]

    def get(p):
        return [all_ref[p, f] for f in range(3)]

    lo_ok = flag(jnp.logical_not((z == 0) & (g == 0)))
    hi_ok = flag(jnp.logical_not((z == 7) & (g == 7)))
    two_levels(grid, get, lo_ok, hi_ok, three_ref, four_ref)
    for f in range(3):
        edge0_ref[f] = three_ref[1, f]
        edge1_ref[f] = three_ref[2, f]


def order8_kernel(own_ref, a0_ref, a1_ref, a2_ref, a3_ref, mid_ref, up_ref, down_ref, all_ref):
    g, z, x = place()
    all_ref[0] = own_ref[...]
    for e, ref in enumerate((a0_ref, a1_ref, a2_ref, a3_ref)):
        for slot in range(2):
            all_ref[1 + 2 * e + slot] = ref[slot]
    for p in range(8):
        far = z ^ p
        holder = jnp.where(far > 4, far - 5, far - 1)
        slot = jnp.where(far > 4, 1, 0)
        source = jnp.where(far == 0, 0, 1 + 2 * (x ^ (holder & 3)) + slot)
        triple = all_ref[source]
        mid_ref[p] = triple
        if p > 0:
            up_ref[p - 1] = triple
        if p < 7:
            down_ref[p] = triple


def group_kernel(
    mid_ref, lo_ref, hi_ref,
    four_ref, five_ref, six_ref, seven_ref, edge0_ref, edge1_ref, all_ref, next_ref,
):
    g, z, x = place()
    grid = Grid()
    for p in range(7):
        all_ref[p] = lo_ref[p]
        all_ref[15 + p] = hi_ref[p]
    for p in range(8):
        all_ref[7 + p] = mid_ref[p]
    lo_ok = flag(g > 0)
    hi_ok = flag(g < 7)

    def step(q, carry):
        triple = halve(grid, lambda p: [all_ref[p, f] for f in range(3)], 1 + 2 * q)
        ok = jnp.where(q < 3, lo_ok, jnp.where(q > 6, hi_ok, 1.0))
        next_ref[q, 0] = triple[0] * ok
        next_ref[q, 1] = triple[1] * ok
        next_ref[q, 2] = triple[2]
        return carry

    lax.fori_loop(0, 10, step, 0)
    for d in range(5):
        four_ref[d] = all_ref[z + 5 + d]
        five_ref[d] = next_ref[z // 2 + 1 + d]

    def get(p):
        return [next_ref[p, f] for f in range(3)]

    two_levels(grid, get, lo_ok, hi_ok, six_ref, seven_ref)
    for f in range(3):
        edge0_ref[f] = six_ref[1, f]
        edge1_ref[f] = six_ref[2, f]


def up_kernel(
    s_ref, c_ref, tex_ref, lab_ref, lo_ref, hi_ref, kappa_ref,
    one_ref, one_lo_ref, one_hi_ref, two_ref,
    three_ref, three_lo_ref, three_hi_ref, four_ref, five_ref,
    six_ref, six_lo_ref, six_hi_ref, near_ref, other_ref,
    grad_ref, sums_ref,
    coarse_ref, power_ref, window_ref, fix_ref, sum_ref,
):
    g, z, x = place()
    grid = Grid()
    zero = jnp.zeros(PLANE, F32)
    y = g // 2
    core = g % 2
    for n in range(8):
        yy, cc = n // 2, n % 2
        mine = near_ref[y ^ yy]
        theirs = other_ref[y ^ yy]
        triple = jnp.where(core == cc, mine, theirs)
        for f in range(3):
            coarse_ref[f, n + 1] = triple[f]
    for f in range(3):
        coarse_ref[f, 0] = zero
        coarse_ref[f, 9] = zero
    for m in range(3):
        for f in range(2):
            power_ref[m, f, 0] = zero
            power_ref[m, f, 9] = zero
    for m in range(3):
        reach = 3 - m

        def source(f, n):
            return coarse_ref[f, n] if m == 0 else power_ref[m - 1, f, n]

        def sweep(n, carry):
            fields = [(source(f, n - 1), source(f, n), source(f, n + 1)) for f in (0, 1)]
            outs = smooth_planes(
                grid, coarse_ref[2, n - 1], coarse_ref[2, n], coarse_ref[2, n + 1], fields
            )
            for f in (0, 1):
                power_ref[m, f, n] = outs[f]
            return carry

        low = jnp.maximum(g + 1 - reach, 1)
        high = jnp.minimum(g + 1 + reach, 8)
        lax.fori_loop(low, high + 1, sweep, 0)

    def around(read):
        return [read(g + d) for d in range(3)]

    p0 = around(lambda n: coarse_ref[0, n])
    p1 = around(lambda n: power_ref[0, 0, n])
    p2 = around(lambda n: power_ref[1, 0, n])
    q0 = around(lambda n: coarse_ref[1, n])
    q1 = around(lambda n: power_ref[0, 1, n])
    q2 = around(lambda n: power_ref[1, 1, n])
    p01 = [a + b for a, b in zip(p0, p1)]
    p012 = [a + b for a, b in zip(p01, p2)]
    total = face_products(grid, q0, p012) + face_products(grid, q1, p01)
    total = 0.2 * (total + face_products(grid, q2, p0))
    sum_ref[0] = total
    for d in range(3):
        inside = (g + d >= 1) & (g + d <= 8)
        for f in range(2):
            value = coarse_ref[f, g + d]
            for m in range(3):
                value = value + power_ref[m, f, g + d]
            fix_ref[f, d] = jnp.where(inside, 0.2 * value, 0.0)

    def level(triples, parity, lo_ok, hi_ok):
        pick = [0, parity, 1, 1 + parity, 2]
        prolonged = [[fix_ref[f, pick[d]] for d in range(5)] for f in range(2)]
        given = [[triples(d, f) for d in range(5)] for f in range(3)]
        fixed = [[0.2 * given[f][d] + prolonged[f][d] for d in range(5)] for f in range(2)]
        scale = [lo_ok, None, hi_ok]
        for d in range(3):
            fields = [(fixed[f][d], fixed[f][d + 1], fixed[f][d + 2]) for f in range(2)]
            outs = smooth_planes(grid, given[2][d], given[2][d + 1], given[2][d + 2], fields)
            for f in range(2):
                value = outs[f] + 0.2 * given[f][d + 1]
                if scale[d] is not None:
                    value = value * scale[d]
                fix_ref[f, d] = value
        part = face_products(grid, given[1][1:4], fixed[0][1:4])
        part = part + face_products(grid, prolonged[1][1:4], given[0][1:4])
        sum_ref[0] = sum_ref[0] + part

    def window(base, lo_edge, mid, hi_edge):
        window_ref[0] = lo_edge[...]
        for p in range(4):
            window_ref[1 + p] = mid[p]
        window_ref[5] = hi_edge[...]
        return lambda d, f: window_ref[base + d, f]

    half6 = z // 4
    half3 = x // 2
    level(window(half6, six_lo_ref, six_ref, six_hi_ref), half6,
          flag((g > 0) | (z > 3)), flag((g < 7) | (z < 4)))
    level(lambda d, f: five_ref[d, f], (z // 2) % 2,
          flag((g > 0) | (z > 1)), flag((g < 7) | (z < 6)))
    level(lambda d, f: four_ref[d, f], z % 2,
          flag((g > 0) | (z > 0)), flag((g < 7) | (z < 7)))
    level(window(half3, three_lo_ref, three_ref, three_hi_ref), half3,
          flag((g > 0) | (z > 0) | (x > 1)), flag((g < 7) | (z < 7) | (x < 2)))
    lo_ok = flag((g > 0) | (z > 0) | (x > 0))
    hi_ok = flag((g < 7) | (z < 7) | (x < 3))
    level(lambda d, f: two_ref[d, f], x % 2, lo_ok, hi_ok)

    def given1(f, p):
        if p == -2:
            return one_lo_ref[f]
        if p == 3:
            return one_hi_ref[f]
        return one_ref[p + 1, f]

    def prolonged1(f, p):
        return fix_ref[f, p // 2 + 1]

    def fixed1(f, p):
        return 0.2 * given1(f, p) + prolonged1(f, p)

    for p in range(-1, 3):
        fields = [(fixed1(f, p - 1), fixed1(f, p), fixed1(f, p + 1)) for f in range(2)]
        outs = smooth_planes(grid, given1(2, p - 1), given1(2, p), given1(2, p + 1), fields)
        scale = lo_ok if p == -1 else hi_ok if p == 2 else None
        for f in range(2):
            value = outs[f] + 0.2 * given1(f, p)
            window_ref[p + 1, f] = value if scale is None else value * scale
    for p in range(2):
        part = face_products(
            grid, [given1(1, p + d) for d in (-1, 0, 1)], [fixed1(0, p + d) for d in (-1, 0, 1)]
        )
        part = part + face_products(
            grid, [prolonged1(1, p + d) for d in (-1, 0, 1)], [given1(0, p + d) for d in (-1, 0, 1)]
        )
        sum_ref[1 + p] = part

    def given0(f, p):
        if p < 0:
            return lo_ref[2 + 3 * f]
        if p > 3:
            return hi_ref[3 * f]
        return (s_ref, c_ref)[f][p]

    def prolonged0(f, p):
        return window_ref[p // 2 + 1, f]

    def fixed0(f, p):
        return 0.2 * given0(f, p) + prolonged0(f, p)

    lane = lax.broadcasted_iota(jnp.int32, (NY, TILE), 1)
    sums = jnp.zeros((NY, TILE), F32)
    for p in range(4):
        outs = smooth_planes(
            grid, kappa_ref[p], kappa_ref[p + 1], kappa_ref[p + 2],
            [(fixed0(1, p - 1), fixed0(1, p), fixed0(1, p + 1))],
        )
        grad_ref[p] = outs[0] + 0.2 * given0(1, p)
        part = face_products(
            grid, [given0(1, p + d) for d in (-1, 0, 1)], [fixed0(0, p + d) for d in (-1, 0, 1)]
        )
        part = part + face_products(
            grid, [prolonged0(1, p + d) for d in (-1, 0, 1)], [given0(0, p + d) for d in (-1, 0, 1)]
        )
        weighted = (part + sum_ref[1 + p // 2] + sum_ref[0]) * tex_ref[p]
        for t in range(2):
            tile = jnp.sum(weighted[:, t * TILE : (t + 1) * TILE], axis=1, keepdims=True)
            sums = sums + jnp.where(lab_ref[p, :, t : t + 1] == lane, tile, 0.0)
    sums_ref[...] = -0.1 * jnp.sum(sums, axis=0, keepdims=True)


def on_device(right_side, cotangent, texture, labels, coef_table):
    with jax.named_scope("fine_halo"):
        row_lo = shift(coef_table, "grp", 1)
        row_hi = shift(coef_table, "grp", -1)
        up, down = call(
            pack_kernel, [(10,) + PLANE] * 2, [], right_side, cotangent, texture, labels
        )
        lo = shift(up, GD, 1)
        hi = shift(down, GD, -1)
    with jax.named_scope("coef_rows"):
        rows = jnp.concatenate([row_lo, coef_table, row_hi], axis=0)
        sent = jnp.broadcast_to(rows[None], (32, 3, 2))
        got = lax.all_to_all(sent, "dev", 0, 0)
        coef = jnp.pad(jnp.transpose(got, (1, 0, 2)).reshape(3, 64), ((0, 0), (0, 64)))
    with jax.named_scope("fine"):
        kappa, one, two, edge0, edge1 = call(
            fine_kernel,
            [(6,) + PLANE, (4,) + TRIPLE, TRIPLE, TRIPLE, TRIPLE],
            [(10,) + PLANE],
            right_side, cotangent, texture, labels, lo, hi, coef,
        )
    with jax.named_scope("block_gather"):
        mates = [swap(two, "dev", mask) for mask in (1, 2, 3)]
        one_lo = shift(edge0, GD, 1)
        one_hi = shift(edge1, GD, -1)
        mid, up, down = call(
            order4_kernel,
            [(4,) + TRIPLE, (3,) + TRIPLE, (3,) + TRIPLE],
            [(4,) + TRIPLE],
            two, *mates,
        )
        blo = shift(up, GD, 4)
        bhi = shift(down, GD, -4)
    with jax.named_scope("block"):
        two_own, three, four, edge0, edge1 = call(
            block_kernel,
            [(5,) + TRIPLE, (4,) + TRIPLE, TRIPLE, TRIPLE, TRIPLE],
            [(10,) + TRIPLE],
            mid, blo, bhi,
        )
    with jax.named_scope("group_gather"):
        near = lax.ppermute(four, "dev", [(i, i ^ (4 * (i % 4 + 1))) for i in range(32)])
        far = lax.ppermute(
            four, "dev", [(i, i ^ (4 * (i % 4 + 5))) for i in range(32) if i % 4 < 3]
        )
        three_lo = shift(edge0, GD, 4)
        three_hi = shift(edge1, GD, -4)
        pair = jnp.stack([near, far])
        pairs = [pair] + [swap(pair, "dev", mask) for mask in (1, 2, 3)]
        mid, up, down = call(
            order8_kernel,
            [(8,) + TRIPLE, (7,) + TRIPLE, (7,) + TRIPLE],
            [(9,) + TRIPLE],
            four, *pairs,
        )
        glo = shift(up, "grp", 1)
        ghi = shift(down, "grp", -1)
    with jax.named_scope("group"):
        four_own, five_own, six, seven, edge0, edge1 = call(
            group_kernel,
            [(5,) + TRIPLE, (5,) + TRIPLE, (4,) + TRIPLE, TRIPLE, TRIPLE, TRIPLE],
            [(22,) + TRIPLE, (10,) + TRIPLE],
            mid, glo, ghi,
        )
    with jax.named_scope("coarse_gather"):
        column = jnp.stack([seven] + [swap(seven, "grp", 2 * mask) for mask in (1, 2, 3)])
        six_lo = shift(edge0, "grp", 1)
        six_hi = shift(edge1, "grp", -1)
        other = swap(column, "grp", 1)
    with jax.named_scope("up"):
        source_grad, sums = call(
            up_kernel,
            [(4,) + PLANE, (1, TILE)],
            [(3, 10) + PLANE, (3, 2, 10) + PLANE, (6,) + TRIPLE, (2, 3) + PLANE, (3,) + PLANE],
            right_side, cotangent, texture, labels, lo, hi, kappa,
            one, one_lo, one_hi, two_own, three, three_lo, three_hi,
            four_own, five_own, six, six_lo, six_hi, column, other,
        )
    with jax.named_scope("table"):
        parts = lax.all_to_all(sums[0, :64].reshape(32, 2), "dev", 0, 0)
        table_grad = jnp.sum(parts, axis=0)[None]
    return (source_grad, table_grad)


def solution(mesh):
    spec = P(GD, None, None)
    table_spec = P("grp", "dev")
    return jax.shard_map(
        on_device,
        mesh=mesh,
        in_specs=(spec, spec, spec, spec, table_spec),
        out_specs=(spec, table_spec),
        check_vma=False,
    )
```

time: 605 us -> 189 us (0.31); the launches traced: 593 us -> 188 us
  starting transfers between devices: 283 us -> 71.5 us
  blocking collectives: 135 us -> 26.5 us
  waiting for transfers between devices: 131 us -> 45.5 us
  Pallas kernels: 0 us -> 33.6 us
  local copies, waits for them, and re-layouts: 24.1 us -> 8.37 us
  other arithmetic: 14.6 us -> 1.56 us
    ppermute x78 -> x26, starting transfers between devices: 283 us -> 71.5 us  [the longest x14 54.8 us: shift(): return lax.ppermute(block, axes, route)]
    unnamed x2 -> x0, blocking collectives: 135 us -> none
    ppermute x78 -> x26, waiting for transfers between devices: 131 us -> 45.5 us  [the longest x14 23 us: shift(): return lax.ppermute(block, axes, route)]
    pallas_call x0 -> x7, Pallas kernels: none -> 33.6 us  [call(): pl.pallas_call(kernel, out_shape=[jax.ShapeDtypeStruct(shape, F32) for sh...]
    all_to_all x0 -> x2, blocking collectives: none -> 26.5 us  [the longest x1 15 us: on_device(): got = lax.all_to_all(sent, 'dev', 0, 0)]
    unnamed x370 -> x59, local copies, waits for them, and re-layouts: 23.3 us -> 7.49 us
  transfers between devices with their start and end apart: 78 -> 26, of which waited for: 39 -> 13; matrix products, arithmetic and copies ran while one was open for 1% -> 0% of each run, Pallas kernels for 0% -> 0%
where the time goes in v1:
time: 189 us; the launch traced here: 188 us
  starting transfers between devices  71.5 us (38%)
  waiting for transfers between devices  45.5 us (24%)
  Pallas kernels  33.6 us (18%)
  blocking collectives  26.5 us (14%)
  local copies, waits for them, and re-layouts  8.37 us (4%)
    ppermute x14, starting transfers between devices, shift(): return lax.ppermute(block, axes, route)  54.8 us
    pallas_call x7, Pallas kernels, call(): pl.pallas_call(kernel, out_shape=[jax.ShapeDtypeStruct(shape, F32) for sh...  33.6 us
    ppermute x14, waiting for transfers between devices, shift(): return lax.ppermute(block, axes, route)  23 us
    ppermute x10, waiting for transfers between devices, swap(): lax.ppermute(block, axis, [(i, i ^ mask) for i in range(lax.axis_size(axi...  17.2 us
    all_to_all x1, blocking collectives, on_device(): got = lax.all_to_all(sent, 'dev', 0, 0)  15 us
    ppermute x10, starting transfers between devices, swap(): lax.ppermute(block, axis, [(i, i ^ mask) for i in range(lax.axis_size(axi...  13.3 us
    all_to_all x1, blocking collectives, on_device(): parts = lax.all_to_all(sums[0, :64].reshape(32, 2), 'dev', 0, 0)  11.6 us
    unnamed x59, local copies, waits for them, and re-layouts  7.49 us
  transfers between devices with their start and end apart: 26, of which 13 were waited for; matrix products, arithmetic and copies ran while one was open for 0% of the time, Pallas kernels for 0%

profile of v1, /device:TPU:1, one launch (start us, length us, event | category | flops | bytes accessed | tf_op | source)
XLA Modules:
  0.0 188.1 jit_solution(15445042548927208226)
XLA Ops:
  4.0 4.1 %collective-permute-start = (f32[10,32,256]{2,1,0:T(8,128)}, f32[10,32,256]{2,1,0:T(8,128)S(1)}, u32[]{:S(2)}, u32[]{:S(2)}) collective-permute-start(f32[10,32,256]{2,1,0:T(8,128)} %get-tuple-element.28), channel_id=1, source_target_pairs={{0,1},{1,2},{2,3},{3,4},{4,5},{5,6},{6,7},{7,8},{8,9},{9,10},{10,1... | collective-permute-start | bytes 983048 | tf_op jit(solution)/shard_map/fine_halo/ppermute | solution.py:110
  8.1 9.0 %collective-permute-start.1 = (f32[10,32,256]{2,1,0:T(8,128)}, f32[10,32,256]{2,1,0:T(8,128)S(1)}, u32[]{:S(2)}, u32[]{:S(2)}) collective-permute-start(f32[10,32,256]{2,1,0:T(8,128)} %get-tuple-element.29), channel_id=1, source_target_pairs={{1,0},{2,1},{3,2},{4,3},{5,4},{6,5},{7,6},{8,7},{9,8},{10,9},{11,1... | collective-permute-start | bytes 983048 | tf_op jit(solution)/shard_map/fine_halo/ppermute | solution.py:110
  25.0 15.0 %all_to_all.14 = f32[32,3,2]{1,2,0:T(2,128)S(1)} all-to-all(f32[32,3,2]{1,2,0:T(2,128)S(1)} %broadcast_in_dim.4), channel_id=1, replica_groups=mesh['grp'=8,'dev'=32] {'dev'}, dimensions={0} | all-to-all | bytes 1536 | tf_op jit(solution)/shard_map/coef_rows/all_to_all | solution.py:464
  42.1 5.2 %fine.1 = (f32[6,32,256]{2,1,0:T(8,128)}, f32[4,3,32,256]{3,2,1,0:T(8,128)}, f32[3,32,256]{2,1,0:T(8,128)}, f32[3,32,256]{2,1,0:T(8,128)}, f32[3,32,256]{2,1,0:T(8,128)}) custom-call(f32[4,32,256]{2,1,0:T(8,128)} %s_ref.5, f32[4,32,256]{2,1,0:T(8,128)} %c_ref.5, f32[4,32,256]{2,1,0:T(8,128)} %tex_ref.5, s32[4,32,2]{2,1,0:T(8,128)} %copy.17.lab_ref, ...), custom_call_target="tpu_custom_call" | custom-call | tf_op jit(solution)/shard_map/fine/pallas_call | solution.py:119
  50.5 5.0 %collective-permute-done.8.a3_ref = f32[3,32,256]{2,1,0:T(8,128)S(1)} collective-permute-done((f32[3,32,256]{2,1,0:T(8,128)}, f32[3,32,256]{2,1,0:T(8,128)S(1)}, u32[]{:S(2)}, u32[]{:S(2)}) %collective-permute-start.8) | collective-permute-done | bytes 98336 | tf_op jit(solution)/shard_map/block_gather/ppermute | solution.py:114
  61.4 4.3 %collective-permute-start.10 = (f32[3,3,32,256]{3,2,1,0:T(8,128)}, f32[3,3,32,256]{3,2,1,0:T(8,128)S(1)}, u32[]{:S(2)}, u32[]{:S(2)}) collective-permute-start(f32[3,3,32,256]{3,2,1,0:T(8,128)} %get-tuple-element.37), channel_id=1, source_target_pairs={{4,0},{5,1},{6,2},{7,3},{8,4},{9,5},{10,6},{11,7},{12,8},{13,9},{1... | collective-permute-start | bytes 884744 | tf_op jit(solution)/shard_map/block_gather/ppermute | solution.py:110
  65.7 4.7 %collective-permute-done.9.lo_ref = f32[3,3,32,256]{3,2,1,0:T(8,128)S(1)} collective-permute-done((f32[3,3,32,256]{3,2,1,0:T(8,128)}, f32[3,3,32,256]{3,2,1,0:T(8,128)S(1)}, u32[]{:S(2)}, u32[]{:S(2)}) %collective-permute-start.9) | collective-permute-done | bytes 294944 | tf_op jit(solution)/shard_map/block_gather/ppermute | solution.py:110
  72.0 3.4 %block.1 = (f32[5,3,32,256]{3,2,1,0:T(8,128)}, f32[4,3,32,256]{3,2,1,0:T(8,128)}, f32[3,32,256]{2,1,0:T(8,128)}, f32[3,32,256]{2,1,0:T(8,128)}, f32[3,32,256]{2,1,0:T(8,128)}) custom-call(f32[4,3,32,256]{3,2,1,0:T(8,128)} %get-tuple-element.35.mid_ref, f32[3,3,32,256]{3,2,1,0:T(8,128)} %copy-done.7, f32[3,3,32,256]{3,2,1,0:T(8,128)} %copy-done.8), custom_call_target="tpu_custom_call" | custom-call | tf_op jit(solution)/shard_map/block/pallas_call | solution.py:119
  78.9 5.2 %collective-permute-done.14 = f32[3,32,256]{2,1,0:T(8,128)S(1)} collective-permute-done((f32[3,32,256]{2,1,0:T(8,128)}, f32[3,32,256]{2,1,0:T(8,128)S(1)}, u32[]{:S(2)}, u32[]{:S(2)}) %collective-permute-start.14) | collective-permute-done | bytes 98336 | tf_op jit(solution)/shard_map/group_gather/ppermute | solution.py:494
  84.3 6.2 %collective-permute-start.16 = (f32[2,3,32,256]{3,2,1,0:T(8,128)S(1)}, f32[2,3,32,256]{3,2,1,0:T(8,128)S(1)}, u32[]{:S(2)}, u32[]{:S(2)}) collective-permute-start(f32[2,3,32,256]{3,2,1,0:T(8,128)S(1)} %pad_maximum_fusion.1.a0_ref), channel_id=1, source_target_pairs={{0,2},{1,3},{2,0},{3,1},{4,6},{5,7},{6,4},{7,5},{8,10},{9,11},{10,... | collective-permute-start | bytes 589832 | tf_op jit(solution)/shard_map/group_gather/ppermute | solution.py:114
  90.5 4.3 %collective-permute-done.16.a2_ref = f32[2,3,32,256]{3,2,1,0:T(8,128)S(1)} collective-permute-done((f32[2,3,32,256]{3,2,1,0:T(8,128)S(1)}, f32[2,3,32,256]{3,2,1,0:T(8,128)S(1)}, u32[]{:S(2)}, u32[]{:S(2)}) %collective-permute-start.16) | collective-permute-done | bytes 196640 | tf_op jit(solution)/shard_map/group_gather/ppermute | solution.py:114
  94.8 3.2 %collective-permute-done.15.a1_ref = f32[2,3,32,256]{3,2,1,0:T(8,128)S(1)} collective-permute-done((f32[2,3,32,256]{3,2,1,0:T(8,128)S(1)}, f32[2,3,32,256]{3,2,1,0:T(8,128)S(1)}, u32[]{:S(2)}, u32[]{:S(2)}) %collective-permute-start.15) | collective-permute-done | bytes 196640 | tf_op jit(solution)/shard_map/group_gather/ppermute | solution.py:114
  101.5 5.0 %collective-permute-start.18 = (f32[7,3,32,256]{3,2,1,0:T(8,128)}, f32[7,3,32,256]{3,2,1,0:T(8,128)S(1)}, u32[]{:S(2)}, u32[]{:S(2)}) collective-permute-start(f32[7,3,32,256]{3,2,1,0:T(8,128)} %get-tuple-element.44), channel_id=1, source_target_pairs={{0,32},{32,64},{64,96},{96,128},{128,160},{160,192},{192,224},{1,3... | collective-permute-start | bytes 2064392 | tf_op jit(solution)/shard_map/group_gather/ppermute | solution.py:110
  108.4 6.2 %collective-permute-done.18.lo_ref = f32[7,3,32,256]{3,2,1,0:T(8,128)S(1)} collective-permute-done((f32[7,3,32,256]{3,2,1,0:T(8,128)}, f32[7,3,32,256]{3,2,1,0:T(8,128)S(1)}, u32[]{:S(2)}, u32[]{:S(2)}) %collective-permute-start.18) | collective-permute-done | bytes 688160 | tf_op jit(solution)/shard_map/group_gather/ppermute | solution.py:110
  114.7 4.3 %collective-permute-done.19.hi_ref = f32[7,3,32,256]{3,2,1,0:T(8,128)S(1)} collective-permute-done((f32[7,3,32,256]{3,2,1,0:T(8,128)}, f32[7,3,32,256]{3,2,1,0:T(8,128)S(1)}, u32[]{:S(2)}, u32[]{:S(2)}) %collective-permute-start.19) | collective-permute-done | bytes 688160 | tf_op jit(solution)/shard_map/group_gather/ppermute | solution.py:110
  119.8 6.6 %group.1 = (f32[5,3,32,256]{3,2,1,0:T(8,128)}, f32[5,3,32,256]{3,2,1,0:T(8,128)}, f32[4,3,32,256]{3,2,1,0:T(8,128)}, f32[3,32,256]{2,1,0:T(8,128)}, f32[3,32,256]{2,1,0:T(8,128)}, /*index=5*/f32[3,32,256]{2,1,0:T(8,128)}) custom-call(f32[8,3,32,256]{3,2,1,0:T(8,128)} %get-tuple-element.43.mid_ref, f32[7,3,32,256]{3,2,1,0:T(8,128)} %copy-done.4, ...), custom_call_target="tpu_custom_call" | custom-call | tf_op jit(solution)/shard_map/group/pallas_call | solution.py:119
  129.7 3.5 %collective-permute-done.24 = f32[3,32,256]{2,1,0:T(8,128)S(1)} collective-permute-done((f32[3,32,256]{2,1,0:T(8,128)}, f32[3,32,256]{2,1,0:T(8,128)S(1)}, u32[]{:S(2)}, u32[]{:S(2)}) %collective-permute-start.24) | collective-permute-done | bytes 98336 | tf_op jit(solution)/shard_map/coarse_gather/ppermute | solution.py:114
  135.6 4.1 %collective-permute-start.4 = (f32[3,32,256]{2,1,0:T(8,128)S(1)}, f32[3,32,256]{2,1,0:T(8,128)S(1)}, u32[]{:S(2)}, u32[]{:S(2)}) collective-permute-start(f32[3,32,256]{2,1,0:T(8,128)S(1)} %copy-done.23), channel_id=1, source_target_pairs={{0,1},{1,2},{2,3},{3,4},{4,5},{5,6},{6,7},{7,8},{8,9},{9,10},{10,1... | collective-permute-start | bytes 294920 | tf_op jit(solution)/shard_map/block_gather/ppermute | solution.py:110
  139.7 5.0 %collective-permute-start.5 = (f32[3,32,256]{2,1,0:T(8,128)S(1)}, f32[3,32,256]{2,1,0:T(8,128)S(1)}, u32[]{:S(2)}, u32[]{:S(2)}) collective-permute-start(f32[3,32,256]{2,1,0:T(8,128)S(1)} %copy-done.22), channel_id=1, source_target_pairs={{1,0},{2,1},{3,2},{4,3},{5,4},{6,5},{7,6},{8,7},{9,8},{10,9},{11,1... | collective-permute-start | bytes 294920 | tf_op jit(solution)/shard_map/block_gather/ppermute | solution.py:110
  146.6 4.9 %collective-permute-start.12 = (f32[3,32,256]{2,1,0:T(8,128)S(1)}, f32[3,32,256]{2,1,0:T(8,128)S(1)}, u32[]{:S(2)}, u32[]{:S(2)}) collective-permute-start(f32[3,32,256]{2,1,0:T(8,128)S(1)} %copy-done.24), channel_id=1, source_target_pairs={{4,0},{5,1},{6,2},{7,3},{8,4},{9,5},{10,6},{11,7},{12,8},{13,9},{1... | collective-permute-start | bytes 294920 | tf_op jit(solution)/shard_map/group_gather/ppermute | solution.py:110
  151.5 5.5 %collective-permute-start.20 = (f32[3,32,256]{2,1,0:T(8,128)S(1)}, f32[3,32,256]{2,1,0:T(8,128)S(1)}, u32[]{:S(2)}, u32[]{:S(2)}) collective-permute-start(f32[3,32,256]{2,1,0:T(8,128)S(1)} %copy-done.27), channel_id=1, source_target_pairs={{0,32},{32,64},{64,96},{96,128},{128,160},{160,192},{192,224},{1,3... | collective-permute-start | bytes 294920 | tf_op jit(solution)/shard_map/coarse_gather/ppermute | solution.py:110
  159.0 3.9 %collective-permute-done.21.six_hi_ref = f32[3,32,256]{2,1,0:T(8,128)S(1)} collective-permute-done((f32[3,32,256]{2,1,0:T(8,128)S(1)}, f32[3,32,256]{2,1,0:T(8,128)S(1)}, u32[]{:S(2)}, u32[]{:S(2)}) %collective-permute-start.21) | collective-permute-done | bytes 98336 | tf_op jit(solution)/shard_map/coarse_gather/ppermute | solution.py:110
  163.8 11.4 %up.1 = (f32[4,32,256]{2,1,0:T(8,128)}, f32[1,128]{1,0:T(1,128)}) custom-call(f32[4,32,256]{2,1,0:T(8,128)} %s_ref.5, f32[4,32,256]{2,1,0:T(8,128)} %c_ref.5, f32[4,32,256]{2,1,0:T(8,128)} %tex_ref.5, s32[4,32,2]{2,1,0:T(8,128)} %copy.17.lab_ref, f32[10,32,256]{2,1,0:T(8,128)} %copy-done.1, f32[10,32,256]{2,1,0:T(8,128)} %copy-done.2, ...), custom_call_target="tpu_custom_call" | custom-call | tf_op jit(solution)/shard_map/up/pallas_call | solution.py:119
  176.0 11.6 %all_to_all.15 = f32[32,1,2]{2,1,0:T(1,128)S(1)} all-to-all(f32[32,1,2]{2,1,0:T(1,128)S(1)} %bitcast.18), channel_id=1, replica_groups=mesh['grp'=8,'dev'=32] {'dev'}, dimensions={0} | all-to-all | bytes 512 | tf_op jit(solution)/shard_map/table/all_to_all | solution.py:531
  (106 shorter events, 45.5 us)
Async XLA Ops:
  4.0 36.6 %collective-permute-start = (f32[10,32,256]{2,1,0:T(8,128)}, f32[10,32,256]{2,1,0:T(8,128)S(1)}, u32[]{:S(2)}, u32[]{:S(2)}) collective-permute-start(f32[10,32,256]{2,1,0:T(8,128)} %get-tuple-element.28), channel_id=1, source_target_pairs={{0,1},{1,2},{2,3},{3,4},{4,5},{5,6},{6,7},{7,8},{8,9},{9,10},{10,1... | collective-permute-start | bytes 983048 | tf_op jit(solution)/shard_map/fine_halo/ppermute | solution.py:110
  8.1 32.5 %collective-permute-start.1 = (f32[10,32,256]{2,1,0:T(8,128)}, f32[10,32,256]{2,1,0:T(8,128)S(1)}, u32[]{:S(2)}, u32[]{:S(2)}) collective-permute-start(f32[10,32,256]{2,1,0:T(8,128)} %get-tuple-element.29), channel_id=1, source_target_pairs={{1,0},{2,1},{3,2},{4,3},{5,4},{6,5},{7,6},{8,7},{9,8},{10,9},{11,1... | collective-permute-start | bytes 983048 | tf_op jit(solution)/shard_map/fine_halo/ppermute | solution.py:110
  20.0 4.9 %collective-permute-start.3 = (f32[1,2]{1,0:T(1,128)S(1)}, f32[1,2]{1,0:T(1,128)S(1)}, u32[]{:S(2)}, u32[]{:S(2)}) collective-permute-start(f32[1,2]{1,0:T(1,128)S(1)} %copy-done.21), channel_id=1, source_target_pairs={{32,0},{64,32},{96,64},{128,96},{160,128},{192,160},{224,192},{33,... | collective-permute-start | bytes 32 | tf_op jit(solution)/shard_map/fine_halo/ppermute | solution.py:110
  47.3 8.2 %collective-permute-start.8 = (f32[3,32,256]{2,1,0:T(8,128)}, f32[3,32,256]{2,1,0:T(8,128)S(1)}, u32[]{:S(2)}, u32[]{:S(2)}) collective-permute-start(f32[3,32,256]{2,1,0:T(8,128)} %get-tuple-element.34.a0_ref), channel_id=1, source_target_pairs={{0,3},{1,2},{2,1},{3,0},{4,7},{5,6},{6,5},{7,4},{8,11},{9,10},{10,... | collective-permute-start | bytes 294920 | tf_op jit(solution)/shard_map/block_gather/ppermute | solution.py:114
  48.3 7.2 %collective-permute-start.7 = (f32[3,32,256]{2,1,0:T(8,128)}, f32[3,32,256]{2,1,0:T(8,128)S(1)}, u32[]{:S(2)}, u32[]{:S(2)}) collective-permute-start(f32[3,32,256]{2,1,0:T(8,128)} %get-tuple-element.34.a0_ref), channel_id=1, source_target_pairs={{0,2},{1,3},{2,0},{3,1},{4,6},{5,7},{6,4},{7,5},{8,10},{9,11},{10,... | collective-permute-start | bytes 294920 | tf_op jit(solution)/shard_map/block_gather/ppermute | solution.py:114
  49.4 6.5 %collective-permute-start.6 = (f32[3,32,256]{2,1,0:T(8,128)}, f32[3,32,256]{2,1,0:T(8,128)S(1)}, u32[]{:S(2)}, u32[]{:S(2)}) collective-permute-start(f32[3,32,256]{2,1,0:T(8,128)} %get-tuple-element.34.a0_ref), channel_id=1, source_target_pairs={{0,1},{1,0},{2,3},{3,2},{4,5},{5,4},{6,7},{7,6},{8,9},{9,8},{10,11... | collective-permute-start | bytes 294920 | tf_op jit(solution)/shard_map/block_gather/ppermute | solution.py:114
  58.9 11.5 %collective-permute-start.9 = (f32[3,3,32,256]{3,2,1,0:T(8,128)}, f32[3,3,32,256]{3,2,1,0:T(8,128)S(1)}, u32[]{:S(2)}, u32[]{:S(2)}) collective-permute-start(f32[3,3,32,256]{3,2,1,0:T(8,128)} %get-tuple-element.36), channel_id=1, source_target_pairs={{0,4},{1,5},{2,6},{3,7},{4,8},{5,9},{6,10},{7,11},{8,12},{9,13},{1... | collective-permute-start | bytes 884744 | tf_op jit(solution)/shard_map/block_gather/ppermute | solution.py:110
  61.4 10.0 %collective-permute-start.10 = (f32[3,3,32,256]{3,2,1,0:T(8,128)}, f32[3,3,32,256]{3,2,1,0:T(8,128)S(1)}, u32[]{:S(2)}, u32[]{:S(2)}) collective-permute-start(f32[3,3,32,256]{3,2,1,0:T(8,128)} %get-tuple-element.37), channel_id=1, source_target_pairs={{4,0},{5,1},{6,2},{7,3},{8,4},{9,5},{10,6},{11,7},{12,8},{13,9},{1... | collective-permute-start | bytes 884744 | tf_op jit(solution)/shard_map/block_gather/ppermute | solution.py:110
  75.5 8.7 %collective-permute-start.14 = (f32[3,32,256]{2,1,0:T(8,128)}, f32[3,32,256]{2,1,0:T(8,128)S(1)}, u32[]{:S(2)}, u32[]{:S(2)}) collective-permute-start(f32[3,32,256]{2,1,0:T(8,128)} %get-tuple-element.42.own_ref), channel_id=1, source_target_pairs={{0,20},{1,25},{2,30},{4,16},{5,29},{6,26},{8,28},{9,17},{10,22},{1... | collective-permute-start | bytes 294920 | tf_op jit(solution)/shard_map/group_gather/ppermute | solution.py:494
  78.5 5.6 %collective-permute-start.13 = (f32[3,32,256]{2,1,0:T(8,128)}, f32[3,32,256]{2,1,0:T(8,128)S(1)}, u32[]{:S(2)}, u32[]{:S(2)}) collective-permute-start(f32[3,32,256]{2,1,0:T(8,128)} %get-tuple-element.42.own_ref), channel_id=1, source_target_pairs={{0,4},{1,9},{2,14},{3,19},{4,0},{5,13},{6,10},{7,23},{8,12},{9,1},... | collective-permute-start | bytes 294920 | tf_op jit(solution)/shard_map/group_gather/ppermute | solution.py:493
  84.2 6.3 %collective-permute-start.17 = (f32[2,3,32,256]{3,2,1,0:T(8,128)S(1)}, f32[2,3,32,256]{3,2,1,0:T(8,128)S(1)}, u32[]{:S(2)}, u32[]{:S(2)}) collective-permute-start(f32[2,3,32,256]{3,2,1,0:T(8,128)S(1)} %pad_maximum_fusion.1.a0_ref), channel_id=1, source_target_pairs={{0,3},{1,2},{2,1},{3,0},{4,7},{5,6},{6,5},{7,4},{8,11},{9,10},{10,... | collective-permute-start | bytes 589832 | tf_op jit(solution)/shard_map/group_gather/ppermute | solution.py:114
  84.3 10.5 %collective-permute-start.16 = (f32[2,3,32,256]{3,2,1,0:T(8,128)S(1)}, f32[2,3,32,256]{3,2,1,0:T(8,128)S(1)}, u32[]{:S(2)}, u32[]{:S(2)}) collective-permute-start(f32[2,3,32,256]{3,2,1,0:T(8,128)S(1)} %pad_maximum_fusion.1.a0_ref), channel_id=1, source_target_pairs={{0,2},{1,3},{2,0},{3,1},{4,6},{5,7},{6,4},{7,5},{8,10},{9,11},{10,... | collective-permute-start | bytes 589832 | tf_op jit(solution)/shard_map/group_gather/ppermute | solution.py:114
  90.5 7.5 %collective-permute-start.15 = (f32[2,3,32,256]{3,2,1,0:T(8,128)S(1)}, f32[2,3,32,256]{3,2,1,0:T(8,128)S(1)}, u32[]{:S(2)}, u32[]{:S(2)}) collective-permute-start(f32[2,3,32,256]{3,2,1,0:T(8,128)S(1)} %pad_maximum_fusion.1.a0_ref), channel_id=1, source_target_pairs={{0,1},{1,0},{2,3},{3,2},{4,5},{5,4},{6,7},{7,6},{8,9},{9,8},{10,11... | collective-permute-start | bytes 589832 | tf_op jit(solution)/shard_map/group_gather/ppermute | solution.py:114
  101.5 13.2 %collective-permute-start.18 = (f32[7,3,32,256]{3,2,1,0:T(8,128)}, f32[7,3,32,256]{3,2,1,0:T(8,128)S(1)}, u32[]{:S(2)}, u32[]{:S(2)}) collective-permute-start(f32[7,3,32,256]{3,2,1,0:T(8,128)} %get-tuple-element.44), channel_id=1, source_target_pairs={{0,32},{32,64},{64,96},{96,128},{128,160},{160,192},{192,224},{1,3... | collective-permute-start | bytes 2064392 | tf_op jit(solution)/shard_map/group_gather/ppermute | solution.py:110
  106.5 12.5 %collective-permute-start.19 = (f32[7,3,32,256]{3,2,1,0:T(8,128)}, f32[7,3,32,256]{3,2,1,0:T(8,128)S(1)}, u32[]{:S(2)}, u32[]{:S(2)}) collective-permute-start(f32[7,3,32,256]{3,2,1,0:T(8,128)} %get-tuple-element.45), channel_id=1, source_target_pairs={{32,0},{64,32},{96,64},{128,96},{160,128},{192,160},{224,192},{33,... | collective-permute-start | bytes 2064392 | tf_op jit(solution)/shard_map/group_gather/ppermute | solution.py:110
  126.5 6.7 %collective-permute-start.24 = (f32[3,32,256]{2,1,0:T(8,128)}, f32[3,32,256]{2,1,0:T(8,128)S(1)}, u32[]{:S(2)}, u32[]{:S(2)}) collective-permute-start(f32[3,32,256]{2,1,0:T(8,128)} %get-tuple-element.51), channel_id=1, source_target_pairs={{0,192},{32,224},{64,128},{96,160},{128,64},{160,96},{192,0},{224,... | collective-permute-start | bytes 294920 | tf_op jit(solution)/shard_map/coarse_gather/ppermute | solution.py:114
  126.5 6.7 %collective-permute-start.23 = (f32[3,32,256]{2,1,0:T(8,128)}, f32[3,32,256]{2,1,0:T(8,128)S(1)}, u32[]{:S(2)}, u32[]{:S(2)}) collective-permute-start(f32[3,32,256]{2,1,0:T(8,128)} %get-tuple-element.51), channel_id=1, source_target_pairs={{0,128},{32,160},{64,192},{96,224},{128,0},{160,32},{192,64},{224,... | collective-permute-start | bytes 294920 | tf_op jit(solution)/shard_map/coarse_gather/ppermute | solution.py:114
  135.1 27.9 %collective-permute-start.25 = (f32[4,3,32,256]{3,2,1,0:T(8,128)S(1)}, f32[4,3,32,256]{3,2,1,0:T(8,128)S(1)}, u32[]{:S(2)}, u32[]{:S(2)}) collective-permute-start(f32[4,3,32,256]{3,2,1,0:T(8,128)S(1)} %pad_maximum_fusion.near_ref), channel_id=1, source_target_pairs={{0,32},{32,0},{64,96},{96,64},{128,160},{160,128},{192,224},{224,1... | collective-permute-start | bytes 1179656 | tf_op jit(solution)/shard_map/coarse_gather/ppermute | solution.py:114
  135.6 15.9 %collective-permute-start.4 = (f32[3,32,256]{2,1,0:T(8,128)S(1)}, f32[3,32,256]{2,1,0:T(8,128)S(1)}, u32[]{:S(2)}, u32[]{:S(2)}) collective-permute-start(f32[3,32,256]{2,1,0:T(8,128)S(1)} %copy-done.23), channel_id=1, source_target_pairs={{0,1},{1,2},{2,3},{3,4},{4,5},{5,6},{6,7},{7,8},{8,9},{9,10},{10,1... | collective-permute-start | bytes 294920 | tf_op jit(solution)/shard_map/block_gather/ppermute | solution.py:110
  139.7 17.3 %collective-permute-start.5 = (f32[3,32,256]{2,1,0:T(8,128)S(1)}, f32[3,32,256]{2,1,0:T(8,128)S(1)}, u32[]{:S(2)}, u32[]{:S(2)}) collective-permute-start(f32[3,32,256]{2,1,0:T(8,128)S(1)} %copy-done.22), channel_id=1, source_target_pairs={{1,0},{2,1},{3,2},{4,3},{5,4},{6,5},{7,6},{8,7},{9,8},{10,9},{11,1... | collective-permute-start | bytes 294920 | tf_op jit(solution)/shard_map/block_gather/ppermute | solution.py:110
  144.7 14.3 %collective-permute-start.11 = (f32[3,32,256]{2,1,0:T(8,128)S(1)}, f32[3,32,256]{2,1,0:T(8,128)S(1)}, u32[]{:S(2)}, u32[]{:S(2)}) collective-permute-start(f32[3,32,256]{2,1,0:T(8,128)S(1)} %copy-done.25), channel_id=1, source_target_pairs={{0,4},{1,5},{2,6},{3,7},{4,8},{5,9},{6,10},{7,11},{8,12},{9,13},{1... | collective-permute-start | bytes 294920 | tf_op jit(solution)/shard_map/group_gather/ppermute | solution.py:110
  146.6 12.4 %collective-permute-start.12 = (f32[3,32,256]{2,1,0:T(8,128)S(1)}, f32[3,32,256]{2,1,0:T(8,128)S(1)}, u32[]{:S(2)}, u32[]{:S(2)}) collective-permute-start(f32[3,32,256]{2,1,0:T(8,128)S(1)} %copy-done.24), channel_id=1, source_target_pairs={{4,0},{5,1},{6,2},{7,3},{8,4},{9,5},{10,6},{11,7},{12,8},{13,9},{1... | collective-permute-start | bytes 294920 | tf_op jit(solution)/shard_map/group_gather/ppermute | solution.py:110
  151.5 7.5 %collective-permute-start.20 = (f32[3,32,256]{2,1,0:T(8,128)S(1)}, f32[3,32,256]{2,1,0:T(8,128)S(1)}, u32[]{:S(2)}, u32[]{:S(2)}) collective-permute-start(f32[3,32,256]{2,1,0:T(8,128)S(1)} %copy-done.27), channel_id=1, source_target_pairs={{0,32},{32,64},{64,96},{96,128},{128,160},{160,192},{192,224},{1,3... | collective-permute-start | bytes 294920 | tf_op jit(solution)/shard_map/coarse_gather/ppermute | solution.py:110
  157.1 5.9 %collective-permute-start.21 = (f32[3,32,256]{2,1,0:T(8,128)S(1)}, f32[3,32,256]{2,1,0:T(8,128)S(1)}, u32[]{:S(2)}, u32[]{:S(2)}) collective-permute-start(f32[3,32,256]{2,1,0:T(8,128)S(1)} %copy-done.26), channel_id=1, source_target_pairs={{32,0},{64,32},{96,64},{128,96},{160,128},{192,160},{224,192},{33,... | collective-permute-start | bytes 294920 | tf_op jit(solution)/shard_map/coarse_gather/ppermute | solution.py:110
  (31 other events, 187.8 us)

commit v2 on v1

--- a/solution.py
+++ b/solution.py
@@ -141,7 +141,7 @@
 
 def fine_kernel(
     s_ref, c_ref, tex_ref, lab_ref, lo_ref, hi_ref, coef_ref,
-    kappa_ref, one_ref, two_ref, edge0_ref, edge1_ref, k_ref,
+    kappa_ref, one_ref, two_ref, to1_ref, to3_ref, k_ref,
 ):
     g, z, x = place()
     grid = Grid()
@@ -182,15 +182,25 @@
     lo_ok = flag(jnp.logical_not(first & (g == 0)))
     hi_ok = flag(jnp.logical_not(last & (g == 7)))
     two_levels(grid, get, lo_ok, hi_ok, one_ref, two_ref)
-    for f in range(3):
-        edge0_ref[f] = one_ref[1, f]
-        edge1_ref[f] = one_ref[2, f]
-
-
-def order4_kernel(a0_ref, a1_ref, a2_ref, a3_ref, mid_ref, up_ref, down_ref, all_ref):
+    odd = x % 2
+    to1_ref[0] = two_ref[...]
+    to3_ref[0] = two_ref[...]
+    to1_ref[1] = one_ref[1 + odd]
+    to3_ref[1] = one_ref[2 - odd]
+
+
+def order4_kernel(
+    a0_ref, a1_ref, a2_ref, a3_ref, mid_ref, up_ref, down_ref, side_ref, all_ref
+):
     g, z, x = place()
-    for e, ref in enumerate((a0_ref, a1_ref, a2_ref, a3_ref)):
-        all_ref[e] = ref[...]
+    all_ref[0] = a0_ref[...]
+    all_ref[1] = a1_ref[0]
+    all_ref[2] = a2_ref[...]
+    all_ref[3] = a3_ref[0]
+    side_ref[0] = a1_ref[1]
+    side_ref[1] = a3_ref[1]
+    up_ref[3] = a3_ref[1]
+    down_ref[3] = a3_ref[1]
     for p in range(4):
         triple = all_ref[x ^ p]
         mid_ref[p] = triple
@@ -201,7 +211,8 @@
 
 
 def block_kernel(
-    mid_ref, lo_ref, hi_ref, own_ref, three_ref, four_ref, edge0_ref, edge1_ref, all_ref
+    mid_ref, lo_ref, hi_ref, side_ref,
+    own_ref, three_ref, near_ref, far_ref, one_lo_ref, one_hi_ref, all_ref, four_ref,
 ):
     g, z, x = place()
     grid = Grid()
@@ -218,23 +229,42 @@
 
     lo_ok = flag(jnp.logical_not((z == 0) & (g == 0)))
     hi_ok = flag(jnp.logical_not((z == 7) & (g == 7)))
+    for f in range(3):
+        side1, side3 = side_ref[0, f], side_ref[1, f]
+        one_lo_ref[f] = jnp.where(
+            x % 2 == 1, side1, jnp.where(x == 2, side3, lo_ref[3, f])
+        )
+        one_hi_ref[f] = jnp.where(
+            x % 2 == 0, side1, jnp.where(x == 1, side3, hi_ref[3, f])
+        )
     two_levels(grid, get, lo_ok, hi_ok, three_ref, four_ref)
-    for f in range(3):
-        edge0_ref[f] = three_ref[1, f]
-        edge1_ref[f] = three_ref[2, f]
-
-
-def order8_kernel(own_ref, a0_ref, a1_ref, a2_ref, a3_ref, mid_ref, up_ref, down_ref, all_ref):
+    odd = z % 2
+    near_ref[0] = four_ref[...]
+    near_ref[1] = three_ref[jnp.where(x == 0, 1 + odd, 2 - odd)]
+    edge = three_ref[2 - odd]
+    far_ref[...] = jnp.where(x == 3, edge, four_ref[...])
+
+
+def order8_kernel(
+    own_ref, a0_ref, a1_ref, a2_ref, a3_ref, mid_ref, up_ref, down_ref, side_ref, all_ref
+):
     g, z, x = place()
-    all_ref[0] = own_ref[...]
+    all_ref[0] = own_ref[0]
     for e, ref in enumerate((a0_ref, a1_ref, a2_ref, a3_ref)):
-        for slot in range(2):
-            all_ref[1 + 2 * e + slot] = ref[slot]
+        for slot in range(3):
+            all_ref[1 + 3 * e + slot] = ref[slot]
+    at1 = 2 + 3 * x
+    at3 = 2 + 3 * (x ^ 2)
+    at7 = 3 + 3 * (x ^ 3)
+    up_ref[7] = all_ref[at7]
+    down_ref[7] = all_ref[at7]
+    side_ref[0] = all_ref[jnp.where(z % 2 == 1, at1, jnp.where(z == 4, at7, at3))]
+    side_ref[1] = all_ref[jnp.where(z % 2 == 0, at1, jnp.where(z == 3, at7, at3))]
     for p in range(8):
         far = z ^ p
         holder = jnp.where(far > 4, far - 5, far - 1)
-        slot = jnp.where(far > 4, 1, 0)
-        source = jnp.where(far == 0, 0, 1 + 2 * (x ^ (holder & 3)) + slot)
+        slot = jnp.where(far > 4, 2, 0)
+        source = jnp.where(far == 0, 0, 1 + 3 * (x ^ (holder & 3)) + slot)
         triple = all_ref[source]
         mid_ref[p] = triple
         if p > 0:
@@ -244,8 +274,9 @@
 
 
 def group_kernel(
-    mid_ref, lo_ref, hi_ref,
-    four_ref, five_ref, six_ref, seven_ref, edge0_ref, edge1_ref, all_ref, next_ref,
+    mid_ref, lo_ref, hi_ref, side_ref,
+    four_ref, five_ref, six_ref, seven_ref, to_y_ref, to_core_ref, three_lo_ref, three_hi_ref,
+    all_ref, next_ref,
 ):
     g, z, x = place()
     grid = Grid()
@@ -273,17 +304,21 @@
     def get(p):
         return [next_ref[p, f] for f in range(3)]
 
+    for f in range(3):
+        three_lo_ref[f] = jnp.where(z == 0, lo_ref[7, f], side_ref[0, f])
+        three_hi_ref[f] = jnp.where(z == 7, hi_ref[7, f], side_ref[1, f])
     two_levels(grid, get, lo_ok, hi_ok, six_ref, seven_ref)
-    for f in range(3):
-        edge0_ref[f] = six_ref[1, f]
-        edge1_ref[f] = six_ref[2, f]
+    core = g % 2
+    to_y_ref[0] = seven_ref[...]
+    to_y_ref[1] = six_ref[2 - core]
+    to_core_ref[...] = six_ref[1 + core]
 
 
 def up_kernel(
     s_ref, c_ref, tex_ref, lab_ref, lo_ref, hi_ref, kappa_ref,
     one_ref, one_lo_ref, one_hi_ref, two_ref,
     three_ref, three_lo_ref, three_hi_ref, four_ref, five_ref,
-    six_ref, six_lo_ref, six_hi_ref, near_ref, other_ref,
+    six_ref, near_ref, other_ref,
     grad_ref, sums_ref,
     coarse_ref, power_ref, window_ref, fix_ref, sum_ref,
 ):
@@ -366,21 +401,23 @@
         sum_ref[0] = sum_ref[0] + part
 
     def window(base, lo_edge, mid, hi_edge):
-        window_ref[0] = lo_edge[...]
+        window_ref[0] = lo_edge
         for p in range(4):
             window_ref[1 + p] = mid[p]
-        window_ref[5] = hi_edge[...]
+        window_ref[5] = hi_edge
         return lambda d, f: window_ref[base + d, f]
 
     half6 = z // 4
     half3 = x // 2
-    level(window(half6, six_lo_ref, six_ref, six_hi_ref), half6,
+    six_lo = other_ref[5 - core] * flag(g > 0)
+    six_hi = other_ref[4 + core] * flag(g < 7)
+    level(window(half6, six_lo, six_ref, six_hi), half6,
           flag((g > 0) | (z > 3)), flag((g < 7) | (z < 4)))
     level(lambda d, f: five_ref[d, f], (z // 2) % 2,
           flag((g > 0) | (z > 1)), flag((g < 7) | (z < 6)))
     level(lambda d, f: four_ref[d, f], z % 2,
           flag((g > 0) | (z > 0)), flag((g < 7) | (z < 7)))
-    level(window(half3, three_lo_ref, three_ref, three_hi_ref), half3,
+    level(window(half3, three_lo_ref[...], three_ref, three_hi_ref[...]), half3,
           flag((g > 0) | (z > 0) | (x > 1)), flag((g < 7) | (z < 7) | (x < 2)))
     lo_ok = flag((g > 0) | (z > 0) | (x > 0))
     hi_ok = flag((g < 7) | (z < 7) | (x < 3))
@@ -464,59 +501,59 @@
         got = lax.all_to_all(sent, "dev", 0, 0)
         coef = jnp.pad(jnp.transpose(got, (1, 0, 2)).reshape(3, 64), ((0, 0), (0, 64)))
     with jax.named_scope("fine"):
-        kappa, one, two, edge0, edge1 = call(
+        kappa, one, two, to1, to3 = call(
             fine_kernel,
-            [(6,) + PLANE, (4,) + TRIPLE, TRIPLE, TRIPLE, TRIPLE],
+            [(6,) + PLANE, (4,) + TRIPLE, TRIPLE, (2,) + TRIPLE, (2,) + TRIPLE],
             [(10,) + PLANE],
             right_side, cotangent, texture, labels, lo, hi, coef,
         )
     with jax.named_scope("block_gather"):
-        mates = [swap(two, "dev", mask) for mask in (1, 2, 3)]
-        one_lo = shift(edge0, GD, 1)
-        one_hi = shift(edge1, GD, -1)
-        mid, up, down = call(
+        mates = [swap(sent, "dev", mask) for sent, mask in ((to1, 1), (two, 2), (to3, 3))]
+        mid, up, down, side = call(
             order4_kernel,
-            [(4,) + TRIPLE, (3,) + TRIPLE, (3,) + TRIPLE],
+            [(4,) + TRIPLE, (4,) + TRIPLE, (4,) + TRIPLE, (2,) + TRIPLE],
             [(4,) + TRIPLE],
             two, *mates,
         )
         blo = shift(up, GD, 4)
         bhi = shift(down, GD, -4)
     with jax.named_scope("block"):
-        two_own, three, four, edge0, edge1 = call(
+        two_own, three, near_sent, far_sent, one_lo, one_hi = call(
             block_kernel,
-            [(5,) + TRIPLE, (4,) + TRIPLE, TRIPLE, TRIPLE, TRIPLE],
-            [(10,) + TRIPLE],
-            mid, blo, bhi,
+            [(5,) + TRIPLE, (4,) + TRIPLE, (2,) + TRIPLE, TRIPLE, TRIPLE, TRIPLE],
+            [(10,) + TRIPLE, TRIPLE],
+            mid, blo, bhi, side,
         )
     with jax.named_scope("group_gather"):
-        near = lax.ppermute(four, "dev", [(i, i ^ (4 * (i % 4 + 1))) for i in range(32)])
-        far = lax.ppermute(
-            four, "dev", [(i, i ^ (4 * (i % 4 + 5))) for i in range(32) if i % 4 < 3]
-        )
-        three_lo = shift(edge0, GD, 4)
-        three_hi = shift(edge1, GD, -4)
-        pair = jnp.stack([near, far])
+        near_mask = (4, 8, 12, 16)
+        far_mask = (20, 24, 28, 28)
+        near = lax.ppermute(near_sent, "dev", [(i, i ^ near_mask[i % 4]) for i in range(32)])
+        far = lax.ppermute(far_sent, "dev", [(i, i ^ far_mask[i % 4]) for i in range(32)])
+        pair = jnp.concatenate([near, far[None]])
         pairs = [pair] + [swap(pair, "dev", mask) for mask in (1, 2, 3)]
-        mid, up, down = call(
+        mid, up, down, side = call(
             order8_kernel,
-            [(8,) + TRIPLE, (7,) + TRIPLE, (7,) + TRIPLE],
-            [(9,) + TRIPLE],
-            four, *pairs,
+            [(8,) + TRIPLE, (8,) + TRIPLE, (8,) + TRIPLE, (2,) + TRIPLE],
+            [(13,) + TRIPLE],
+            near_sent, *pairs,
         )
         glo = shift(up, "grp", 1)
         ghi = shift(down, "grp", -1)
     with jax.named_scope("group"):
-        four_own, five_own, six, seven, edge0, edge1 = call(
+        four_own, five_own, six, seven, to_y, to_core, three_lo, three_hi = call(
             group_kernel,
-            [(5,) + TRIPLE, (5,) + TRIPLE, (4,) + TRIPLE, TRIPLE, TRIPLE, TRIPLE],
+            [(5,) + TRIPLE, (5,) + TRIPLE, (4,) + TRIPLE, TRIPLE, (2,) + TRIPLE]
+            + [TRIPLE, TRIPLE, TRIPLE],
             [(22,) + TRIPLE, (10,) + TRIPLE],
-            mid, glo, ghi,
+            mid, glo, ghi, side,
         )
     with jax.named_scope("coarse_gather"):
-        column = jnp.stack([seven] + [swap(seven, "grp", 2 * mask) for mask in (1, 2, 3)])
-        six_lo = shift(edge0, "grp", 1)
-        six_hi = shift(edge1, "grp", -1)
+        at1 = swap(to_y, "grp", 2)
+        at2 = swap(seven, "grp", 4)
+        at3 = swap(to_y, "grp", 6)
+        g = lax.axis_index("grp")
+        relayed = jnp.where((g // 2) % 2 == g % 2, at1[1], at3[1])
+        column = jnp.stack([seven, at1[0], at2, at3[0], to_core, relayed])
         other = swap(column, "grp", 1)
     with jax.named_scope("up"):
         source_grad, sums = call(
@@ -525,7 +562,7 @@
             [(3, 10) + PLANE, (3, 2, 10) + PLANE, (6,) + TRIPLE, (2, 3) + PLANE, (3,) + PLANE],
             right_side, cotangent, texture, labels, lo, hi, kappa,
             one, one_lo, one_hi, two_own, three, three_lo, three_hi,
-            four_own, five_own, six, six_lo, six_hi, column, other,
+            four_own, five_own, six, column, other,
         )
     with jax.named_scope("table"):
         parts = lax.all_to_all(sums[0, :64].reshape(32, 2), "dev", 0, 0)

time: 189 us -> 182 us (0.963)
  starting transfers between devices: 71.5 us -> 56.6 us
  waiting for transfers between devices: 45.5 us -> 50.6 us
    ppermute x14 -> x8, starting transfers between devices: 54.8 us -> 31.1 us  [shift(): return lax.ppermute(block, axes, route)]
    ppermute x10, waiting for transfers between devices: 17.2 us -> 28.2 us  [swap(): lax.ppermute(block, axis, [(i, i ^ mask) for i in range(lax.axis_size(axi...]
    ppermute x10, starting transfers between devices: 13.3 us -> 22.9 us  [swap(): lax.ppermute(block, axis, [(i, i ^ mask) for i in range(lax.axis_size(axi...]
    ppermute x14 -> x8, waiting for transfers between devices: 23 us -> 17.3 us  [shift(): return lax.ppermute(block, axes, route)]
    unnamed x59 -> x42, local copies, waits for them, and re-layouts: 7.49 us -> 9.14 us
  transfers between devices with their start and end apart: 26 -> 20, of which waited for: 13 -> 13; matrix products, arithmetic and copies ran while one was open for 0% -> 1% of each run, Pallas kernels for 0% -> 0%
where the time goes in v2:
time: 182 us; the launch traced here: 181 us
  starting transfers between devices  56.6 us (31%)
  waiting for transfers between devices  50.6 us (28%)
  Pallas kernels  34.5 us (19%)
  blocking collectives  27.9 us (15%)
  local copies, waits for them, and re-layouts  10 us (5%)
    pallas_call x7, Pallas kernels, call(): pl.pallas_call(kernel, out_shape=[jax.ShapeDtypeStruct(shape, F32) for sh...  34.5 us
    ppermute x8, starting transfers between devices, shift(): return lax.ppermute(block, axes, route)  31.1 us
    ppermute x10, waiting for transfers between devices, swap(): lax.ppermute(block, axis, [(i, i ^ mask) for i in range(lax.axis_size(axi...  28.2 us
    ppermute x10, starting transfers between devices, swap(): lax.ppermute(block, axis, [(i, i ^ mask) for i in range(lax.axis_size(axi...  22.9 us
    ppermute x8, waiting for transfers between devices, shift(): return lax.ppermute(block, axes, route)  17.3 us
    all_to_all x1, blocking collectives, on_device(): got = lax.all_to_all(sent, 'dev', 0, 0)  14.5 us
    all_to_all x1, blocking collectives, on_device(): parts = lax.all_to_all(sums[0, :64].reshape(32, 2), 'dev', 0, 0)  13.4 us
    unnamed x42, local copies, waits for them, and re-layouts  9.14 us
  transfers between devices with their start and end apart: 20, of which 13 were waited for; matrix products, arithmetic and copies ran while one was open for 1% of the time, Pallas kernels for 0%

profile of v2, /device:TPU:1, one launch (start us, length us, event | category | flops | bytes accessed | tf_op | source)
XLA Modules:
  0.0 181.1 jit_solution(12597792164633970927)
XLA Ops:
  4.0 4.1 %collective-permute-start = (f32[10,32,256]{2,1,0:T(8,128)}, f32[10,32,256]{2,1,0:T(8,128)S(1)}, u32[]{:S(2)}, u32[]{:S(2)}) collective-permute-start(f32[10,32,256]{2,1,0:T(8,128)} %get-tuple-element.33), channel_id=1, source_target_pairs={{0,1},{1,2},{2,3},{3,4},{4,5},{5,6},{6,7},{7,8},{8,9},{9,10},{10,1... | collective-permute-start | bytes 983048 | tf_op jit(solution)/shard_map/fine_halo/ppermute | solution.py:110
  8.1 9.0 %collective-permute-start.1 = (f32[10,32,256]{2,1,0:T(8,128)}, f32[10,32,256]{2,1,0:T(8,128)S(1)}, u32[]{:S(2)}, u32[]{:S(2)}) collective-permute-start(f32[10,32,256]{2,1,0:T(8,128)} %get-tuple-element.34), channel_id=1, source_target_pairs={{1,0},{2,1},{3,2},{4,3},{5,4},{6,5},{7,6},{8,7},{9,8},{10,9},{11,1... | collective-permute-start | bytes 983048 | tf_op jit(solution)/shard_map/fine_halo/ppermute | solution.py:110
  19.1 3.6 %collective-permute-start.2 = (f32[1,2]{1,0:T(1,128)S(1)}, f32[1,2]{1,0:T(1,128)S(1)}, u32[]{:S(2)}, u32[]{:S(2)}) collective-permute-start(f32[1,2]{1,0:T(1,128)S(1)} %copy-done.16), channel_id=1, source_target_pairs={{0,32},{32,64},{64,96},{96,128},{128,160},{160,192},{192,224},{1,3... | collective-permute-start | bytes 32 | tf_op jit(solution)/shard_map/fine_halo/ppermute | solution.py:110
  23.6 14.5 %all_to_all.14 = f32[32,3,2]{1,2,0:T(2,128)S(1)} all-to-all(f32[32,3,2]{1,2,0:T(2,128)S(1)} %broadcast_in_dim.12), channel_id=1, replica_groups=mesh['grp'=8,'dev'=32] {'dev'}, dimensions={0} | all-to-all | bytes 1536 | tf_op jit(solution)/shard_map/coef_rows/all_to_all | solution.py:501
  40.2 5.3 %fine.1 = (f32[6,32,256]{2,1,0:T(8,128)}, f32[4,3,32,256]{3,2,1,0:T(8,128)}, f32[3,32,256]{2,1,0:T(8,128)}, f32[2,3,32,256]{3,2,1,0:T(8,128)}, f32[2,3,32,256]{3,2,1,0:T(8,128)}) custom-call(f32[4,32,256]{2,1,0:T(8,128)} %s_ref.5, f32[4,32,256]{2,1,0:T(8,128)} %c_ref.5, f32[4,32,256]{2,1,0:T(8,128)} %tex_ref.5, s32[4,32,2]{2,1,0:T(8,128)} %copy.17.lab_ref, ...), custom_call_target="tpu_custom_call" | custom-call | tf_op jit(solution)/shard_map/fine/pallas_call | solution.py:119
  46.6 2.1 %collective-permute-start.5 = (f32[3,32,256]{2,1,0:T(8,128)}, f32[3,32,256]{2,1,0:T(8,128)S(1)}, u32[]{:S(2)}, u32[]{:S(2)}) collective-permute-start(f32[3,32,256]{2,1,0:T(8,128)} %get-tuple-element.37.a0_ref), channel_id=1, source_target_pairs={{0,2},{1,3},{2,0},{3,1},{4,6},{5,7},{6,4},{7,5},{8,10},{9,11},{10,... | collective-permute-start | bytes 294920 | tf_op jit(solution)/shard_map/block_gather/ppermute | solution.py:114
  48.8 4.6 %collective-permute-done.5.a2_ref = f32[3,32,256]{2,1,0:T(8,128)S(1)} collective-permute-done((f32[3,32,256]{2,1,0:T(8,128)}, f32[3,32,256]{2,1,0:T(8,128)S(1)}, u32[]{:S(2)}, u32[]{:S(2)}) %collective-permute-start.5) | collective-permute-done | bytes 98336 | tf_op jit(solution)/shard_map/block_gather/ppermute | solution.py:114
  54.8 2.3 %block_gather.1 = (f32[4,3,32,256]{3,2,1,0:T(8,128)}, f32[4,3,32,256]{3,2,1,0:T(8,128)}, f32[4,3,32,256]{3,2,1,0:T(8,128)}, f32[2,3,32,256]{3,2,1,0:T(8,128)}) custom-call(f32[3,32,256]{2,1,0:T(8,128)} %get-tuple-element.37.a0_ref, f32[2,3,32,256]{3,2,1,0:T(8,128)} %copy-done.12, f32[3,32,256]{2,1,0:T(8,128)} %copy-done.14, f32[2,3,32,256]{3,2,1,0:T(8,128)} %copy-done.13), custom_call_target="tpu_custom_call" | custom-call | tf_op jit(solution)/shard_map/block_gather/pallas_call | solution.py:119
  59.1 4.7 %collective-permute-start.8 = (f32[4,3,32,256]{3,2,1,0:T(8,128)}, f32[4,3,32,256]{3,2,1,0:T(8,128)S(1)}, u32[]{:S(2)}, u32[]{:S(2)}) collective-permute-start(f32[4,3,32,256]{3,2,1,0:T(8,128)} %get-tuple-element.42), channel_id=1, source_target_pairs={{4,0},{5,1},{6,2},{7,3},{8,4},{9,5},{10,6},{11,7},{12,8},{13,9},{1... | collective-permute-start | bytes 1179656 | tf_op jit(solution)/shard_map/block_gather/ppermute | solution.py:110
  63.9 5.0 %collective-permute-done.7.lo_ref = f32[4,3,32,256]{3,2,1,0:T(8,128)S(1)} collective-permute-done((f32[4,3,32,256]{3,2,1,0:T(8,128)}, f32[4,3,32,256]{3,2,1,0:T(8,128)S(1)}, u32[]{:S(2)}, u32[]{:S(2)}) %collective-permute-start.7) | collective-permute-done | bytes 393248 | tf_op jit(solution)/shard_map/block_gather/ppermute | solution.py:110
  69.7 3.6 %block.1 = (f32[5,3,32,256]{3,2,1,0:T(8,128)}, f32[4,3,32,256]{3,2,1,0:T(8,128)}, f32[2,3,32,256]{3,2,1,0:T(8,128)}, f32[3,32,256]{2,1,0:T(8,128)}, f32[3,32,256]{2,1,0:T(8,128)}, /*index=5*/f32[3,32,256]{2,1,0:T(8,128)}) custom-call(f32[4,3,32,256]{3,2,1,0:T(8,128)} %get-tuple-element.40.mid_ref, f32[4,3,32,256]{3,2,1,0:T(8,128)} %copy-done.7, ...), custom_call_target="tpu_custom_call" | custom-call | tf_op jit(solution)/shard_map/block/pallas_call | solution.py:119
  75.9 5.1 %collective-permute-done.10 = f32[3,32,256]{2,1,0:T(8,128)S(1)} collective-permute-done((f32[3,32,256]{2,1,0:T(8,128)}, f32[3,32,256]{2,1,0:T(8,128)S(1)}, u32[]{:S(2)}, u32[]{:S(2)}) %collective-permute-start.10) | collective-permute-done | bytes 98336 | tf_op jit(solution)/shard_map/group_gather/ppermute | solution.py:531
  81.1 6.3 %collective-permute-start.11 = (f32[3,3,32,256]{3,2,1,0:T(8,128)S(1)}, f32[3,3,32,256]{3,2,1,0:T(8,128)S(1)}, u32[]{:S(2)}, u32[]{:S(2)}) collective-permute-start(f32[3,3,32,256]{3,2,1,0:T(8,128)S(1)} %pad_maximum_fusion.a0_ref), channel_id=1, source_target_pairs={{0,1},{1,0},{2,3},{3,2},{4,5},{5,4},{6,7},{7,6},{8,9},{9,8},{10,11... | collective-permute-start | bytes 884744 | tf_op jit(solution)/shard_map/group_gather/ppermute | solution.py:114
  87.4 9.8 %collective-permute-start.12 = (f32[3,3,32,256]{3,2,1,0:T(8,128)S(1)}, f32[3,3,32,256]{3,2,1,0:T(8,128)S(1)}, u32[]{:S(2)}, u32[]{:S(2)}) collective-permute-start(f32[3,3,32,256]{3,2,1,0:T(8,128)S(1)} %pad_maximum_fusion.a0_ref), channel_id=1, source_target_pairs={{0,2},{1,3},{2,0},{3,1},{4,6},{5,7},{6,4},{7,5},{8,10},{9,11},{10,... | collective-permute-start | bytes 884744 | tf_op jit(solution)/shard_map/group_gather/ppermute | solution.py:114
  97.2 13.0 %collective-permute-done.12.a2_ref = f32[3,3,32,256]{3,2,1,0:T(8,128)S(1)} collective-permute-done((f32[3,3,32,256]{3,2,1,0:T(8,128)S(1)}, f32[3,3,32,256]{3,2,1,0:T(8,128)S(1)}, u32[]{:S(2)}, u32[]{:S(2)}) %collective-permute-start.12) | collective-permute-done | bytes 294944 | tf_op jit(solution)/shard_map/group_gather/ppermute | solution.py:114
  112.9 3.0 %group_gather.1 = (f32[8,3,32,256]{3,2,1,0:T(8,128)}, f32[8,3,32,256]{3,2,1,0:T(8,128)}, f32[8,3,32,256]{3,2,1,0:T(8,128)}, f32[2,3,32,256]{3,2,1,0:T(8,128)}) custom-call(f32[2,3,32,256]{3,2,1,0:T(8,128)} %get-tuple-element.48.own_ref, f32[3,3,32,256]{3,2,1,0:T(8,128)} %copy-done.2, f32[3,3,32,256]{3,2,1,0:T(8,128)} %copy-done.9, ...), custom_call_target="tpu_custom_call" | custom-call | tf_op jit(solution)/shard_map/group_gather/pallas_call | solution.py:119
  115.9 3.8 %collective-permute-start.14 = (f32[8,3,32,256]{3,2,1,0:T(8,128)}, f32[8,3,32,256]{3,2,1,0:T(8,128)S(1)}, u32[]{:S(2)}, u32[]{:S(2)}) collective-permute-start(f32[8,3,32,256]{3,2,1,0:T(8,128)} %get-tuple-element.51), channel_id=1, source_target_pairs={{0,32},{32,64},{64,96},{96,128},{128,160},{160,192},{192,224},{1,3... | collective-permute-start | bytes 2359304 | tf_op jit(solution)/shard_map/group_gather/ppermute | solution.py:110
  121.6 7.3 %collective-permute-done.14.lo_ref = f32[8,3,32,256]{3,2,1,0:T(8,128)S(1)} collective-permute-done((f32[8,3,32,256]{3,2,1,0:T(8,128)}, f32[8,3,32,256]{3,2,1,0:T(8,128)S(1)}, u32[]{:S(2)}, u32[]{:S(2)}) %collective-permute-start.14) | collective-permute-done | bytes 786464 | tf_op jit(solution)/shard_map/group_gather/ppermute | solution.py:110
  128.9 4.3 %collective-permute-done.15.hi_ref = f32[8,3,32,256]{3,2,1,0:T(8,128)S(1)} collective-permute-done((f32[8,3,32,256]{3,2,1,0:T(8,128)}, f32[8,3,32,256]{3,2,1,0:T(8,128)S(1)}, u32[]{:S(2)}, u32[]{:S(2)}) %collective-permute-start.15) | collective-permute-done | bytes 786464 | tf_op jit(solution)/shard_map/group_gather/ppermute | solution.py:110
  134.1 6.8 %group.1 = (f32[5,3,32,256]{3,2,1,0:T(8,128)}, f32[5,3,32,256]{3,2,1,0:T(8,128)}, f32[4,3,32,256]{3,2,1,0:T(8,128)}, f32[3,32,256]{2,1,0:T(8,128)}, f32[2,3,32,2...) custom-call(f32[8,3,32,256]{3,2,1,0:T(8,128)} %get-tuple-element.50.mid_ref, ...), custom_call_target="tpu_custom_call" | custom-call | tf_op jit(solution)/shard_map/group/pallas_call | solution.py:119
  145.2 2.2 %collective-permute-done.16 = f32[2,3,32,256]{3,2,1,0:T(8,128)S(1)} collective-permute-done((f32[2,3,32,256]{3,2,1,0:T(8,128)}, f32[2,3,32,256]{3,2,1,0:T(8,128)S(1)}, u32[]{:S(2)}, u32[]{:S(2)}) %collective-permute-start.16) | collective-permute-done | bytes 196640 | tf_op jit(solution)/shard_map/coarse_gather/ppermute | solution.py:114
  148.6 3.3 %collective-permute-done.18 = f32[2,3,32,256]{3,2,1,0:T(8,128)S(1)} collective-permute-done((f32[2,3,32,256]{3,2,1,0:T(8,128)}, f32[2,3,32,256]{3,2,1,0:T(8,128)S(1)}, u32[]{:S(2)}, u32[]{:S(2)}) %collective-permute-start.18) | collective-permute-done | bytes 196640 | tf_op jit(solution)/shard_map/coarse_gather/ppermute | solution.py:114
  154.9 11.5 %up.1 = (f32[4,32,256]{2,1,0:T(8,128)}, f32[1,128]{1,0:T(1,128)}) custom-call(f32[4,32,256]{2,1,0:T(8,128)} %s_ref.5, f32[4,32,256]{2,1,0:T(8,128)} %c_ref.5, f32[4,32,256]{2,1,0:T(8,128)} %tex_ref.5, s32[4,32,2]{2,1,0:T(8,128)} %copy.17.lab_ref, f32[10,32,256]{2,1,0:T(8,128)} %copy-done, f32[10,32,256]{2,1,0:T(8,128)} %copy-done.1, ...), custom_call_target="tpu_custom_call" | custom-call | tf_op jit(solution)/shard_map/up/pallas_call | solution.py:119
  167.2 13.4 %all_to_all.15 = f32[32,1,2]{2,1,0:T(1,128)S(1)} all-to-all(f32[32,1,2]{2,1,0:T(1,128)S(1)} %bitcast.14), channel_id=1, replica_groups=mesh['grp'=8,'dev'=32] {'dev'}, dimensions={0} | all-to-all | bytes 512 | tf_op jit(solution)/shard_map/table/all_to_all | solution.py:568
  (77 shorter events, 31.6 us)
Async XLA Ops:
  4.0 13.1 %copy-start.16 = (f32[1,2]{1,0:T(1,128)S(1)}, f32[1,2]{1,0:T(1,128)}, u32[]{:S(2)}) copy-start(f32[1,2]{1,0:T(1,128)} %param.9) | copy-start | bytes 28
  4.0 34.7 %collective-permute-start = (f32[10,32,256]{2,1,0:T(8,128)}, f32[10,32,256]{2,1,0:T(8,128)S(1)}, u32[]{:S(2)}, u32[]{:S(2)}) collective-permute-start(f32[10,32,256]{2,1,0:T(8,128)} %get-tuple-element.33), channel_id=1, source_target_pairs={{0,1},{1,2},{2,3},{3,4},{4,5},{5,6},{6,7},{7,8},{8,9},{9,10},{10,1... | collective-permute-start | bytes 983048 | tf_op jit(solution)/shard_map/fine_halo/ppermute | solution.py:110
  8.1 30.6 %collective-permute-start.1 = (f32[10,32,256]{2,1,0:T(8,128)}, f32[10,32,256]{2,1,0:T(8,128)S(1)}, u32[]{:S(2)}, u32[]{:S(2)}) collective-permute-start(f32[10,32,256]{2,1,0:T(8,128)} %get-tuple-element.34), channel_id=1, source_target_pairs={{1,0},{2,1},{3,2},{4,3},{5,4},{6,5},{7,6},{8,7},{9,8},{10,9},{11,1... | collective-permute-start | bytes 983048 | tf_op jit(solution)/shard_map/fine_halo/ppermute | solution.py:110
  17.2 5.6 %collective-permute-start.3 = (f32[1,2]{1,0:T(1,128)S(1)}, f32[1,2]{1,0:T(1,128)S(1)}, u32[]{:S(2)}, u32[]{:S(2)}) collective-permute-start(f32[1,2]{1,0:T(1,128)S(1)} %copy-done.16), channel_id=1, source_target_pairs={{32,0},{64,32},{96,64},{128,96},{160,128},{192,160},{224,192},{33,... | collective-permute-start | bytes 32 | tf_op jit(solution)/shard_map/fine_halo/ppermute | solution.py:110
  19.1 4.3 %collective-permute-start.2 = (f32[1,2]{1,0:T(1,128)S(1)}, f32[1,2]{1,0:T(1,128)S(1)}, u32[]{:S(2)}, u32[]{:S(2)}) collective-permute-start(f32[1,2]{1,0:T(1,128)S(1)} %copy-done.16), channel_id=1, source_target_pairs={{0,32},{32,64},{64,96},{96,128},{128,160},{160,192},{192,224},{1,3... | collective-permute-start | bytes 32 | tf_op jit(solution)/shard_map/fine_halo/ppermute | solution.py:110
  45.5 7.9 %collective-permute-start.4 = (f32[2,3,32,256]{3,2,1,0:T(8,128)}, f32[2,3,32,256]{3,2,1,0:T(8,128)S(1)}, u32[]{:S(2)}, u32[]{:S(2)}) collective-permute-start(f32[2,3,32,256]{3,2,1,0:T(8,128)} %get-tuple-element.38), channel_id=1, source_target_pairs={{0,1},{1,0},{2,3},{3,2},{4,5},{5,4},{6,7},{7,6},{8,9},{9,8},{10,11... | collective-permute-start | bytes 589832 | tf_op jit(solution)/shard_map/block_gather/ppermute | solution.py:114
  45.5 7.9 %collective-permute-start.6 = (f32[2,3,32,256]{3,2,1,0:T(8,128)}, f32[2,3,32,256]{3,2,1,0:T(8,128)S(1)}, u32[]{:S(2)}, u32[]{:S(2)}) collective-permute-start(f32[2,3,32,256]{3,2,1,0:T(8,128)} %get-tuple-element.39), channel_id=1, source_target_pairs={{0,3},{1,2},{2,1},{3,0},{4,7},{5,6},{6,5},{7,4},{8,11},{9,10},{10,... | collective-permute-start | bytes 589832 | tf_op jit(solution)/shard_map/block_gather/ppermute | solution.py:114
  46.6 6.8 %collective-permute-start.5 = (f32[3,32,256]{2,1,0:T(8,128)}, f32[3,32,256]{2,1,0:T(8,128)S(1)}, u32[]{:S(2)}, u32[]{:S(2)}) collective-permute-start(f32[3,32,256]{2,1,0:T(8,128)} %get-tuple-element.37.a0_ref), channel_id=1, source_target_pairs={{0,2},{1,3},{2,0},{3,1},{4,6},{5,7},{6,4},{7,5},{8,10},{9,11},{10,... | collective-permute-start | bytes 294920 | tf_op jit(solution)/shard_map/block_gather/ppermute | solution.py:114
  57.1 11.7 %collective-permute-start.7 = (f32[4,3,32,256]{3,2,1,0:T(8,128)}, f32[4,3,32,256]{3,2,1,0:T(8,128)S(1)}, u32[]{:S(2)}, u32[]{:S(2)}) collective-permute-start(f32[4,3,32,256]{3,2,1,0:T(8,128)} %get-tuple-element.41), channel_id=1, source_target_pairs={{0,4},{1,5},{2,6},{3,7},{4,8},{5,9},{6,10},{7,11},{8,12},{9,13},{1... | collective-permute-start | bytes 1179656 | tf_op jit(solution)/shard_map/block_gather/ppermute | solution.py:110
  59.1 9.8 %collective-permute-start.8 = (f32[4,3,32,256]{3,2,1,0:T(8,128)}, f32[4,3,32,256]{3,2,1,0:T(8,128)S(1)}, u32[]{:S(2)}, u32[]{:S(2)}) collective-permute-start(f32[4,3,32,256]{3,2,1,0:T(8,128)} %get-tuple-element.42), channel_id=1, source_target_pairs={{4,0},{5,1},{6,2},{7,3},{8,4},{9,5},{10,6},{11,7},{12,8},{13,9},{1... | collective-permute-start | bytes 1179656 | tf_op jit(solution)/shard_map/block_gather/ppermute | solution.py:110
  73.3 7.7 %collective-permute-start.9 = (f32[2,3,32,256]{3,2,1,0:T(8,128)}, f32[2,3,32,256]{3,2,1,0:T(8,128)S(1)}, u32[]{:S(2)}, u32[]{:S(2)}) collective-permute-start(f32[2,3,32,256]{3,2,1,0:T(8,128)} %get-tuple-element.48.own_ref), channel_id=1, source_target_pairs={{0,4},{1,9},{2,14},{3,19},{4,0},{5,13},{6,10},{7,23},{8,12},{9,1},... | collective-permute-start | bytes 589832 | tf_op jit(solution)/shard_map/group_gather/ppermute | solution.py:530
  74.4 6.7 %collective-permute-start.10 = (f32[3,32,256]{2,1,0:T(8,128)}, f32[3,32,256]{2,1,0:T(8,128)S(1)}, u32[]{:S(2)}, u32[]{:S(2)}) collective-permute-start(f32[3,32,256]{2,1,0:T(8,128)} %get-tuple-element.49), channel_id=1, source_target_pairs={{0,20},{1,25},{2,30},{3,31},{4,16},{5,29},{6,26},{7,27},{8,28},{9,... | collective-permute-start | bytes 294920 | tf_op jit(solution)/shard_map/group_gather/ppermute | solution.py:531
  81.1 31.1 %copy-start.2 = (f32[3,3,32,256]{3,2,1,0:T(8,128)}, f32[3,3,32,256]{3,2,1,0:T(8,128)S(1)}, u32[]{:S(2)}) copy-start(f32[3,3,32,256]{3,2,1,0:T(8,128)S(1)} %pad_maximum_fusion.a0_ref) | copy-start | bytes 884740
  81.1 16.1 %collective-permute-start.11 = (f32[3,3,32,256]{3,2,1,0:T(8,128)S(1)}, f32[3,3,32,256]{3,2,1,0:T(8,128)S(1)}, u32[]{:S(2)}, u32[]{:S(2)}) collective-permute-start(f32[3,3,32,256]{3,2,1,0:T(8,128)S(1)} %pad_maximum_fusion.a0_ref), channel_id=1, source_target_pairs={{0,1},{1,0},{2,3},{3,2},{4,5},{5,4},{6,7},{7,6},{8,9},{9,8},{10,11... | collective-permute-start | bytes 884744 | tf_op jit(solution)/shard_map/group_gather/ppermute | solution.py:114
  87.4 22.8 %collective-permute-start.12 = (f32[3,3,32,256]{3,2,1,0:T(8,128)S(1)}, f32[3,3,32,256]{3,2,1,0:T(8,128)S(1)}, u32[]{:S(2)}, u32[]{:S(2)}) collective-permute-start(f32[3,3,32,256]{3,2,1,0:T(8,128)S(1)} %pad_maximum_fusion.a0_ref), channel_id=1, source_target_pairs={{0,2},{1,3},{2,0},{3,1},{4,6},{5,7},{6,4},{7,5},{8,10},{9,11},{10,... | collective-permute-start | bytes 884744 | tf_op jit(solution)/shard_map/group_gather/ppermute | solution.py:114
  97.2 15.0 %collective-permute-start.13 = (f32[3,3,32,256]{3,2,1,0:T(8,128)S(1)}, f32[3,3,32,256]{3,2,1,0:T(8,128)S(1)}, u32[]{:S(2)}, u32[]{:S(2)}) collective-permute-start(f32[3,3,32,256]{3,2,1,0:T(8,128)S(1)} %pad_maximum_fusion.a0_ref), channel_id=1, source_target_pairs={{0,3},{1,2},{2,1},{3,0},{4,7},{5,6},{6,5},{7,4},{8,11},{9,10},{10,... | collective-permute-start | bytes 884744 | tf_op jit(solution)/shard_map/group_gather/ppermute | solution.py:114
  97.2 15.0 %copy-start.9 = (f32[3,3,32,256]{3,2,1,0:T(8,128)}, f32[3,3,32,256]{3,2,1,0:T(8,128)S(1)}, u32[]{:S(2)}) copy-start(f32[3,3,32,256]{3,2,1,0:T(8,128)S(1)} %collective-permute-done.11.a1_ref) | copy-start | bytes 884740
  115.9 13.0 %collective-permute-start.14 = (f32[8,3,32,256]{3,2,1,0:T(8,128)}, f32[8,3,32,256]{3,2,1,0:T(8,128)S(1)}, u32[]{:S(2)}, u32[]{:S(2)}) collective-permute-start(f32[8,3,32,256]{3,2,1,0:T(8,128)} %get-tuple-element.51), channel_id=1, source_target_pairs={{0,32},{32,64},{64,96},{96,128},{128,160},{160,192},{192,224},{1,3... | collective-permute-start | bytes 2359304 | tf_op jit(solution)/shard_map/group_gather/ppermute | solution.py:110
  119.7 13.5 %collective-permute-start.15 = (f32[8,3,32,256]{3,2,1,0:T(8,128)}, f32[8,3,32,256]{3,2,1,0:T(8,128)S(1)}, u32[]{:S(2)}, u32[]{:S(2)}) collective-permute-start(f32[8,3,32,256]{3,2,1,0:T(8,128)} %get-tuple-element.52), channel_id=1, source_target_pairs={{32,0},{64,32},{96,64},{128,96},{160,128},{192,160},{224,192},{33,... | collective-permute-start | bytes 2359304 | tf_op jit(solution)/shard_map/group_gather/ppermute | solution.py:110
  128.9 4.3 %copy-start.4 = (f32[8,3,32,256]{3,2,1,0:T(8,128)}, f32[8,3,32,256]{3,2,1,0:T(8,128)S(1)}, u32[]{:S(2)}) copy-start(f32[8,3,32,256]{3,2,1,0:T(8,128)S(1)} %collective-permute-done.14.lo_ref) | copy-start | bytes 2359300
  140.9 6.5 %collective-permute-start.16 = (f32[2,3,32,256]{3,2,1,0:T(8,128)}, f32[2,3,32,256]{3,2,1,0:T(8,128)S(1)}, u32[]{:S(2)}, u32[]{:S(2)}) collective-permute-start(f32[2,3,32,256]{3,2,1,0:T(8,128)} %get-tuple-element.60), channel_id=1, source_target_pairs={{0,64},{32,96},{64,0},{96,32},{128,192},{160,224},{192,128},{224,1... | collective-permute-start | bytes 589832 | tf_op jit(solution)/shard_map/coarse_gather/ppermute | solution.py:114
  142.4 9.5 %collective-permute-start.18 = (f32[2,3,32,256]{3,2,1,0:T(8,128)}, f32[2,3,32,256]{3,2,1,0:T(8,128)S(1)}, u32[]{:S(2)}, u32[]{:S(2)}) collective-permute-start(f32[2,3,32,256]{3,2,1,0:T(8,128)} %get-tuple-element.60), channel_id=1, source_target_pairs={{0,192},{32,224},{64,128},{96,160},{128,64},{160,96},{192,0},{224,... | collective-permute-start | bytes 589832 | tf_op jit(solution)/shard_map/coarse_gather/ppermute | solution.py:114
  142.4 6.2 %collective-permute-start.17 = (f32[3,32,256]{2,1,0:T(8,128)}, f32[3,32,256]{2,1,0:T(8,128)S(1)}, u32[]{:S(2)}, u32[]{:S(2)}) collective-permute-start(f32[3,32,256]{2,1,0:T(8,128)} %get-tuple-element.59), channel_id=1, source_target_pairs={{0,128},{32,160},{64,192},{96,224},{128,0},{160,32},{192,64},{224,... | collective-permute-start | bytes 294920 | tf_op jit(solution)/shard_map/coarse_gather/ppermute | solution.py:114
  151.9 2.1 %collective-permute-start.19 = (f32[6,3,32,256]{3,2,1,0:T(8,128)S(1)}, f32[6,3,32,256]{3,2,1,0:T(8,128)S(1)}, u32[]{:S(2)}, u32[]{:S(2)}) collective-permute-start(f32[6,3,32,256]{3,2,1,0:T(8,128)S(1)} %fusion.near_ref), channel_id=1, source_target_pairs={{0,32},{32,0},{64,96},{96,64},{128,160},{160,128},{192,224},{224,1... | collective-permute-start | bytes 1769480 | tf_op jit(solution)/shard_map/coarse_gather/ppermute | solution.py:114
  (14 other events, 15.6 us)

commit v3 on v2

--- a/solution.py
+++ b/solution.py
@@ -125,59 +125,47 @@
     )(*args)
 
 
-def pack_kernel(s_ref, c_ref, tex_ref, lab_ref, up_ref, down_ref):
-    lane = lax.broadcasted_iota(jnp.int32, PLANE, 1)
-    for out_ref, first in ((up_ref, 1), (down_ref, 0)):
-        marks = jnp.zeros(PLANE, F32)
-        for p in range(3):
-            out_ref[p] = s_ref[first + p]
-            out_ref[3 + p] = c_ref[first + p]
-            out_ref[6 + p] = tex_ref[first + p]
-            for t in range(2):
-                column = lab_ref[first + p, :, t : t + 1].astype(F32)
-                marks = jnp.where(lane == 2 * p + t, column, marks)
-        out_ref[9] = marks
+def pack_kernel(s_ref, c_ref, up_ref, down_ref):
+    for p in range(3):
+        up_ref[p] = s_ref[1 + p]
+        up_ref[3 + p] = c_ref[1 + p]
+        down_ref[p] = s_ref[p]
+        down_ref[3 + p] = c_ref[p]
+
+
+def kappa_kernel(tex_ref, lab_ref, coef_ref, kappa_ref, up_ref, down_ref):
+    lane = lax.broadcasted_iota(jnp.int32, (NY, TILE), 1)
+    row = coef_ref[...]
+    for p in range(4):
+        for t in range(2):
+            hit = lane == lab_ref[p, :, t : t + 1]
+            value = jnp.sum(jnp.where(hit, row, 0.0), axis=1, keepdims=True)
+            cut = slice(t * TILE, (t + 1) * TILE)
+            kappa_ref[p, :, cut] = value * tex_ref[p, :, cut]
+    for p in range(3):
+        up_ref[p] = kappa_ref[1 + p]
+        down_ref[p] = kappa_ref[p]
 
 
 def fine_kernel(
-    s_ref, c_ref, tex_ref, lab_ref, lo_ref, hi_ref, coef_ref,
-    kappa_ref, one_ref, two_ref, to1_ref, to3_ref, k_ref,
+    s_ref, c_ref, own_ref, lo_ref, hi_ref, k_lo_ref, k_hi_ref,
+    kappa_ref, one_ref, two_ref, to1_ref, to3_ref,
 ):
     g, z, x = place()
     grid = Grid()
     first = (z == 0) & (x == 0)
     last = (z == 7) & (x == 3)
-    row_here = coef_ref[1:2, :]
-    row_lo = jnp.where(first, coef_ref[0:1, :], row_here)
-    row_hi = jnp.where(last, coef_ref[2:3, :], row_here)
-    lane = lax.broadcasted_iota(jnp.int32, (NY, TILE), 1)
-    lane_f = lane.astype(F32)
-
-    def looked_up(column, row):
-        hit = lane_f == column
-        return jnp.sum(jnp.where(hit, row, 0.0), axis=1, keepdims=True)
-
-    for p in range(10):
-        for t in range(2):
-            if p < 3:
-                column, row, tex = lo_ref[9, :, 2 * p + t : 2 * p + t + 1], row_lo, lo_ref[6 + p]
-            elif p < 7:
-                column, row = lab_ref[p - 3, :, t : t + 1].astype(F32), row_here
-                tex = tex_ref[p - 3]
-            else:
-                q = p - 7
-                column, row, tex = hi_ref[9, :, 2 * q + t : 2 * q + t + 1], row_hi, hi_ref[6 + q]
-            cut = slice(t * TILE, (t + 1) * TILE)
-            k_ref[p, :, cut] = looked_up(column, row) * tex[:, cut]
-    for p in range(6):
-        kappa_ref[p] = k_ref[2 + p]
+    kappa_ref[0] = k_lo_ref[2]
+    kappa_ref[5] = k_hi_ref[0]
+    for p in range(4):
+        kappa_ref[1 + p] = own_ref[p]
 
     def get(p):
         if p < 3:
-            return [lo_ref[p], lo_ref[3 + p], k_ref[p]]
+            return [lo_ref[p], lo_ref[3 + p], k_lo_ref[p]]
         if p < 7:
-            return [s_ref[p - 3], c_ref[p - 3], k_ref[p]]
-        return [hi_ref[p - 7], hi_ref[p - 4], k_ref[p]]
+            return [s_ref[p - 3], c_ref[p - 3], own_ref[p - 3]]
+        return [hi_ref[p - 7], hi_ref[p - 4], k_hi_ref[p - 7]]
 
     lo_ok = flag(jnp.logical_not(first & (g == 0)))
     hi_ok = flag(jnp.logical_not(last & (g == 7)))
@@ -212,7 +200,7 @@
 
 def block_kernel(
     mid_ref, lo_ref, hi_ref, side_ref,
-    own_ref, three_ref, near_ref, far_ref, one_lo_ref, one_hi_ref, all_ref, four_ref,
+    own_ref, three_ref, four_ref, to1_ref, to3_ref, to7_ref, one_lo_ref, one_hi_ref, all_ref,
 ):
     g, z, x = place()
     grid = Grid()
@@ -239,32 +227,33 @@
         )
     two_levels(grid, get, lo_ok, hi_ok, three_ref, four_ref)
     odd = z % 2
-    near_ref[0] = four_ref[...]
-    near_ref[1] = three_ref[jnp.where(x == 0, 1 + odd, 2 - odd)]
-    edge = three_ref[2 - odd]
-    far_ref[...] = jnp.where(x == 3, edge, four_ref[...])
+    to1_ref[0] = four_ref[...]
+    to3_ref[0] = four_ref[...]
+    to1_ref[1] = three_ref[1 + odd]
+    to3_ref[1] = three_ref[2 - odd]
+    to7_ref[...] = three_ref[2 - odd]
 
 
 def order8_kernel(
-    own_ref, a0_ref, a1_ref, a2_ref, a3_ref, mid_ref, up_ref, down_ref, side_ref, all_ref
+    own_ref, b1_ref, b2_ref, b3_ref, b7_ref, a0_ref, a1_ref, a2_ref, a3_ref,
+    mid_ref, up_ref, down_ref, side_ref, all_ref,
 ):
     g, z, x = place()
-    all_ref[0] = own_ref[0]
+    all_ref[0] = own_ref[...]
+    all_ref[1] = b1_ref[0]
+    all_ref[2] = b2_ref[...]
+    all_ref[3] = b3_ref[0]
     for e, ref in enumerate((a0_ref, a1_ref, a2_ref, a3_ref)):
-        for slot in range(3):
-            all_ref[1 + 3 * e + slot] = ref[slot]
-    at1 = 2 + 3 * x
-    at3 = 2 + 3 * (x ^ 2)
-    at7 = 3 + 3 * (x ^ 3)
-    up_ref[7] = all_ref[at7]
-    down_ref[7] = all_ref[at7]
-    side_ref[0] = all_ref[jnp.where(z % 2 == 1, at1, jnp.where(z == 4, at7, at3))]
-    side_ref[1] = all_ref[jnp.where(z % 2 == 0, at1, jnp.where(z == 3, at7, at3))]
+        all_ref[4 + e] = ref[...]
+    up_ref[7] = b7_ref[...]
+    down_ref[7] = b7_ref[...]
+    for f in range(3):
+        side1, side3, side7 = b1_ref[1, f], b3_ref[1, f], b7_ref[f]
+        side_ref[0, f] = jnp.where(z % 2 == 1, side1, jnp.where(z == 4, side7, side3))
+        side_ref[1, f] = jnp.where(z % 2 == 0, side1, jnp.where(z == 3, side7, side3))
     for p in range(8):
         far = z ^ p
-        holder = jnp.where(far > 4, far - 5, far - 1)
-        slot = jnp.where(far > 4, 2, 0)
-        source = jnp.where(far == 0, 0, 1 + 3 * (x ^ (holder & 3)) + slot)
+        source = jnp.where(far < 4, far, 4 + ((far & 3) ^ x))
         triple = all_ref[source]
         mid_ref[p] = triple
         if p > 0:
@@ -488,24 +477,25 @@
 
 def on_device(right_side, cotangent, texture, labels, coef_table):
     with jax.named_scope("fine_halo"):
-        row_lo = shift(coef_table, "grp", 1)
-        row_hi = shift(coef_table, "grp", -1)
-        up, down = call(
-            pack_kernel, [(10,) + PLANE] * 2, [], right_side, cotangent, texture, labels
-        )
+        up, down = call(pack_kernel, [(6,) + PLANE] * 2, [], right_side, cotangent)
         lo = shift(up, GD, 1)
         hi = shift(down, GD, -1)
     with jax.named_scope("coef_rows"):
-        rows = jnp.concatenate([row_lo, coef_table, row_hi], axis=0)
-        sent = jnp.broadcast_to(rows[None], (32, 3, 2))
+        sent = jnp.broadcast_to(coef_table[None], (32, 1, 2))
         got = lax.all_to_all(sent, "dev", 0, 0)
-        coef = jnp.pad(jnp.transpose(got, (1, 0, 2)).reshape(3, 64), ((0, 0), (0, 64)))
+        coef = jnp.pad(got.reshape(1, 64), ((0, 0), (0, 64)))
+    with jax.named_scope("kappa_halo"):
+        kappa_own, up, down = call(
+            kappa_kernel, [(4,) + PLANE, (3,) + PLANE, (3,) + PLANE], [], texture, labels, coef
+        )
+        k_lo = shift(up, GD, 1)
+        k_hi = shift(down, GD, -1)
     with jax.named_scope("fine"):
         kappa, one, two, to1, to3 = call(
             fine_kernel,
             [(6,) + PLANE, (4,) + TRIPLE, TRIPLE, (2,) + TRIPLE, (2,) + TRIPLE],
-            [(10,) + PLANE],
-            right_side, cotangent, texture, labels, lo, hi, coef,
+            [],
+            right_side, cotangent, kappa_own, lo, hi, k_lo, k_hi,
         )
     with jax.named_scope("block_gather"):
         mates = [swap(sent, "dev", mask) for sent, mask in ((to1, 1), (two, 2), (to3, 3))]
@@ -518,24 +508,25 @@
         blo = shift(up, GD, 4)
         bhi = shift(down, GD, -4)
     with jax.named_scope("block"):
-        two_own, three, near_sent, far_sent, one_lo, one_hi = call(
+        two_own, three, four, to1, to3, to7, one_lo, one_hi = call(
             block_kernel,
-            [(5,) + TRIPLE, (4,) + TRIPLE, (2,) + TRIPLE, TRIPLE, TRIPLE, TRIPLE],
-            [(10,) + TRIPLE, TRIPLE],
+            [(5,) + TRIPLE, (4,) + TRIPLE, TRIPLE, (2,) + TRIPLE, (2,) + TRIPLE]
+            + [TRIPLE, TRIPLE, TRIPLE],
+            [(10,) + TRIPLE],
             mid, blo, bhi, side,
         )
     with jax.named_scope("group_gather"):
-        near_mask = (4, 8, 12, 16)
-        far_mask = (20, 24, 28, 28)
-        near = lax.ppermute(near_sent, "dev", [(i, i ^ near_mask[i % 4]) for i in range(32)])
-        far = lax.ppermute(far_sent, "dev", [(i, i ^ far_mask[i % 4]) for i in range(32)])
-        pair = jnp.concatenate([near, far[None]])
-        pairs = [pair] + [swap(pair, "dev", mask) for mask in (1, 2, 3)]
+        far = lax.ppermute(four, "dev", [(i, i ^ (16 + 4 * (i % 4))) for i in range(32)])
+        direct = [swap(sent, "dev", mask) for sent, mask in ((to1, 4), (four, 8), (to3, 12))]
+        direct.append(
+            lax.ppermute(to7, "dev", [(i, i ^ 28) for i in range(32) if i // 4 in (0, 3, 4, 7)])
+        )
+        fars = [far] + [swap(far, "dev", mask) for mask in (1, 2, 3)]
         mid, up, down, side = call(
             order8_kernel,
             [(8,) + TRIPLE, (8,) + TRIPLE, (8,) + TRIPLE, (2,) + TRIPLE],
-            [(13,) + TRIPLE],
-            near_sent, *pairs,
+            [(8,) + TRIPLE],
+            four, *direct, *fars,
         )
         glo = shift(up, "grp", 1)
         ghi = shift(down, "grp", -1)

time: 182 us -> 176 us (0.967)
  starting transfers between devices: 56.6 us -> 73.1 us
  blocking collectives: 27.9 us -> 11.6 us
  waiting for transfers between devices: 50.6 us -> 44.4 us
    all_to_all x1 -> x0, blocking collectives: 14.5 us -> none  [on_device(): got = lax.all_to_all(sent, 'dev', 0, 0)]
    ppermute x10 -> x13, waiting for transfers between devices: 28.2 us -> 15.4 us  [swap(): lax.ppermute(block, axis, [(i, i ^ mask) for i in range(lax.axis_size(axi...]
    ppermute x2, starting transfers between devices: 2.6 us -> 11.9 us  [the longest x1 10 us: on_device(): lax.ppermute(four, 'dev', [(i, i ^ 16 + 4 * (i % 4)) for i in range(32)])]
    all_to_all x0 -> x1, waiting for transfers between devices: none -> 7.77 us  [on_device(): got = lax.all_to_all(sent, 'dev', 0, 0)]
    all_to_all x0 -> x1, starting transfers between devices: none -> 5.15 us  [on_device(): got = lax.all_to_all(sent, 'dev', 0, 0)]
    ppermute x8, starting transfers between devices: 31.1 us -> 35.6 us  [shift(): return lax.ppermute(block, axes, route)]
    ppermute x10 -> x13, starting transfers between devices: 22.9 us -> 20.3 us  [swap(): lax.ppermute(block, axis, [(i, i ^ mask) for i in range(lax.axis_size(axi...]
    ppermute x2, waiting for transfers between devices: 5.14 us -> 3.23 us  [the longest x1 3.23 us: on_device(): lax.ppermute(four, 'dev', [(i, i ^ 16 + 4 * (i % 4)) for i in range(32)])]
  transfers between devices with their start and end apart: 20 -> 24, of which waited for: 13 -> 15; matrix products, arithmetic and copies ran while one was open for 1% -> 2% of each run, Pallas kernels for 0% -> 1%
where the time goes in v3:
time: 176 us
  starting transfers between devices  73.1 us (42%)
  waiting for transfers between devices  44.4 us (25%)
  Pallas kernels  34.8 us (20%)
  blocking collectives  11.6 us (7%)
  local copies, waits for them, and re-layouts  9.58 us (5%)
    ppermute x8, starting transfers between devices, shift(): return lax.ppermute(block, axes, route)  35.6 us
    pallas_call x8, Pallas kernels, call(): pl.pallas_call(kernel, out_shape=[jax.ShapeDtypeStruct(shape, F32) for sh...  34.8 us
    ppermute x13, starting transfers between devices, swap(): lax.ppermute(block, axis, [(i, i ^ mask) for i in range(lax.axis_size(axi...  20.3 us
    ppermute x8, waiting for transfers between devices, shift(): return lax.ppermute(block, axes, route)  18 us
    ppermute x13, waiting for transfers between devices, swap(): lax.ppermute(block, axis, [(i, i ^ mask) for i in range(lax.axis_size(axi...  15.4 us
    all_to_all x1, blocking collectives, on_device(): parts = lax.all_to_all(sums[0, :64].reshape(32, 2), 'dev', 0, 0)  11.6 us
    ppermute x1, starting transfers between devices, on_device(): lax.ppermute(four, 'dev', [(i, i ^ 16 + 4 * (i % 4)) for i in range(32)])  10 us
    all_to_all x1, waiting for transfers between devices, on_device(): got = lax.all_to_all(sent, 'dev', 0, 0)  7.77 us
  transfers between devices with their start and end apart: 24, of which 15 were waited for; matrix products, arithmetic and copies ran while one was open for 2% of the time, Pallas kernels for 1%

profile of v3, /device:TPU:1, one launch (start us, length us, event | category | flops | bytes accessed | tf_op | source)
XLA Modules:
  0.0 175.6 jit_solution(1189899197789835124)
XLA Ops:
  2.4 3.9 %collective-permute-start = (f32[6,32,256]{2,1,0:T(8,128)}, f32[6,32,256]{2,1,0:T(8,128)S(1)}, u32[]{:S(2)}, u32[]{:S(2)}) collective-permute-start(f32[6,32,256]{2,1,0:T(8,128)} %get-tuple-element.38), channel_id=1, source_target_pairs={{0,1},{1,2},{2,3},{3,4},{4,5},{5,6},{6,7},{7,8},{8,9},{9,10},{10,1... | collective-permute-start | bytes 589832 | tf_op jit(solution)/shard_map/fine_halo/ppermute | solution.py:110
  6.3 9.0 %collective-permute-start.1 = (f32[6,32,256]{2,1,0:T(8,128)}, f32[6,32,256]{2,1,0:T(8,128)S(1)}, u32[]{:S(2)}, u32[]{:S(2)}) collective-permute-start(f32[6,32,256]{2,1,0:T(8,128)} %get-tuple-element.39), channel_id=1, source_target_pairs={{1,0},{2,1},{3,2},{4,3},{5,4},{6,5},{7,6},{8,7},{9,8},{10,9},{11,1... | collective-permute-start | bytes 589832 | tf_op jit(solution)/shard_map/fine_halo/ppermute | solution.py:110
  16.0 5.2 %all-to-all-start = ((f32[32,1,2]{2,1,0:T(1,128)}), f32[32,1,2]{2,1,0:T(1,128)S(1)}, u32[]{:S(2)}, u32[]{:S(2)}) async-start(f32[32,1,2]{2,1,0:T(1,128)} %broadcast_in_dim.12), calls=%async_computation | async-start | bytes 32768 | tf_op jit(solution)/shard_map/coef_rows/all_to_all | solution.py:485
  21.9 7.8 %all-to-all-done = f32[32,1,2]{2,1,0:T(1,128)S(1)} async-done(((f32[32,1,2]{2,1,0:T(1,128)}), f32[32,1,2]{2,1,0:T(1,128)S(1)}, u32[]{:S(2)}, u32[]{:S(2)}) %all-to-all-start) | async-done | bytes 288 | tf_op jit(solution)/shard_map/coef_rows/all_to_all | solution.py:485
  35.8 6.7 %collective-permute-start.3 = (f32[3,32,256]{2,1,0:T(8,128)}, f32[3,32,256]{2,1,0:T(8,128)S(1)}, u32[]{:S(2)}, u32[]{:S(2)}) collective-permute-start(f32[3,32,256]{2,1,0:T(8,128)} %get-tuple-element.42), channel_id=1, source_target_pairs={{1,0},{2,1},{3,2},{4,3},{5,4},{6,5},{7,6},{8,7},{9,8},{10,9},{11,1... | collective-permute-start | bytes 294920 | tf_op jit(solution)/shard_map/kappa_halo/ppermute | solution.py:110
  45.3 3.6 %fine.1 = (f32[6,32,256]{2,1,0:T(8,128)}, f32[4,3,32,256]{3,2,1,0:T(8,128)}, f32[3,32,256]{2,1,0:T(8,128)}, f32[2,3,32,256]{3,2,1,0:T(8,128)}, f32[2,3,32,256]{3,2,1,0:T(8,128)}) custom-call(f32[4,32,256]{2,1,0:T(8,128)} %s_ref.5, f32[4,32,256]{2,1,0:T(8,128)} %c_ref.5, f32[4,32,256]{2,1,0:T(8,128)} %get-tuple-element.40.own_ref, f32[6,32,256]{2,1,0:T(8,128)} %copy-done.1, ...), custom_call_target="tpu_custom_call" | custom-call | tf_op jit(solution)/shard_map/fine/pallas_call | solution.py:119
  52.1 3.7 %collective-permute-done.5.a2_ref = f32[3,32,256]{2,1,0:T(8,128)S(1)} collective-permute-done((f32[3,32,256]{2,1,0:T(8,128)}, f32[3,32,256]{2,1,0:T(8,128)S(1)}, u32[]{:S(2)}, u32[]{:S(2)}) %collective-permute-start.5) | collective-permute-done | bytes 98336 | tf_op jit(solution)/shard_map/block_gather/ppermute | solution.py:114
  57.2 2.3 %block_gather.1 = (f32[4,3,32,256]{3,2,1,0:T(8,128)}, f32[4,3,32,256]{3,2,1,0:T(8,128)}, f32[4,3,32,256]{3,2,1,0:T(8,128)}, f32[2,3,32,256]{3,2,1,0:T(8,128)}) custom-call(f32[3,32,256]{2,1,0:T(8,128)} %get-tuple-element.45.a0_ref, f32[2,3,32,256]{3,2,1,0:T(8,128)} %copy-done.8, f32[3,32,256]{2,1,0:T(8,128)} %copy-done.18, f32[2,3,32,256]{3,2,1,0:T(8,128)} %copy-done.9), custom_call_target="tpu_custom_call" | custom-call | tf_op jit(solution)/shard_map/block_gather/pallas_call | solution.py:119
  61.8 7.2 %collective-permute-start.8 = (f32[4,3,32,256]{3,2,1,0:T(8,128)}, f32[4,3,32,256]{3,2,1,0:T(8,128)S(1)}, u32[]{:S(2)}, u32[]{:S(2)}) collective-permute-start(f32[4,3,32,256]{3,2,1,0:T(8,128)} %get-tuple-element.50), channel_id=1, source_target_pairs={{4,0},{5,1},{6,2},{7,3},{8,4},{9,5},{10,6},{11,7},{12,8},{13,9},{1... | collective-permute-start | bytes 1179656 | tf_op jit(solution)/shard_map/block_gather/ppermute | solution.py:110
  69.0 4.9 %collective-permute-done.7.lo_ref = f32[4,3,32,256]{3,2,1,0:T(8,128)S(1)} collective-permute-done((f32[4,3,32,256]{3,2,1,0:T(8,128)}, f32[4,3,32,256]{3,2,1,0:T(8,128)S(1)}, u32[]{:S(2)}, u32[]{:S(2)}) %collective-permute-start.7) | collective-permute-done | bytes 393248 | tf_op jit(solution)/shard_map/block_gather/ppermute | solution.py:110
  74.8 3.7 %block.1 = (f32[5,3,32,256]{3,2,1,0:T(8,128)}, f32[4,3,32,256]{3,2,1,0:T(8,128)}, f32[3,32,256]{2,1,0:T(8,128)}, f32[2,3,32,256]{3,2,1,0:T(8,128)}, f32[2,3,32,2...) custom-call(f32[4,3,32,256]{3,2,1,0:T(8,128)} %get-tuple-element.48.mid_ref, ...), custom_call_target="tpu_custom_call" | custom-call | tf_op jit(solution)/shard_map/block/pallas_call | solution.py:119
  78.6 10.0 %collective-permute-start.13 = (f32[3,32,256]{2,1,0:T(8,128)}, f32[3,32,256]{2,1,0:T(8,128)S(1)}, u32[]{:S(2)}, u32[]{:S(2)}) collective-permute-start(f32[3,32,256]{2,1,0:T(8,128)} %get-tuple-element.56.own_ref), channel_id=1, source_target_pairs={{0,16},{1,21},{2,26},{3,31},{4,20},{5,17},{6,30},{7,27},{8,24},{9,... | collective-permute-start | bytes 294920 | tf_op jit(solution)/shard_map/group_gather/ppermute | solution.py:519
  92.4 3.2 %collective-permute-done.13.a0_ref = f32[3,32,256]{2,1,0:T(8,128)S(1)} collective-permute-done((f32[3,32,256]{2,1,0:T(8,128)}, f32[3,32,256]{2,1,0:T(8,128)S(1)}, u32[]{:S(2)}, u32[]{:S(2)}) %collective-permute-start.13) | collective-permute-done | bytes 98336 | tf_op jit(solution)/shard_map/group_gather/ppermute | solution.py:519
  95.6 9.0 %collective-permute-start.14 = (f32[3,32,256]{2,1,0:T(8,128)S(1)}, f32[3,32,256]{2,1,0:T(8,128)S(1)}, u32[]{:S(2)}, u32[]{:S(2)}) collective-permute-start(f32[3,32,256]{2,1,0:T(8,128)S(1)} %collective-permute-done.13.a0_ref), channel_id=1, source_target_pairs={{0,1},{1,0},{2,3},{3,2},{4,5},{5,4},{6,7},{7,6},{8,9},{9,8},{10,11... | collective-permute-start | bytes 294920 | tf_op jit(solution)/shard_map/group_gather/ppermute | solution.py:114
  104.7 2.5 %collective-permute-start.16 = (f32[3,32,256]{2,1,0:T(8,128)S(1)}, f32[3,32,256]{2,1,0:T(8,128)S(1)}, u32[]{:S(2)}, u32[]{:S(2)}) collective-permute-start(f32[3,32,256]{2,1,0:T(8,128)S(1)} %collective-permute-done.13.a0_ref), channel_id=1, source_target_pairs={{0,3},{1,2},{2,1},{3,0},{4,7},{5,6},{6,5},{7,4},{8,11},{9,10},{10,... | collective-permute-start | bytes 294920 | tf_op jit(solution)/shard_map/group_gather/ppermute | solution.py:114
  107.2 2.5 %collective-permute-done.15.a2_ref = f32[3,32,256]{2,1,0:T(8,128)S(1)} collective-permute-done((f32[3,32,256]{2,1,0:T(8,128)S(1)}, f32[3,32,256]{2,1,0:T(8,128)S(1)}, u32[]{:S(2)}, u32[]{:S(2)}) %collective-permute-start.15) | collective-permute-done | bytes 98336 | tf_op jit(solution)/shard_map/group_gather/ppermute | solution.py:114
  111.2 3.0 %group_gather.1 = (f32[8,3,32,256]{3,2,1,0:T(8,128)}, f32[8,3,32,256]{3,2,1,0:T(8,128)}, f32[8,3,32,256]{3,2,1,0:T(8,128)}, f32[2,3,32,256]{3,2,1,0:T(8,128)}) custom-call(f32[3,32,256]{2,1,0:T(8,128)} %get-tuple-element.56.own_ref, f32[2,3,32,256]{3,2,1,0:T(8,128)} %copy-done.10, f32[3,32,256]{2,1,0:T(8,128)} %copy-done.12, f32[2,3,32,256]{3,2,1,0:T(8,128)} %copy-done.11, ...), custom_call_target="tpu_custom_call" | custom-call | tf_op jit(solution)/shard_map/group_gather/pallas_call | solution.py:119
  116.1 2.5 %collective-permute-start.18 = (f32[8,3,32,256]{3,2,1,0:T(8,128)}, f32[8,3,32,256]{3,2,1,0:T(8,128)S(1)}, u32[]{:S(2)}, u32[]{:S(2)}) collective-permute-start(f32[8,3,32,256]{3,2,1,0:T(8,128)} %get-tuple-element.62), channel_id=1, source_target_pairs={{32,0},{64,32},{96,64},{128,96},{160,128},{192,160},{224,192},{33,... | collective-permute-start | bytes 2359304 | tf_op jit(solution)/shard_map/group_gather/ppermute | solution.py:110
  118.6 6.7 %collective-permute-done.17.lo_ref = f32[8,3,32,256]{3,2,1,0:T(8,128)S(1)} collective-permute-done((f32[8,3,32,256]{3,2,1,0:T(8,128)}, f32[8,3,32,256]{3,2,1,0:T(8,128)S(1)}, u32[]{:S(2)}, u32[]{:S(2)}) %collective-permute-start.17) | collective-permute-done | bytes 786464 | tf_op jit(solution)/shard_map/group_gather/ppermute | solution.py:110
  125.3 4.3 %collective-permute-done.18.hi_ref = f32[8,3,32,256]{3,2,1,0:T(8,128)S(1)} collective-permute-done((f32[8,3,32,256]{3,2,1,0:T(8,128)}, f32[8,3,32,256]{3,2,1,0:T(8,128)S(1)}, u32[]{:S(2)}, u32[]{:S(2)}) %collective-permute-start.18) | collective-permute-done | bytes 786464 | tf_op jit(solution)/shard_map/group_gather/ppermute | solution.py:110
  130.5 6.8 %group.1 = (f32[5,3,32,256]{3,2,1,0:T(8,128)}, f32[5,3,32,256]{3,2,1,0:T(8,128)}, f32[4,3,32,256]{3,2,1,0:T(8,128)}, f32[3,32,256]{2,1,0:T(8,128)}, f32[2,3,32,2...) custom-call(f32[8,3,32,256]{3,2,1,0:T(8,128)} %get-tuple-element.60.mid_ref, ...), custom_call_target="tpu_custom_call" | custom-call | tf_op jit(solution)/shard_map/group/pallas_call | solution.py:119
  145.0 3.3 %collective-permute-done.21 = f32[2,3,32,256]{3,2,1,0:T(8,128)S(1)} collective-permute-done((f32[2,3,32,256]{3,2,1,0:T(8,128)}, f32[2,3,32,256]{3,2,1,0:T(8,128)S(1)}, u32[]{:S(2)}, u32[]{:S(2)}) %collective-permute-start.21) | collective-permute-done | bytes 196640 | tf_op jit(solution)/shard_map/coarse_gather/ppermute | solution.py:114
  151.3 11.5 %up.1 = (f32[4,32,256]{2,1,0:T(8,128)}, f32[1,128]{1,0:T(1,128)}) custom-call(f32[4,32,256]{2,1,0:T(8,128)} %s_ref.5, f32[4,32,256]{2,1,0:T(8,128)} %c_ref.5, f32[4,32,256]{2,1,0:T(8,128)} %tex_ref.3, s32[4,32,2]{2,1,0:T(8,128)} %copy.12.lab_ref, f32[6,32,256]{2,1,0:T(8,128)} %copy-done.1, f32[6,32,256]{2,1,0:T(8,128)} %copy-done.2, ...), custom_call_target="tpu_custom_call" | custom-call | tf_op jit(solution)/shard_map/up/pallas_call | solution.py:119
  163.5 11.6 %all_to_all.14 = f32[32,1,2]{2,1,0:T(1,128)S(1)} all-to-all(f32[32,1,2]{2,1,0:T(1,128)S(1)} %bitcast.9), channel_id=1, replica_groups=mesh['grp'=8,'dev'=32] {'dev'}, dimensions={0} | all-to-all | bytes 512 | tf_op jit(solution)/shard_map/table/all_to_all | solution.py:559
  (98 shorter events, 39.7 us)
Async XLA Ops:
  2.4 42.1 %collective-permute-start = (f32[6,32,256]{2,1,0:T(8,128)}, f32[6,32,256]{2,1,0:T(8,128)S(1)}, u32[]{:S(2)}, u32[]{:S(2)}) collective-permute-start(f32[6,32,256]{2,1,0:T(8,128)} %get-tuple-element.38), channel_id=1, source_target_pairs={{0,1},{1,2},{2,3},{3,4},{4,5},{5,6},{6,7},{7,8},{8,9},{9,10},{10,1... | collective-permute-start | bytes 589832 | tf_op jit(solution)/shard_map/fine_halo/ppermute | solution.py:110
  6.3 38.2 %collective-permute-start.1 = (f32[6,32,256]{2,1,0:T(8,128)}, f32[6,32,256]{2,1,0:T(8,128)S(1)}, u32[]{:S(2)}, u32[]{:S(2)}) collective-permute-start(f32[6,32,256]{2,1,0:T(8,128)} %get-tuple-element.39), channel_id=1, source_target_pairs={{1,0},{2,1},{3,2},{4,3},{5,4},{6,5},{7,6},{8,7},{9,8},{10,9},{11,1... | collective-permute-start | bytes 589832 | tf_op jit(solution)/shard_map/fine_halo/ppermute | solution.py:110
  16.0 13.7 %all-to-all-start = ((f32[32,1,2]{2,1,0:T(1,128)}), f32[32,1,2]{2,1,0:T(1,128)S(1)}, u32[]{:S(2)}, u32[]{:S(2)}) async-start(f32[32,1,2]{2,1,0:T(1,128)} %broadcast_in_dim.12), calls=%async_computation | async-start | bytes 32768 | tf_op jit(solution)/shard_map/coef_rows/all_to_all | solution.py:485
  33.6 9.5 %collective-permute-start.2 = (f32[3,32,256]{2,1,0:T(8,128)}, f32[3,32,256]{2,1,0:T(8,128)S(1)}, u32[]{:S(2)}, u32[]{:S(2)}) collective-permute-start(f32[3,32,256]{2,1,0:T(8,128)} %get-tuple-element.41), channel_id=1, source_target_pairs={{0,1},{1,2},{2,3},{3,4},{4,5},{5,6},{6,7},{7,8},{8,9},{9,10},{10,1... | collective-permute-start | bytes 294920 | tf_op jit(solution)/shard_map/kappa_halo/ppermute | solution.py:110
  35.8 8.6 %collective-permute-start.3 = (f32[3,32,256]{2,1,0:T(8,128)}, f32[3,32,256]{2,1,0:T(8,128)S(1)}, u32[]{:S(2)}, u32[]{:S(2)}) collective-permute-start(f32[3,32,256]{2,1,0:T(8,128)} %get-tuple-element.42), channel_id=1, source_target_pairs={{1,0},{2,1},{3,2},{4,3},{5,4},{6,5},{7,6},{8,7},{9,8},{10,9},{11,1... | collective-permute-start | bytes 294920 | tf_op jit(solution)/shard_map/kappa_halo/ppermute | solution.py:110
  48.8 7.0 %collective-permute-start.4 = (f32[2,3,32,256]{3,2,1,0:T(8,128)}, f32[2,3,32,256]{3,2,1,0:T(8,128)S(1)}, u32[]{:S(2)}, u32[]{:S(2)}) collective-permute-start(f32[2,3,32,256]{3,2,1,0:T(8,128)} %get-tuple-element.46), channel_id=1, source_target_pairs={{0,1},{1,0},{2,3},{3,2},{4,5},{5,4},{6,7},{7,6},{8,9},{9,8},{10,11... | collective-permute-start | bytes 589832 | tf_op jit(solution)/shard_map/block_gather/ppermute | solution.py:114
  48.9 7.0 %collective-permute-start.6 = (f32[2,3,32,256]{3,2,1,0:T(8,128)}, f32[2,3,32,256]{3,2,1,0:T(8,128)S(1)}, u32[]{:S(2)}, u32[]{:S(2)}) collective-permute-start(f32[2,3,32,256]{3,2,1,0:T(8,128)} %get-tuple-element.47), channel_id=1, source_target_pairs={{0,3},{1,2},{2,1},{3,0},{4,7},{5,6},{6,5},{7,4},{8,11},{9,10},{10,... | collective-permute-start | bytes 589832 | tf_op jit(solution)/shard_map/block_gather/ppermute | solution.py:114
  50.3 5.5 %collective-permute-start.5 = (f32[3,32,256]{2,1,0:T(8,128)}, f32[3,32,256]{2,1,0:T(8,128)S(1)}, u32[]{:S(2)}, u32[]{:S(2)}) collective-permute-start(f32[3,32,256]{2,1,0:T(8,128)} %get-tuple-element.45.a0_ref), channel_id=1, source_target_pairs={{0,2},{1,3},{2,0},{3,1},{4,6},{5,7},{6,4},{7,5},{8,10},{9,11},{10,... | collective-permute-start | bytes 294920 | tf_op jit(solution)/shard_map/block_gather/ppermute | solution.py:114
  59.5 14.4 %collective-permute-start.7 = (f32[4,3,32,256]{3,2,1,0:T(8,128)}, f32[4,3,32,256]{3,2,1,0:T(8,128)S(1)}, u32[]{:S(2)}, u32[]{:S(2)}) collective-permute-start(f32[4,3,32,256]{3,2,1,0:T(8,128)} %get-tuple-element.49), channel_id=1, source_target_pairs={{0,4},{1,5},{2,6},{3,7},{4,8},{5,9},{6,10},{7,11},{8,12},{9,13},{1... | collective-permute-start | bytes 1179656 | tf_op jit(solution)/shard_map/block_gather/ppermute | solution.py:110
  61.8 12.2 %collective-permute-start.8 = (f32[4,3,32,256]{3,2,1,0:T(8,128)}, f32[4,3,32,256]{3,2,1,0:T(8,128)S(1)}, u32[]{:S(2)}, u32[]{:S(2)}) collective-permute-start(f32[4,3,32,256]{3,2,1,0:T(8,128)} %get-tuple-element.50), channel_id=1, source_target_pairs={{4,0},{5,1},{6,2},{7,3},{8,4},{9,5},{10,6},{11,7},{12,8},{13,9},{1... | collective-permute-start | bytes 1179656 | tf_op jit(solution)/shard_map/block_gather/ppermute | solution.py:110
  78.6 26.1 %collective-permute-start.10 = (f32[3,32,256]{2,1,0:T(8,128)}, f32[3,32,256]{2,1,0:T(8,128)S(1)}, u32[]{:S(2)}, u32[]{:S(2)}) collective-permute-start(f32[3,32,256]{2,1,0:T(8,128)} %get-tuple-element.56.own_ref), channel_id=1, source_target_pairs={{0,8},{1,9},{2,10},{3,11},{4,12},{5,13},{6,14},{7,15},{8,0},{9,1},... | collective-permute-start | bytes 294920 | tf_op jit(solution)/shard_map/group_gather/ppermute | solution.py:114
  78.6 17.1 %collective-permute-start.13 = (f32[3,32,256]{2,1,0:T(8,128)}, f32[3,32,256]{2,1,0:T(8,128)S(1)}, u32[]{:S(2)}, u32[]{:S(2)}) collective-permute-start(f32[3,32,256]{2,1,0:T(8,128)} %get-tuple-element.56.own_ref), channel_id=1, source_target_pairs={{0,16},{1,21},{2,26},{3,31},{4,20},{5,17},{6,30},{7,27},{8,24},{9,... | collective-permute-start | bytes 294920 | tf_op jit(solution)/shard_map/group_gather/ppermute | solution.py:519
  88.6 18.5 %collective-permute-start.9 = (f32[2,3,32,256]{3,2,1,0:T(8,128)}, f32[2,3,32,256]{3,2,1,0:T(8,128)S(1)}, u32[]{:S(2)}, u32[]{:S(2)}) collective-permute-start(f32[2,3,32,256]{3,2,1,0:T(8,128)} %get-tuple-element.57), channel_id=1, source_target_pairs={{0,4},{1,5},{2,6},{3,7},{4,0},{5,1},{6,2},{7,3},{8,12},{9,13},{10,... | collective-permute-start | bytes 589832 | tf_op jit(solution)/shard_map/group_gather/ppermute | solution.py:114
  90.0 17.2 %collective-permute-start.11 = (f32[2,3,32,256]{3,2,1,0:T(8,128)}, f32[2,3,32,256]{3,2,1,0:T(8,128)S(1)}, u32[]{:S(2)}, u32[]{:S(2)}) collective-permute-start(f32[2,3,32,256]{3,2,1,0:T(8,128)} %get-tuple-element.58), channel_id=1, source_target_pairs={{0,12},{1,13},{2,14},{3,15},{4,8},{5,9},{6,10},{7,11},{8,4},{9,5},... | collective-permute-start | bytes 589832 | tf_op jit(solution)/shard_map/group_gather/ppermute | solution.py:114
  90.5 14.2 %collective-permute-start.12 = (f32[3,32,256]{2,1,0:T(8,128)}, f32[3,32,256]{2,1,0:T(8,128)S(1)}, u32[]{:S(2)}, u32[]{:S(2)}) collective-permute-start(f32[3,32,256]{2,1,0:T(8,128)} %get-tuple-element.59), channel_id=1, source_target_pairs={{0,28},{1,29},{2,30},{3,31},{12,16},{13,17},{14,18},{15,19},{16,12... | collective-permute-start | bytes 294920 | tf_op jit(solution)/shard_map/group_gather/ppermute | solution.py:522
  95.6 11.5 %collective-permute-start.14 = (f32[3,32,256]{2,1,0:T(8,128)S(1)}, f32[3,32,256]{2,1,0:T(8,128)S(1)}, u32[]{:S(2)}, u32[]{:S(2)}) collective-permute-start(f32[3,32,256]{2,1,0:T(8,128)S(1)} %collective-permute-done.13.a0_ref), channel_id=1, source_target_pairs={{0,1},{1,0},{2,3},{3,2},{4,5},{5,4},{6,7},{7,6},{8,9},{9,8},{10,11... | collective-permute-start | bytes 294920 | tf_op jit(solution)/shard_map/group_gather/ppermute | solution.py:114
  104.7 5.1 %collective-permute-start.15 = (f32[3,32,256]{2,1,0:T(8,128)S(1)}, f32[3,32,256]{2,1,0:T(8,128)S(1)}, u32[]{:S(2)}, u32[]{:S(2)}) collective-permute-start(f32[3,32,256]{2,1,0:T(8,128)S(1)} %collective-permute-done.13.a0_ref), channel_id=1, source_target_pairs={{0,2},{1,3},{2,0},{3,1},{4,6},{5,7},{6,4},{7,5},{8,10},{9,11},{10,... | collective-permute-start | bytes 294920 | tf_op jit(solution)/shard_map/group_gather/ppermute | solution.py:114
  104.7 5.8 %collective-permute-start.16 = (f32[3,32,256]{2,1,0:T(8,128)S(1)}, f32[3,32,256]{2,1,0:T(8,128)S(1)}, u32[]{:S(2)}, u32[]{:S(2)}) collective-permute-start(f32[3,32,256]{2,1,0:T(8,128)S(1)} %collective-permute-done.13.a0_ref), channel_id=1, source_target_pairs={{0,3},{1,2},{2,1},{3,0},{4,7},{5,6},{6,5},{7,4},{8,11},{9,10},{10,... | collective-permute-start | bytes 294920 | tf_op jit(solution)/shard_map/group_gather/ppermute | solution.py:114
  114.2 11.1 %collective-permute-start.17 = (f32[8,3,32,256]{3,2,1,0:T(8,128)}, f32[8,3,32,256]{3,2,1,0:T(8,128)S(1)}, u32[]{:S(2)}, u32[]{:S(2)}) collective-permute-start(f32[8,3,32,256]{3,2,1,0:T(8,128)} %get-tuple-element.61), channel_id=1, source_target_pairs={{0,32},{32,64},{64,96},{96,128},{128,160},{160,192},{192,224},{1,3... | collective-permute-start | bytes 2359304 | tf_op jit(solution)/shard_map/group_gather/ppermute | solution.py:110
  116.1 13.5 %collective-permute-start.18 = (f32[8,3,32,256]{3,2,1,0:T(8,128)}, f32[8,3,32,256]{3,2,1,0:T(8,128)S(1)}, u32[]{:S(2)}, u32[]{:S(2)}) collective-permute-start(f32[8,3,32,256]{3,2,1,0:T(8,128)} %get-tuple-element.62), channel_id=1, source_target_pairs={{32,0},{64,32},{96,64},{128,96},{160,128},{192,160},{224,192},{33,... | collective-permute-start | bytes 2359304 | tf_op jit(solution)/shard_map/group_gather/ppermute | solution.py:110
  137.3 6.3 %collective-permute-start.19 = (f32[2,3,32,256]{3,2,1,0:T(8,128)}, f32[2,3,32,256]{3,2,1,0:T(8,128)S(1)}, u32[]{:S(2)}, u32[]{:S(2)}) collective-permute-start(f32[2,3,32,256]{3,2,1,0:T(8,128)} %get-tuple-element.70), channel_id=1, source_target_pairs={{0,64},{32,96},{64,0},{96,32},{128,192},{160,224},{192,128},{224,1... | collective-permute-start | bytes 589832 | tf_op jit(solution)/shard_map/coarse_gather/ppermute | solution.py:114
  138.6 9.7 %collective-permute-start.21 = (f32[2,3,32,256]{3,2,1,0:T(8,128)}, f32[2,3,32,256]{3,2,1,0:T(8,128)S(1)}, u32[]{:S(2)}, u32[]{:S(2)}) collective-permute-start(f32[2,3,32,256]{3,2,1,0:T(8,128)} %get-tuple-element.70), channel_id=1, source_target_pairs={{0,192},{32,224},{64,128},{96,160},{128,64},{160,96},{192,0},{224,... | collective-permute-start | bytes 589832 | tf_op jit(solution)/shard_map/coarse_gather/ppermute | solution.py:114
  138.6 6.4 %collective-permute-start.20 = (f32[3,32,256]{2,1,0:T(8,128)}, f32[3,32,256]{2,1,0:T(8,128)S(1)}, u32[]{:S(2)}, u32[]{:S(2)}) collective-permute-start(f32[3,32,256]{2,1,0:T(8,128)} %get-tuple-element.69), channel_id=1, source_target_pairs={{0,128},{32,160},{64,192},{96,224},{128,0},{160,32},{192,64},{224,... | collective-permute-start | bytes 294920 | tf_op jit(solution)/shard_map/coarse_gather/ppermute | solution.py:114
  148.4 2.1 %collective-permute-start.22 = (f32[6,3,32,256]{3,2,1,0:T(8,128)S(1)}, f32[6,3,32,256]{3,2,1,0:T(8,128)S(1)}, u32[]{:S(2)}, u32[]{:S(2)}) collective-permute-start(f32[6,3,32,256]{3,2,1,0:T(8,128)S(1)} %fusion.near_ref), channel_id=1, source_target_pairs={{0,32},{32,0},{64,96},{96,64},{128,160},{160,128},{192,224},{224,1... | collective-permute-start | bytes 1769480 | tf_op jit(solution)/shard_map/coarse_gather/ppermute | solution.py:114
  (25 other events, 71.5 us)

commit v4 on v2

--- a/solution.py
+++ b/solution.py
@@ -212,7 +212,7 @@
 
 def block_kernel(
     mid_ref, lo_ref, hi_ref, side_ref,
-    own_ref, three_ref, near_ref, far_ref, one_lo_ref, one_hi_ref, all_ref, four_ref,
+    own_ref, three_ref, four_ref, to1_ref, to3_ref, to7_ref, one_lo_ref, one_hi_ref, all_ref,
 ):
     g, z, x = place()
     grid = Grid()
@@ -239,32 +239,33 @@
         )
     two_levels(grid, get, lo_ok, hi_ok, three_ref, four_ref)
     odd = z % 2
-    near_ref[0] = four_ref[...]
-    near_ref[1] = three_ref[jnp.where(x == 0, 1 + odd, 2 - odd)]
-    edge = three_ref[2 - odd]
-    far_ref[...] = jnp.where(x == 3, edge, four_ref[...])
+    to1_ref[0] = four_ref[...]
+    to3_ref[0] = four_ref[...]
+    to1_ref[1] = three_ref[1 + odd]
+    to3_ref[1] = three_ref[2 - odd]
+    to7_ref[...] = three_ref[2 - odd]
 
 
 def order8_kernel(
-    own_ref, a0_ref, a1_ref, a2_ref, a3_ref, mid_ref, up_ref, down_ref, side_ref, all_ref
+    own_ref, b1_ref, b2_ref, b3_ref, b7_ref, a0_ref, a1_ref, a2_ref, a3_ref,
+    mid_ref, up_ref, down_ref, side_ref, all_ref,
 ):
     g, z, x = place()
-    all_ref[0] = own_ref[0]
+    all_ref[0] = own_ref[...]
+    all_ref[1] = b1_ref[0]
+    all_ref[2] = b2_ref[...]
+    all_ref[3] = b3_ref[0]
     for e, ref in enumerate((a0_ref, a1_ref, a2_ref, a3_ref)):
-        for slot in range(3):
-            all_ref[1 + 3 * e + slot] = ref[slot]
-    at1 = 2 + 3 * x
-    at3 = 2 + 3 * (x ^ 2)
-    at7 = 3 + 3 * (x ^ 3)
-    up_ref[7] = all_ref[at7]
-    down_ref[7] = all_ref[at7]
-    side_ref[0] = all_ref[jnp.where(z % 2 == 1, at1, jnp.where(z == 4, at7, at3))]
-    side_ref[1] = all_ref[jnp.where(z % 2 == 0, at1, jnp.where(z == 3, at7, at3))]
+        all_ref[4 + e] = ref[...]
+    up_ref[7] = b7_ref[...]
+    down_ref[7] = b7_ref[...]
+    for f in range(3):
+        side1, side3, side7 = b1_ref[1, f], b3_ref[1, f], b7_ref[f]
+        side_ref[0, f] = jnp.where(z % 2 == 1, side1, jnp.where(z == 4, side7, side3))
+        side_ref[1, f] = jnp.where(z % 2 == 0, side1, jnp.where(z == 3, side7, side3))
     for p in range(8):
         far = z ^ p
-        holder = jnp.where(far > 4, far - 5, far - 1)
-        slot = jnp.where(far > 4, 2, 0)
-        source = jnp.where(far == 0, 0, 1 + 3 * (x ^ (holder & 3)) + slot)
+        source = jnp.where(far < 4, far, 4 + ((far & 3) ^ x))
         triple = all_ref[source]
         mid_ref[p] = triple
         if p > 0:
@@ -493,6 +494,7 @@
         up, down = call(
             pack_kernel, [(10,) + PLANE] * 2, [], right_side, cotangent, texture, labels
         )
+        up, down, row_lo, row_hi = lax.optimization_barrier((up, down, row_lo, row_hi))
         lo = shift(up, GD, 1)
         hi = shift(down, GD, -1)
     with jax.named_scope("coef_rows"):
@@ -518,24 +520,25 @@
         blo = shift(up, GD, 4)
         bhi = shift(down, GD, -4)
     with jax.named_scope("block"):
-        two_own, three, near_sent, far_sent, one_lo, one_hi = call(
+        two_own, three, four, to1, to3, to7, one_lo, one_hi = call(
             block_kernel,
-            [(5,) + TRIPLE, (4,) + TRIPLE, (2,) + TRIPLE, TRIPLE, TRIPLE, TRIPLE],
-            [(10,) + TRIPLE, TRIPLE],
+            [(5,) + TRIPLE, (4,) + TRIPLE, TRIPLE, (2,) + TRIPLE, (2,) + TRIPLE]
+            + [TRIPLE, TRIPLE, TRIPLE],
+            [(10,) + TRIPLE],
             mid, blo, bhi, side,
         )
     with jax.named_scope("group_gather"):
-        near_mask = (4, 8, 12, 16)
-        far_mask = (20, 24, 28, 28)
-        near = lax.ppermute(near_sent, "dev", [(i, i ^ near_mask[i % 4]) for i in range(32)])
-        far = lax.ppermute(far_sent, "dev", [(i, i ^ far_mask[i % 4]) for i in range(32)])
-        pair = jnp.concatenate([near, far[None]])
-        pairs = [pair] + [swap(pair, "dev", mask) for mask in (1, 2, 3)]
+        far = lax.ppermute(four, "dev", [(i, i ^ (16 + 4 * (i % 4))) for i in range(32)])
+        direct = [swap(sent, "dev", mask) for sent, mask in ((to1, 4), (four, 8), (to3, 12))]
+        direct.append(
+            lax.ppermute(to7, "dev", [(i, i ^ 28) for i in range(32) if i // 4 in (0, 3, 4, 7)])
+        )
+        fars = [far] + [swap(far, "dev", mask) for mask in (1, 2, 3)]
         mid, up, down, side = call(
             order8_kernel,
             [(8,) + TRIPLE, (8,) + TRIPLE, (8,) + TRIPLE, (2,) + TRIPLE],
-            [(13,) + TRIPLE],
-            near_sent, *pairs,
+            [(8,) + TRIPLE],
+            four, *direct, *fars,
         )
         glo = shift(up, "grp", 1)
         ghi = shift(down, "grp", -1)

time: 182 us -> 169 us (0.929)
  waiting for transfers between devices: 50.6 us -> 40.7 us
  starting transfers between devices: 56.6 us -> 51.9 us
    ppermute x10 -> x13, starting transfers between devices: 22.9 us -> 14.5 us  [swap(): lax.ppermute(block, axis, [(i, i ^ mask) for i in range(lax.axis_size(axi...]
    ppermute x10 -> x13, waiting for transfers between devices: 28.2 us -> 19.9 us  [swap(): lax.ppermute(block, axis, [(i, i ^ mask) for i in range(lax.axis_size(axi...]
    ppermute x2, starting transfers between devices: 2.6 us -> 8.22 us  [the longest x1 6.05 us: on_device(): lax.ppermute(four, 'dev', [(i, i ^ 16 + 4 * (i % 4)) for i in range(32)])]
    ppermute x2, waiting for transfers between devices: 5.14 us -> 2.14 us  [the longest x1 1.16 us: on_device(): lax.ppermute(to7, 'dev', [(i, i ^ 28) for i in range(32) if i // 4 in (0,...]
    ppermute x8, starting transfers between devices: 31.1 us -> 29.2 us  [shift(): return lax.ppermute(block, axes, route)]
    unnamed x42 -> x50, local copies, waits for them, and re-layouts: 9.14 us -> 9.01 us
  transfers between devices with their start and end apart: 20 -> 23, of which waited for: 13 -> 13; matrix products, arithmetic and copies ran while one was open for 1% -> 2% of each run, Pallas kernels for 0% -> 1%
where the time goes in v4:
time: 169 us; the launch traced here: 168 us
  starting transfers between devices  51.9 us (31%)
  waiting for transfers between devices  40.7 us (24%)
  Pallas kernels  34.7 us (21%)
  blocking collectives  29.6 us (18%)
  local copies, waits for them, and re-layouts  9.91 us (6%)
    pallas_call x7, Pallas kernels, call(): pl.pallas_call(kernel, out_shape=[jax.ShapeDtypeStruct(shape, F32) for sh...  34.7 us
    ppermute x8, starting transfers between devices, shift(): return lax.ppermute(block, axes, route)  29.2 us
    ppermute x13, waiting for transfers between devices, swap(): lax.ppermute(block, axis, [(i, i ^ mask) for i in range(lax.axis_size(axi...  19.9 us
    ppermute x8, waiting for transfers between devices, shift(): return lax.ppermute(block, axes, route)  18.7 us
    all_to_all x1, blocking collectives, on_device(): got = lax.all_to_all(sent, 'dev', 0, 0)  16.1 us
    ppermute x13, starting transfers between devices, swap(): lax.ppermute(block, axis, [(i, i ^ mask) for i in range(lax.axis_size(axi...  14.5 us
    all_to_all x1, blocking collectives, on_device(): parts = lax.all_to_all(sums[0, :64].reshape(32, 2), 'dev', 0, 0)  13.5 us
    unnamed x50, local copies, waits for them, and re-layouts  9.01 us
  transfers between devices with their start and end apart: 23, of which 13 were waited for; matrix products, arithmetic and copies ran while one was open for 2% of the time, Pallas kernels for 1%

profile of v4, /device:TPU:1, one launch (start us, length us, event | category | flops | bytes accessed | tf_op | source)
XLA Modules:
  0.0 168.3 jit_solution(8075289130432784318)
XLA Ops:
  0.6 4.6 %collective-permute-start = (f32[1,2]{1,0:T(1,128)}, f32[1,2]{1,0:T(1,128)S(1)}, u32[]{:S(2)}, u32[]{:S(2)}) collective-permute-start(f32[1,2]{1,0:T(1,128)} %param.9), channel_id=1, source_target_pairs={{0,32},{32,64},{64,96},{96,128},{128,160},{160,192},{192,224},{1,3... | collective-permute-start | bytes 32 | tf_op jit(solution)/shard_map/fine_halo/ppermute | solution.py:110
  10.6 3.1 %collective-permute-start.2 = (f32[10,32,256]{2,1,0:T(8,128)}, f32[10,32,256]{2,1,0:T(8,128)S(1)}, u32[]{:S(2)}, u32[]{:S(2)}) collective-permute-start(f32[10,32,256]{2,1,0:T(8,128)} %get-tuple-element.41), channel_id=1, source_target_pairs={{0,1},{1,2},{2,3},{3,4},{4,5},{5,6},{6,7},{7,8},{8,9},{9,10},{10,1... | collective-permute-start | bytes 983048 | tf_op jit(solution)/shard_map/fine_halo/ppermute | solution.py:110
  13.7 6.4 %collective-permute-start.3 = (f32[10,32,256]{2,1,0:T(8,128)}, f32[10,32,256]{2,1,0:T(8,128)S(1)}, u32[]{:S(2)}, u32[]{:S(2)}) collective-permute-start(f32[10,32,256]{2,1,0:T(8,128)} %get-tuple-element.42), channel_id=1, source_target_pairs={{1,0},{2,1},{3,2},{4,3},{5,4},{6,5},{7,6},{8,7},{9,8},{10,9},{11,1... | collective-permute-start | bytes 983048 | tf_op jit(solution)/shard_map/fine_halo/ppermute | solution.py:110
  20.2 16.1 %all_to_all.14 = f32[32,3,2]{1,2,0:T(2,128)S(1)} all-to-all(f32[32,3,2]{1,2,0:T(2,128)S(1)} %broadcast_in_dim.4), channel_id=1, replica_groups=mesh['grp'=8,'dev'=32] {'dev'}, dimensions={0} | all-to-all | bytes 1536 | tf_op jit(solution)/shard_map/coef_rows/all_to_all | solution.py:503
  38.5 5.3 %fine.1 = (f32[6,32,256]{2,1,0:T(8,128)}, f32[4,3,32,256]{3,2,1,0:T(8,128)}, f32[3,32,256]{2,1,0:T(8,128)}, f32[2,3,32,256]{3,2,1,0:T(8,128)}, f32[2,3,32,256]{3,2,1,0:T(8,128)}) custom-call(f32[4,32,256]{2,1,0:T(8,128)} %s_ref.5, f32[4,32,256]{2,1,0:T(8,128)} %c_ref.5, f32[4,32,256]{2,1,0:T(8,128)} %tex_ref.5, s32[4,32,2]{2,1,0:T(8,128)} %copy.17.lab_ref, ...), custom_call_target="tpu_custom_call" | custom-call | tf_op jit(solution)/shard_map/fine/pallas_call | solution.py:119
  47.0 6.4 %collective-permute-done.5.a2_ref = f32[3,32,256]{2,1,0:T(8,128)S(1)} collective-permute-done((f32[3,32,256]{2,1,0:T(8,128)}, f32[3,32,256]{2,1,0:T(8,128)S(1)}, u32[]{:S(2)}, u32[]{:S(2)}) %collective-permute-start.5) | collective-permute-done | bytes 98336 | tf_op jit(solution)/shard_map/block_gather/ppermute | solution.py:114
  54.9 2.3 %block_gather.1 = (f32[4,3,32,256]{3,2,1,0:T(8,128)}, f32[4,3,32,256]{3,2,1,0:T(8,128)}, f32[4,3,32,256]{3,2,1,0:T(8,128)}, f32[2,3,32,256]{3,2,1,0:T(8,128)}) custom-call(f32[3,32,256]{2,1,0:T(8,128)} %get-tuple-element.47.a0_ref, f32[2,3,32,256]{3,2,1,0:T(8,128)} %copy-done.8, f32[3,32,256]{2,1,0:T(8,128)} %copy-done.18, f32[2,3,32,256]{3,2,1,0:T(8,128)} %copy-done.9), custom_call_target="tpu_custom_call" | custom-call | tf_op jit(solution)/shard_map/block_gather/pallas_call | solution.py:119
  57.2 2.3 %collective-permute-start.7 = (f32[4,3,32,256]{3,2,1,0:T(8,128)}, f32[4,3,32,256]{3,2,1,0:T(8,128)S(1)}, u32[]{:S(2)}, u32[]{:S(2)}) collective-permute-start(f32[4,3,32,256]{3,2,1,0:T(8,128)} %get-tuple-element.51), channel_id=1, source_target_pairs={{0,4},{1,5},{2,6},{3,7},{4,8},{5,9},{6,10},{7,11},{8,12},{9,13},{1... | collective-permute-start | bytes 1179656 | tf_op jit(solution)/shard_map/block_gather/ppermute | solution.py:110
  59.5 4.5 %collective-permute-start.8 = (f32[4,3,32,256]{3,2,1,0:T(8,128)}, f32[4,3,32,256]{3,2,1,0:T(8,128)S(1)}, u32[]{:S(2)}, u32[]{:S(2)}) collective-permute-start(f32[4,3,32,256]{3,2,1,0:T(8,128)} %get-tuple-element.52), channel_id=1, source_target_pairs={{4,0},{5,1},{6,2},{7,3},{8,4},{9,5},{10,6},{11,7},{12,8},{13,9},{1... | collective-permute-start | bytes 1179656 | tf_op jit(solution)/shard_map/block_gather/ppermute | solution.py:110
  64.0 6.3 %collective-permute-done.7.lo_ref = f32[4,3,32,256]{3,2,1,0:T(8,128)S(1)} collective-permute-done((f32[4,3,32,256]{3,2,1,0:T(8,128)}, f32[4,3,32,256]{3,2,1,0:T(8,128)S(1)}, u32[]{:S(2)}, u32[]{:S(2)}) %collective-permute-start.7) | collective-permute-done | bytes 393248 | tf_op jit(solution)/shard_map/block_gather/ppermute | solution.py:110
  71.8 3.7 %block.1 = (f32[5,3,32,256]{3,2,1,0:T(8,128)}, f32[4,3,32,256]{3,2,1,0:T(8,128)}, f32[3,32,256]{2,1,0:T(8,128)}, f32[2,3,32,256]{3,2,1,0:T(8,128)}, f32[2,3,32,2...) custom-call(f32[4,3,32,256]{3,2,1,0:T(8,128)} %get-tuple-element.50.mid_ref, ...), custom_call_target="tpu_custom_call" | custom-call | tf_op jit(solution)/shard_map/block/pallas_call | solution.py:119
  75.6 6.0 %collective-permute-start.13 = (f32[3,32,256]{2,1,0:T(8,128)}, f32[3,32,256]{2,1,0:T(8,128)S(1)}, u32[]{:S(2)}, u32[]{:S(2)}) collective-permute-start(f32[3,32,256]{2,1,0:T(8,128)} %get-tuple-element.58.own_ref), channel_id=1, source_target_pairs={{0,16},{1,21},{2,26},{3,31},{4,20},{5,17},{6,30},{7,27},{8,24},{9,... | collective-permute-start | bytes 294920 | tf_op jit(solution)/shard_map/group_gather/ppermute | solution.py:531
  83.4 2.2 %collective-permute-start.12 = (f32[3,32,256]{2,1,0:T(8,128)}, f32[3,32,256]{2,1,0:T(8,128)S(1)}, u32[]{:S(2)}, u32[]{:S(2)}) collective-permute-start(f32[3,32,256]{2,1,0:T(8,128)} %get-tuple-element.61), channel_id=1, source_target_pairs={{0,28},{1,29},{2,30},{3,31},{12,16},{13,17},{14,18},{15,19},{16,12... | collective-permute-start | bytes 294920 | tf_op jit(solution)/shard_map/group_gather/ppermute | solution.py:534
  86.6 3.5 %collective-permute-start.14 = (f32[3,32,256]{2,1,0:T(8,128)S(1)}, f32[3,32,256]{2,1,0:T(8,128)S(1)}, u32[]{:S(2)}, u32[]{:S(2)}) collective-permute-start(f32[3,32,256]{2,1,0:T(8,128)S(1)} %collective-permute-done.13.a0_ref), channel_id=1, source_target_pairs={{0,1},{1,0},{2,3},{3,2},{4,5},{5,4},{6,7},{7,6},{8,9},{9,8},{10,11... | collective-permute-start | bytes 294920 | tf_op jit(solution)/shard_map/group_gather/ppermute | solution.py:114
  91.3 2.1 %collective-permute-start.16 = (f32[3,32,256]{2,1,0:T(8,128)S(1)}, f32[3,32,256]{2,1,0:T(8,128)S(1)}, u32[]{:S(2)}, u32[]{:S(2)}) collective-permute-start(f32[3,32,256]{2,1,0:T(8,128)S(1)} %collective-permute-done.13.a0_ref), channel_id=1, source_target_pairs={{0,3},{1,2},{2,1},{3,0},{4,7},{5,6},{6,5},{7,4},{8,11},{9,10},{10,... | collective-permute-start | bytes 294920 | tf_op jit(solution)/shard_map/group_gather/ppermute | solution.py:114
  93.3 3.2 %collective-permute-done.11.b3_ref = f32[2,3,32,256]{3,2,1,0:T(8,128)S(1)} collective-permute-done((f32[2,3,32,256]{3,2,1,0:T(8,128)}, f32[2,3,32,256]{3,2,1,0:T(8,128)S(1)}, u32[]{:S(2)}, u32[]{:S(2)}) %collective-permute-start.11) | collective-permute-done | bytes 196640 | tf_op jit(solution)/shard_map/group_gather/ppermute | solution.py:114
  99.1 3.0 %group_gather.1 = (f32[8,3,32,256]{3,2,1,0:T(8,128)}, f32[8,3,32,256]{3,2,1,0:T(8,128)}, f32[8,3,32,256]{3,2,1,0:T(8,128)}, f32[2,3,32,256]{3,2,1,0:T(8,128)}) custom-call(f32[3,32,256]{2,1,0:T(8,128)} %get-tuple-element.58.own_ref, f32[2,3,32,256]{3,2,1,0:T(8,128)} %copy-done.10, f32[3,32,256]{2,1,0:T(8,128)} %copy-done.12, f32[2,3,32,256]{3,2,1,0:T(8,128)} %copy-done.11, ...), custom_call_target="tpu_custom_call" | custom-call | tf_op jit(solution)/shard_map/group_gather/pallas_call | solution.py:119
  102.1 4.5 %collective-permute-start.17 = (f32[8,3,32,256]{3,2,1,0:T(8,128)}, f32[8,3,32,256]{3,2,1,0:T(8,128)S(1)}, u32[]{:S(2)}, u32[]{:S(2)}) collective-permute-start(f32[8,3,32,256]{3,2,1,0:T(8,128)} %get-tuple-element.63), channel_id=1, source_target_pairs={{0,32},{32,64},{64,96},{96,128},{128,160},{160,192},{192,224},{1,3... | collective-permute-start | bytes 2359304 | tf_op jit(solution)/shard_map/group_gather/ppermute | solution.py:110
  108.6 7.3 %collective-permute-done.17.lo_ref = f32[8,3,32,256]{3,2,1,0:T(8,128)S(1)} collective-permute-done((f32[8,3,32,256]{3,2,1,0:T(8,128)}, f32[8,3,32,256]{3,2,1,0:T(8,128)S(1)}, u32[]{:S(2)}, u32[]{:S(2)}) %collective-permute-start.17) | collective-permute-done | bytes 786464 | tf_op jit(solution)/shard_map/group_gather/ppermute | solution.py:110
  115.8 4.3 %collective-permute-done.18.hi_ref = f32[8,3,32,256]{3,2,1,0:T(8,128)S(1)} collective-permute-done((f32[8,3,32,256]{3,2,1,0:T(8,128)}, f32[8,3,32,256]{3,2,1,0:T(8,128)S(1)}, u32[]{:S(2)}, u32[]{:S(2)}) %collective-permute-start.18) | collective-permute-done | bytes 786464 | tf_op jit(solution)/shard_map/group_gather/ppermute | solution.py:110
  121.0 6.8 %group.1 = (f32[5,3,32,256]{3,2,1,0:T(8,128)}, f32[5,3,32,256]{3,2,1,0:T(8,128)}, f32[4,3,32,256]{3,2,1,0:T(8,128)}, f32[3,32,256]{2,1,0:T(8,128)}, f32[2,3,32,2...) custom-call(f32[8,3,32,256]{3,2,1,0:T(8,128)} %get-tuple-element.62.mid_ref, ...), custom_call_target="tpu_custom_call" | custom-call | tf_op jit(solution)/shard_map/group/pallas_call | solution.py:119
  136.1 2.9 %collective-permute-done.21 = f32[2,3,32,256]{3,2,1,0:T(8,128)S(1)} collective-permute-done((f32[2,3,32,256]{3,2,1,0:T(8,128)}, f32[2,3,32,256]{3,2,1,0:T(8,128)S(1)}, u32[]{:S(2)}, u32[]{:S(2)}) %collective-permute-start.21) | collective-permute-done | bytes 196640 | tf_op jit(solution)/shard_map/coarse_gather/ppermute | solution.py:114
  142.0 11.5 %up.1 = (f32[4,32,256]{2,1,0:T(8,128)}, f32[1,128]{1,0:T(1,128)}) custom-call(f32[4,32,256]{2,1,0:T(8,128)} %s_ref.5, f32[4,32,256]{2,1,0:T(8,128)} %c_ref.5, f32[4,32,256]{2,1,0:T(8,128)} %tex_ref.5, s32[4,32,2]{2,1,0:T(8,128)} %copy.17.lab_ref, f32[10,32,256]{2,1,0:T(8,128)} %copy-done, f32[10,32,256]{2,1,0:T(8,128)} %copy-done.1, ...), custom_call_target="tpu_custom_call" | custom-call | tf_op jit(solution)/shard_map/up/pallas_call | solution.py:119
  154.3 13.5 %all_to_all.15 = f32[32,1,2]{2,1,0:T(1,128)S(1)} all-to-all(f32[32,1,2]{2,1,0:T(1,128)S(1)} %bitcast.12), channel_id=1, replica_groups=mesh['grp'=8,'dev'=32] {'dev'}, dimensions={0} | all-to-all | bytes 512 | tf_op jit(solution)/shard_map/table/all_to_all | solution.py:571
  (90 shorter events, 35.5 us)
Async XLA Ops:
  0.6 9.9 %collective-permute-start = (f32[1,2]{1,0:T(1,128)}, f32[1,2]{1,0:T(1,128)S(1)}, u32[]{:S(2)}, u32[]{:S(2)}) collective-permute-start(f32[1,2]{1,0:T(1,128)} %param.9), channel_id=1, source_target_pairs={{0,32},{32,64},{64,96},{96,128},{128,160},{160,192},{192,224},{1,3... | collective-permute-start | bytes 32 | tf_op jit(solution)/shard_map/fine_halo/ppermute | solution.py:110
  5.2 5.3 %collective-permute-start.1 = (f32[1,2]{1,0:T(1,128)}, f32[1,2]{1,0:T(1,128)S(1)}, u32[]{:S(2)}, u32[]{:S(2)}) collective-permute-start(f32[1,2]{1,0:T(1,128)} %param.9), channel_id=1, source_target_pairs={{32,0},{64,32},{96,64},{128,96},{160,128},{192,160},{224,192},{33,... | collective-permute-start | bytes 32 | tf_op jit(solution)/shard_map/fine_halo/ppermute | solution.py:110
  10.6 26.4 %collective-permute-start.2 = (f32[10,32,256]{2,1,0:T(8,128)}, f32[10,32,256]{2,1,0:T(8,128)S(1)}, u32[]{:S(2)}, u32[]{:S(2)}) collective-permute-start(f32[10,32,256]{2,1,0:T(8,128)} %get-tuple-element.41), channel_id=1, source_target_pairs={{0,1},{1,2},{2,3},{3,4},{4,5},{5,6},{6,7},{7,8},{8,9},{9,10},{10,1... | collective-permute-start | bytes 983048 | tf_op jit(solution)/shard_map/fine_halo/ppermute | solution.py:110
  13.7 23.3 %collective-permute-start.3 = (f32[10,32,256]{2,1,0:T(8,128)}, f32[10,32,256]{2,1,0:T(8,128)S(1)}, u32[]{:S(2)}, u32[]{:S(2)}) collective-permute-start(f32[10,32,256]{2,1,0:T(8,128)} %get-tuple-element.42), channel_id=1, source_target_pairs={{1,0},{2,1},{3,2},{4,3},{5,4},{6,5},{7,6},{8,7},{9,8},{10,9},{11,1... | collective-permute-start | bytes 983048 | tf_op jit(solution)/shard_map/fine_halo/ppermute | solution.py:110
  43.8 9.7 %collective-permute-start.4 = (f32[2,3,32,256]{3,2,1,0:T(8,128)}, f32[2,3,32,256]{3,2,1,0:T(8,128)S(1)}, u32[]{:S(2)}, u32[]{:S(2)}) collective-permute-start(f32[2,3,32,256]{3,2,1,0:T(8,128)} %get-tuple-element.48), channel_id=1, source_target_pairs={{0,1},{1,0},{2,3},{3,2},{4,5},{5,4},{6,7},{7,6},{8,9},{9,8},{10,11... | collective-permute-start | bytes 589832 | tf_op jit(solution)/shard_map/block_gather/ppermute | solution.py:114
  44.1 9.4 %collective-permute-start.6 = (f32[2,3,32,256]{3,2,1,0:T(8,128)}, f32[2,3,32,256]{3,2,1,0:T(8,128)S(1)}, u32[]{:S(2)}, u32[]{:S(2)}) collective-permute-start(f32[2,3,32,256]{3,2,1,0:T(8,128)} %get-tuple-element.49), channel_id=1, source_target_pairs={{0,3},{1,2},{2,1},{3,0},{4,7},{5,6},{6,5},{7,4},{8,11},{9,10},{10,... | collective-permute-start | bytes 589832 | tf_op jit(solution)/shard_map/block_gather/ppermute | solution.py:114
  45.1 8.4 %collective-permute-start.5 = (f32[3,32,256]{2,1,0:T(8,128)}, f32[3,32,256]{2,1,0:T(8,128)S(1)}, u32[]{:S(2)}, u32[]{:S(2)}) collective-permute-start(f32[3,32,256]{2,1,0:T(8,128)} %get-tuple-element.47.a0_ref), channel_id=1, source_target_pairs={{0,2},{1,3},{2,0},{3,1},{4,6},{5,7},{6,4},{7,5},{8,10},{9,11},{10,... | collective-permute-start | bytes 294920 | tf_op jit(solution)/shard_map/block_gather/ppermute | solution.py:114
  57.2 13.1 %collective-permute-start.7 = (f32[4,3,32,256]{3,2,1,0:T(8,128)}, f32[4,3,32,256]{3,2,1,0:T(8,128)S(1)}, u32[]{:S(2)}, u32[]{:S(2)}) collective-permute-start(f32[4,3,32,256]{3,2,1,0:T(8,128)} %get-tuple-element.51), channel_id=1, source_target_pairs={{0,4},{1,5},{2,6},{3,7},{4,8},{5,9},{6,10},{7,11},{8,12},{9,13},{1... | collective-permute-start | bytes 1179656 | tf_op jit(solution)/shard_map/block_gather/ppermute | solution.py:110
  59.5 11.6 %collective-permute-start.8 = (f32[4,3,32,256]{3,2,1,0:T(8,128)}, f32[4,3,32,256]{3,2,1,0:T(8,128)S(1)}, u32[]{:S(2)}, u32[]{:S(2)}) collective-permute-start(f32[4,3,32,256]{3,2,1,0:T(8,128)} %get-tuple-element.52), channel_id=1, source_target_pairs={{4,0},{5,1},{6,2},{7,3},{8,4},{9,5},{10,6},{11,7},{12,8},{13,9},{1... | collective-permute-start | bytes 1179656 | tf_op jit(solution)/shard_map/block_gather/ppermute | solution.py:110
  75.6 14.5 %collective-permute-start.10 = (f32[3,32,256]{2,1,0:T(8,128)}, f32[3,32,256]{2,1,0:T(8,128)S(1)}, u32[]{:S(2)}, u32[]{:S(2)}) collective-permute-start(f32[3,32,256]{2,1,0:T(8,128)} %get-tuple-element.58.own_ref), channel_id=1, source_target_pairs={{0,8},{1,9},{2,10},{3,11},{4,12},{5,13},{6,14},{7,15},{8,0},{9,1},... | collective-permute-start | bytes 294920 | tf_op jit(solution)/shard_map/group_gather/ppermute | solution.py:114
  75.6 10.9 %collective-permute-start.13 = (f32[3,32,256]{2,1,0:T(8,128)}, f32[3,32,256]{2,1,0:T(8,128)S(1)}, u32[]{:S(2)}, u32[]{:S(2)}) collective-permute-start(f32[3,32,256]{2,1,0:T(8,128)} %get-tuple-element.58.own_ref), channel_id=1, source_target_pairs={{0,16},{1,21},{2,26},{3,31},{4,20},{5,17},{6,30},{7,27},{8,24},{9,... | collective-permute-start | bytes 294920 | tf_op jit(solution)/shard_map/group_gather/ppermute | solution.py:531
  81.7 11.7 %collective-permute-start.9 = (f32[2,3,32,256]{3,2,1,0:T(8,128)}, f32[2,3,32,256]{3,2,1,0:T(8,128)S(1)}, u32[]{:S(2)}, u32[]{:S(2)}) collective-permute-start(f32[2,3,32,256]{3,2,1,0:T(8,128)} %get-tuple-element.59), channel_id=1, source_target_pairs={{0,4},{1,5},{2,6},{3,7},{4,0},{5,1},{6,2},{7,3},{8,12},{9,13},{10,... | collective-permute-start | bytes 589832 | tf_op jit(solution)/shard_map/group_gather/ppermute | solution.py:114
  83.4 13.2 %collective-permute-start.11 = (f32[2,3,32,256]{3,2,1,0:T(8,128)}, f32[2,3,32,256]{3,2,1,0:T(8,128)S(1)}, u32[]{:S(2)}, u32[]{:S(2)}) collective-permute-start(f32[2,3,32,256]{3,2,1,0:T(8,128)} %get-tuple-element.60), channel_id=1, source_target_pairs={{0,12},{1,13},{2,14},{3,15},{4,8},{5,9},{6,10},{7,11},{8,4},{9,5},... | collective-permute-start | bytes 589832 | tf_op jit(solution)/shard_map/group_gather/ppermute | solution.py:114
  83.4 7.9 %collective-permute-start.12 = (f32[3,32,256]{2,1,0:T(8,128)}, f32[3,32,256]{2,1,0:T(8,128)S(1)}, u32[]{:S(2)}, u32[]{:S(2)}) collective-permute-start(f32[3,32,256]{2,1,0:T(8,128)} %get-tuple-element.61), channel_id=1, source_target_pairs={{0,28},{1,29},{2,30},{3,31},{12,16},{13,17},{14,18},{15,19},{16,12... | collective-permute-start | bytes 294920 | tf_op jit(solution)/shard_map/group_gather/ppermute | solution.py:534
  86.6 11.9 %copy-start.13 = (f32[3,32,256]{2,1,0:T(8,128)}, f32[3,32,256]{2,1,0:T(8,128)S(1)}, u32[]{:S(2)}) copy-start(f32[3,32,256]{2,1,0:T(8,128)S(1)} %collective-permute-done.13.a0_ref) | copy-start | bytes 294916
  86.6 10.0 %collective-permute-start.14 = (f32[3,32,256]{2,1,0:T(8,128)S(1)}, f32[3,32,256]{2,1,0:T(8,128)S(1)}, u32[]{:S(2)}, u32[]{:S(2)}) collective-permute-start(f32[3,32,256]{2,1,0:T(8,128)S(1)} %collective-permute-done.13.a0_ref), channel_id=1, source_target_pairs={{0,1},{1,0},{2,3},{3,2},{4,5},{5,4},{6,7},{7,6},{8,9},{9,8},{10,11... | collective-permute-start | bytes 294920 | tf_op jit(solution)/shard_map/group_gather/ppermute | solution.py:114
  90.1 6.5 %collective-permute-start.15 = (f32[3,32,256]{2,1,0:T(8,128)S(1)}, f32[3,32,256]{2,1,0:T(8,128)S(1)}, u32[]{:S(2)}, u32[]{:S(2)}) collective-permute-start(f32[3,32,256]{2,1,0:T(8,128)S(1)} %collective-permute-done.13.a0_ref), channel_id=1, source_target_pairs={{0,2},{1,3},{2,0},{3,1},{4,6},{5,7},{6,4},{7,5},{8,10},{9,11},{10,... | collective-permute-start | bytes 294920 | tf_op jit(solution)/shard_map/group_gather/ppermute | solution.py:114
  91.3 7.2 %collective-permute-start.16 = (f32[3,32,256]{2,1,0:T(8,128)S(1)}, f32[3,32,256]{2,1,0:T(8,128)S(1)}, u32[]{:S(2)}, u32[]{:S(2)}) collective-permute-start(f32[3,32,256]{2,1,0:T(8,128)S(1)} %collective-permute-done.13.a0_ref), channel_id=1, source_target_pairs={{0,3},{1,2},{2,1},{3,0},{4,7},{5,6},{6,5},{7,4},{8,11},{9,10},{10,... | collective-permute-start | bytes 294920 | tf_op jit(solution)/shard_map/group_gather/ppermute | solution.py:114
  102.1 13.7 %collective-permute-start.17 = (f32[8,3,32,256]{3,2,1,0:T(8,128)}, f32[8,3,32,256]{3,2,1,0:T(8,128)S(1)}, u32[]{:S(2)}, u32[]{:S(2)}) collective-permute-start(f32[8,3,32,256]{3,2,1,0:T(8,128)} %get-tuple-element.63), channel_id=1, source_target_pairs={{0,32},{32,64},{64,96},{96,128},{128,160},{160,192},{192,224},{1,3... | collective-permute-start | bytes 2359304 | tf_op jit(solution)/shard_map/group_gather/ppermute | solution.py:110
  106.6 13.5 %collective-permute-start.18 = (f32[8,3,32,256]{3,2,1,0:T(8,128)}, f32[8,3,32,256]{3,2,1,0:T(8,128)S(1)}, u32[]{:S(2)}, u32[]{:S(2)}) collective-permute-start(f32[8,3,32,256]{3,2,1,0:T(8,128)} %get-tuple-element.64), channel_id=1, source_target_pairs={{32,0},{64,32},{96,64},{128,96},{160,128},{192,160},{224,192},{33,... | collective-permute-start | bytes 2359304 | tf_op jit(solution)/shard_map/group_gather/ppermute | solution.py:110
  127.8 6.4 %collective-permute-start.19 = (f32[2,3,32,256]{3,2,1,0:T(8,128)}, f32[2,3,32,256]{3,2,1,0:T(8,128)S(1)}, u32[]{:S(2)}, u32[]{:S(2)}) collective-permute-start(f32[2,3,32,256]{3,2,1,0:T(8,128)} %get-tuple-element.72), channel_id=1, source_target_pairs={{0,64},{32,96},{64,0},{96,32},{128,192},{160,224},{192,128},{224,1... | collective-permute-start | bytes 589832 | tf_op jit(solution)/shard_map/coarse_gather/ppermute | solution.py:114
  129.3 9.7 %collective-permute-start.21 = (f32[2,3,32,256]{3,2,1,0:T(8,128)}, f32[2,3,32,256]{3,2,1,0:T(8,128)S(1)}, u32[]{:S(2)}, u32[]{:S(2)}) collective-permute-start(f32[2,3,32,256]{3,2,1,0:T(8,128)} %get-tuple-element.72), channel_id=1, source_target_pairs={{0,192},{32,224},{64,128},{96,160},{128,64},{160,96},{192,0},{224,... | collective-permute-start | bytes 589832 | tf_op jit(solution)/shard_map/coarse_gather/ppermute | solution.py:114
  129.3 6.7 %collective-permute-start.20 = (f32[3,32,256]{2,1,0:T(8,128)}, f32[3,32,256]{2,1,0:T(8,128)S(1)}, u32[]{:S(2)}, u32[]{:S(2)}) collective-permute-start(f32[3,32,256]{2,1,0:T(8,128)} %get-tuple-element.71), channel_id=1, source_target_pairs={{0,128},{32,160},{64,192},{96,224},{128,0},{160,32},{192,64},{224,... | collective-permute-start | bytes 294920 | tf_op jit(solution)/shard_map/coarse_gather/ppermute | solution.py:114
  139.1 2.1 %collective-permute-start.22 = (f32[6,3,32,256]{3,2,1,0:T(8,128)S(1)}, f32[6,3,32,256]{3,2,1,0:T(8,128)S(1)}, u32[]{:S(2)}, u32[]{:S(2)}) collective-permute-start(f32[6,3,32,256]{3,2,1,0:T(8,128)S(1)} %fusion.near_ref), channel_id=1, source_target_pairs={{0,32},{32,0},{64,96},{96,64},{128,160},{160,128},{192,224},{224,1... | collective-permute-start | bytes 1769480 | tf_op jit(solution)/shard_map/coarse_gather/ppermute | solution.py:114
  (21 other events, 53.2 us)
